TPU v7x, 32 devices: a whole 2x2x4 slice. The times are simulated.
32 devices in a mesh: dp: 8 (over z, core), fsdp: 4 (over y, x).
Axes of the slice: x: 2, y: 2, z: 4, core: 2. Of those that a mesh axis runs over, the one named last changes fastest.
Arguments:
- pixels: bfloat16 [32768, 768], P(('dp', 'fsdp')), may hold values from -6 to 6
- valid_mask: int32 [32768, 768], P(('dp', 'fsdp')), may hold values from 0 to 1
- size_groups: int32 [32], P(('dp', 'fsdp')), may hold values from 0 to 2
- code_index: int32 [4, 8192], P(None, ('dp', 'fsdp')), may hold values from 0 to 16383, as said below
- w_pixel: float32 [2, 768, 512], P(None, 'fsdp', 'dp'), may hold values from -0.625 to 0.625
- w_res: float32 [4, 4608, 512], P(None, 'fsdp', 'dp'), may hold values from -0.1875 to 0.1875
- w_scale: float32 [2, 2048, 512], P(None, 'fsdp', 'dp'), may hold values from -0.5 to 0.5
- w_latent: float32 [2, 512, 256], P(None, 'fsdp', 'dp'), may hold values from -0.75 to 0.75
- norm_gains: float32 [8, 512], replicated, may hold values from -0.9 to 1.5
- moment_pixel: float32 [2, 768, 512], P(None, 'fsdp', 'dp'), may hold values from -4.4703484e-08 to 4.4703484e-08
- moment_res: float32 [4, 4608, 512], P(None, 'fsdp', 'dp'), may hold values from -4.4703484e-08 to 4.4703484e-08
- moment_scale: float32 [2, 2048, 512], P(None, 'fsdp', 'dp'), may hold values from -4.4703484e-08 to 4.4703484e-08
- moment_latent: float32 [2, 512, 256], P(None, 'fsdp', 'dp'), may hold values from -4.4703484e-08 to 4.4703484e-08
- moment_gains: float32 [8, 512], replicated, may hold values from -1.4901161e-07 to 1.4901161e-07
- second_pixel: float32 [2, 768, 512], P(None, 'fsdp', 'dp'), may hold values from 7.84e-18 to 3.136e-17
- second_res: float32 [4, 4608, 512], P(None, 'fsdp', 'dp'), may hold values from 7.84e-18 to 3.136e-17
- second_scale: float32 [2, 2048, 512], P(None, 'fsdp', 'dp'), may hold values from 7.84e-18 to 3.136e-17
- second_latent: float32 [2, 512, 256], P(None, 'fsdp', 'dp'), may hold values from 7.84e-18 to 3.136e-17
- second_gains: float32 [8, 512], replicated, may hold values from 1e-16 to 4e-16
- ema_counts: float32 [16384], P(('dp', 'fsdp')), may hold values from 0.5 to 4
- ema_sums: float32 [16384, 256], P(('dp', 'fsdp')), may hold values from -6 to 6
Outputs:
- loss_parts: float32 [3], replicated
- grad_norm: float32 [1], replicated
- next_pixel: float32 [2, 768, 512], P(None, 'fsdp', 'dp')
- next_moment_pixel: float32 [2, 768, 512], P(None, 'fsdp', 'dp')
- next_second_pixel: float32 [2, 768, 512], P(None, 'fsdp', 'dp')
- copy_pixel: bfloat16 [2, 768, 512], P(None, 'fsdp', 'dp')
- next_res: float32 [4, 4608, 512], P(None, 'fsdp', 'dp')
- next_moment_res: float32 [4, 4608, 512], P(None, 'fsdp', 'dp')
- next_second_res: float32 [4, 4608, 512], P(None, 'fsdp', 'dp')
- copy_res: bfloat16 [4, 4608, 512], P(None, 'fsdp', 'dp')
- next_scale: float32 [2, 2048, 512], P(None, 'fsdp', 'dp')
- next_moment_scale: float32 [2, 2048, 512], P(None, 'fsdp', 'dp')
- next_second_scale: float32 [2, 2048, 512], P(None, 'fsdp', 'dp')
- copy_scale: bfloat16 [2, 2048, 512], P(None, 'fsdp', 'dp')
- next_latent: float32 [2, 512, 256], P(None, 'fsdp', 'dp')
- next_moment_latent: float32 [2, 512, 256], P(None, 'fsdp', 'dp')
- next_second_latent: float32 [2, 512, 256], P(None, 'fsdp', 'dp')
- copy_latent: bfloat16 [2, 512, 256], P(None, 'fsdp', 'dp')
- next_gains: float32 [8, 512], replicated
- next_moment_gains: float32 [8, 512], replicated
- next_second_gains: float32 [8, 512], replicated
- next_counts: float32 [16384], P(('dp', 'fsdp'))
- next_sums: float32 [16384, 256], P(('dp', 'fsdp'))
- codebook: float32 [16384, 256], P(('dp', 'fsdp'))
- codebook_copy: bfloat16 [16384, 256], P(('dp', 'fsdp'))
Inputs may be any that keep to these rules, and one draw needn't show every extreme that they name: `code_index`: among the 4 x 256 codes of one device's positions, at most 64 lie in any one device's block of 16384 / 32 consecutive codes, and on every device some block holds exactly 64 of them.
All inputs are finite; a program needn't handle non-finite values.
Results may differ from a plain program's by a relative error of at most 0.0061.
Values may be sent and summed in bfloat16 or wider, within the bound.
No kernel may reach another device: no remote copies, remote signals or barrier semaphores. Data moves between devices by JAX's collectives and lax.ppermute only.
A program may use at most 256 MiB of HBM per device.

v0:
```python
import jax
import jax.numpy as jnp
from jax import lax
from jax.sharding import PartitionSpec as P

C = 512
ZD = 256
K = 16384
GROUPS = 32
SIDE = 32
DEPTH = 4
STEP = 5


HIGH = lax.Precision.HIGHEST
TAPS = [(dy, dx) for dy in (-1, 0, 1) for dx in (-1, 0, 1)]
COMMIT_WEIGHT = 0.25
CLIP_AT = 1e-05
EMA_DECAY = 0.8
WEIGHT_RATE = 0.03
GAIN_RATE = 0.4


def geometry(groups, size, width):
    span = jnp.left_shift(jnp.ones_like(groups), groups)
    sides = size // 4 * span
    tile = jnp.arange(16, dtype=jnp.int32)[None, :]
    image = tile // 4 // span[:, None] * (4 // span[:, None]) + tile % 4 // span[:, None]
    member = (image[:, :, None] == jnp.arange(16, dtype=jnp.int32)[None, None, :]).astype(
        jnp.float32
    )
    count = (sides * sides).astype(jnp.float32) * (width // GROUPS)
    return (sides, member, count)


def image_means(field, member, count):
    batch, size, _, width = field.shape
    tile = size // 4
    sums = jnp.sum(field.reshape(batch, 4, tile, 4, tile, width), axis=(2, 4)).reshape(
        batch, 16, width
    )
    per_image = jnp.einsum("btm,btc->bmc", member, sums, precision=HIGH)
    grouped = (
        jnp.sum(per_image.reshape(batch, 16, GROUPS, width // GROUPS), axis=3)
        / count[:, None, None]
    )
    spread = jnp.einsum("btm,bmg->btg", member, grouped, precision=HIGH)
    full = jnp.repeat(spread, width // GROUPS, axis=2).reshape(batch, 4, 1, 4, 1, width)
    return jnp.broadcast_to(full, (batch, 4, tile, 4, tile, width)).reshape(
        batch, size, size, width
    )


def gn_silu(field, gamma, beta, geom):
    mean = image_means(field, geom[1], geom[2])
    centered = field - mean
    var = image_means(centered * centered, geom[1], geom[2])
    return jax.nn.silu(centered * lax.rsqrt(var + 1e-05) * gamma + beta)


def silu_slope(value):
    gate = jax.nn.sigmoid(value)
    return gate * (1.0 + value * (1.0 - gate))


def side_masks(sides, size, delta):
    pos = jnp.arange(size, dtype=jnp.int32)
    near = pos + delta
    inside = (near >= 0) & (near < size)
    same = near[None, :] // sides[:, None] == pos[None, :] // sides[:, None]
    return (inside[None, :] & same).astype(jnp.float32)


def shifted(act, sides, dy, dx):
    size = act.shape[1]
    padded = jnp.pad(act, ((0, 0), (1, 1), (1, 1), (0, 0)))
    part = padded[:, 1 + dy : 1 + dy + size, 1 + dx : 1 + dx + size, :]
    keep = side_masks(sides, size, dy)[:, :, None] * side_masks(sides, size, dx)[:, None, :]
    return part * keep[..., None].astype(act.dtype)


def along_rows(left, right):
    return lax.dot_general(
        left, right, (((0,), (0,)), ((), ())), preferred_element_type=jnp.float32
    )


def along_cols(left, right):
    return lax.dot_general(
        left, right, (((1,), (1,)), ((), ())), preferred_element_type=jnp.float32
    )


def conv_forward(act, taps, geom):
    width = act.shape[3]
    total = jnp.zeros((act.shape[0] * act.shape[1] * act.shape[2], width), jnp.float32)
    for index, (dy, dx) in enumerate(TAPS):
        piece = shifted(act, geom[0], dy, dx).reshape(-1, width)
        total = total + jnp.dot(piece, taps[index], preferred_element_type=jnp.float32)
    return total.reshape(act.shape)


def conv_backward(act, taps, grad_out, geom):
    width = act.shape[3]
    grad_low = grad_out.reshape(-1, width).astype(jnp.bfloat16)
    weight_parts = []
    grad_act = jnp.zeros(act.shape, jnp.float32)
    for index, (dy, dx) in enumerate(TAPS):
        piece = shifted(act, geom[0], dy, dx).reshape(-1, width)
        weight_parts.append(along_rows(piece, grad_low))
        back = along_cols(grad_low, taps[index]).reshape(act.shape)
        grad_act = grad_act + shifted(back, geom[0], -dy, -dx)
    return (jnp.concatenate(weight_parts, axis=0), grad_act)


def block_forward(field, taps_pair, gains, first, geom):
    a_one = gn_silu(field, gains[first], gains[4 + first], geom).astype(jnp.bfloat16)
    t_one = conv_forward(a_one, taps_pair[0], geom)
    a_two = gn_silu(t_one, gains[first + 1], gains[5 + first], geom).astype(jnp.bfloat16)
    t_two = conv_forward(a_two, taps_pair[1], geom)
    return (field + t_two, (field, a_one, t_one, a_two))


def block_backward(grad, kept, taps_pair, gains, first, geom):
    field, a_one, t_one, a_two = kept
    grad_two, d_a_two = conv_backward(a_two, taps_pair[1], grad, geom)
    _, pull = jax.vjp(
        lambda x, g, b: gn_silu(x, g, b, geom), t_one, gains[first + 1], gains[5 + first]
    )
    d_t_one, scale_two, shift_two = pull(d_a_two)
    grad_one, d_a_one = conv_backward(a_one, taps_pair[0], d_t_one, geom)
    _, pull = jax.vjp(lambda x, g, b: gn_silu(x, g, b, geom), field, gains[first], gains[4 + first])
    d_field, scale_one, shift_one = pull(d_a_one)
    return (grad + d_field, (grad_one, grad_two), (scale_one, scale_two, shift_one, shift_two))


def to_depth(field):
    batch, size, _, width = field.shape
    half = size // 2
    parts = field.reshape(batch, half, 2, half, 2, width).transpose(0, 1, 3, 2, 4, 5)
    return parts.reshape(batch * half * half, 4 * width)


def from_depth(rows, batch, size):
    half = size // 2
    width = rows.shape[1] // 4
    parts = rows.reshape(batch, half, half, 2, 2, width).transpose(0, 1, 3, 2, 4, 5)
    return parts.reshape(batch, size, size, width)


def fetch(shard):
    cols = lax.all_gather(shard.astype(jnp.bfloat16), "dp", axis=1, tiled=True)
    return lax.all_gather(cols, "fsdp", axis=0, tiled=True)


def backward_copy(shard, ready):
    return fetch(shard).reshape(ready.shape)


def reduce_grad(full):
    rows = lax.psum_scatter(full, "fsdp", scatter_dimension=0, tiled=True)
    return lax.psum_scatter(rows, "dp", scatter_dimension=1, tiled=True)


def adam_step(weight, moment, second, grad, rate):
    moment_new = 0.5 * moment + 0.5 * grad
    second_new = 0.5 * second + 0.5 * grad * grad
    fix = 1.0 - 0.5**STEP
    weight_new = weight - rate * (
        moment_new / fix / (jnp.sqrt(second_new / fix) + 1e-12) + 0.01 * weight
    )
    return (weight_new, moment_new, second_new)


def owner_slots(flat_codes, devices, capacity, rows_own):
    owner = flat_codes // rows_own
    order = jnp.argsort(owner, stable=True)
    ranked = owner[order]
    first = jnp.searchsorted(ranked, jnp.arange(devices, dtype=jnp.int32))
    place = jnp.arange(flat_codes.shape[0], dtype=jnp.int32) - first[ranked]
    return jnp.zeros_like(flat_codes).at[order].set(ranked * capacity + place)


def on_device(
    pixels,
    valid_mask,
    size_groups,
    code_index,
    w_pixel,
    w_res,
    w_scale,
    w_latent,
    norm_gains,
    moment_pixel,
    moment_res,
    moment_scale,
    moment_latent,
    moment_gains,
    second_pixel,
    second_res,
    second_scale,
    second_latent,
    second_gains,
    ema_counts,
    ema_sums,
):
    canv = size_groups.shape[0]
    n_outer = lax.axis_size("dp")
    n_inner = lax.axis_size("fsdp")
    devices = n_outer * n_inner
    latent_all = code_index.shape[1] * devices
    rows = ema_sums.shape[0]
    flat_codes = code_index.reshape(-1)
    capacity = max(2, 2 * flat_codes.shape[0] // devices)
    slot = owner_slots(flat_codes, devices, capacity, rows)
    local_row = flat_codes % rows
    geom = geometry(size_groups, SIDE, C)
    mask = valid_mask.astype(jnp.float32)
    total_valid = lax.psum(jnp.sum(mask), ("dp", "fsdp"))
    book = (ema_sums / ema_counts[:, None]).astype(jnp.bfloat16)
    wanted = jnp.full((devices * capacity,), -1, jnp.int32).at[slot].set(local_row)
    wanted = wanted.reshape(n_outer, n_inner, capacity)
    asked = lax.all_to_all(
        lax.all_to_all(wanted, "dp", split_axis=0, concat_axis=0, tiled=True),
        "fsdp",
        split_axis=1,
        concat_axis=1,
        tiled=True,
    )
    answer = jnp.take(book, jnp.maximum(asked, 0), axis=0)
    replies = lax.all_to_all(
        lax.all_to_all(answer, "dp", split_axis=0, concat_axis=0, tiled=True),
        "fsdp",
        split_axis=1,
        concat_axis=1,
        tiled=True,
    )
    picked_rows = replies.reshape(devices * capacity, -1)[slot].reshape(
        code_index.shape + (book.shape[1],)
    )
    q_cum = jnp.cumsum(picked_rows.astype(jnp.float32), axis=0)
    patch_in = fetch(w_pixel[0])
    field = jnp.dot(pixels, patch_in, preferred_element_type=jnp.float32).reshape(
        canv, SIDE, SIDE, C
    )
    enc_taps = (fetch(w_res[0]).reshape(9, C, C), fetch(w_res[1]).reshape(9, C, C))
    field, kept_enc = block_forward(field, enc_taps, norm_gains, 0, geom)
    e_four = to_depth(field.astype(jnp.bfloat16))
    w_down = fetch(w_scale[0])
    hidden = jnp.dot(e_four, w_down, preferred_element_type=jnp.float32)
    s_one = jax.nn.silu(hidden).astype(jnp.bfloat16)
    w_proj = fetch(w_latent[0])
    latent = jnp.dot(s_one, w_proj, preferred_element_type=jnp.float32)
    diff = latent[None] - q_cum
    commit = jnp.sum(diff * diff)
    shift = q_cum[DEPTH - 1] - latent
    quant = (latent + shift).astype(jnp.bfloat16)
    w_back = fetch(w_latent[1])
    inner = along_cols(quant, w_back)
    s_two = jax.nn.silu(inner).astype(jnp.bfloat16)
    w_up = fetch(w_scale[1])
    upper = along_cols(s_two, w_up)
    dec_field = from_depth(upper, canv, SIDE)
    dec_taps = (fetch(w_res[2]).reshape(9, C, C), fetch(w_res[3]).reshape(9, C, C))
    dec_field, kept_dec = block_forward(dec_field, dec_taps, norm_gains, 2, geom)
    outer = jax.nn.silu(dec_field).astype(jnp.bfloat16).reshape(-1, C)
    w_head = fetch(w_pixel[1])
    recon = along_cols(outer, w_head)
    err = recon - pixels.astype(jnp.float32)
    smooth = jnp.sqrt(err * err + 1.0)
    l1_local = jnp.sum(mask * (smooth - 1.0))
    grad_rec = (mask * err / smooth / total_valid).astype(jnp.bfloat16)
    d_head = along_rows(grad_rec, outer)
    head_b = backward_copy(w_pixel[1], w_head)
    d_outer = jnp.dot(grad_rec, head_b, preferred_element_type=jnp.float32)
    d_dec = (d_outer * silu_slope(dec_field.reshape(-1, C))).reshape(dec_field.shape)
    dec_b = (backward_copy(w_res[2], dec_taps[0]), backward_copy(w_res[3], dec_taps[1]))
    d_dec, dec_grads, dec_gain = block_backward(d_dec, kept_dec, dec_b, norm_gains, 2, geom)
    d_upper = to_depth(d_dec).astype(jnp.bfloat16)
    d_up = along_rows(d_upper, s_two)
    up_b = backward_copy(w_scale[1], w_up)
    d_s_two = jnp.dot(d_upper, up_b, preferred_element_type=jnp.float32)
    d_inner = (d_s_two * silu_slope(inner)).astype(jnp.bfloat16)
    d_back = along_rows(d_inner, quant)
    back_b = backward_copy(w_latent[1], w_back)
    d_quant = jnp.dot(d_inner, back_b, preferred_element_type=jnp.float32)
    d_latent = d_quant + 2.0 * COMMIT_WEIGHT / (latent_all * ZD) * jnp.sum(diff, axis=0)
    d_latent = d_latent.astype(jnp.bfloat16)
    d_proj = along_rows(s_one, d_latent)
    proj_b = backward_copy(w_latent[0], w_proj)
    d_s_one = along_cols(d_latent, proj_b)
    d_hidden = (d_s_one * silu_slope(hidden)).astype(jnp.bfloat16)
    d_down = along_rows(e_four, d_hidden)
    down_b = backward_copy(w_scale[0], w_down)
    d_e_four = along_cols(d_hidden, down_b)
    d_enc = from_depth(d_e_four, canv, SIDE)
    enc_b = (backward_copy(w_res[0], enc_taps[0]), backward_copy(w_res[1], enc_taps[1]))
    d_enc, enc_grads, enc_gain = block_backward(d_enc, kept_enc, enc_b, norm_gains, 0, geom)
    d_first = d_enc.reshape(-1, C).astype(jnp.bfloat16)
    d_patch = along_rows(pixels, d_first)
    grad_pixel = jnp.stack([reduce_grad(d_patch), reduce_grad(d_head)])
    grad_res = jnp.stack(
        [
            reduce_grad(enc_grads[0]),
            reduce_grad(enc_grads[1]),
            reduce_grad(dec_grads[0]),
            reduce_grad(dec_grads[1]),
        ]
    )
    grad_scale = jnp.stack([reduce_grad(d_down), reduce_grad(d_up)])
    grad_latent = jnp.stack([reduce_grad(d_proj), reduce_grad(d_back)])
    gain_local = jnp.stack(
        [
            enc_gain[0],
            enc_gain[1],
            dec_gain[0],
            dec_gain[1],
            enc_gain[2],
            enc_gain[3],
            dec_gain[2],
            dec_gain[3],
        ]
    )
    grad_gains, smooth_sum, commit_sum = lax.psum((gain_local, l1_local, commit), ("dp", "fsdp"))
    shard_squares = jnp.sum(grad_pixel * grad_pixel) + jnp.sum(grad_res * grad_res)
    shard_squares = (
        shard_squares + jnp.sum(grad_scale * grad_scale) + jnp.sum(grad_latent * grad_latent)
    )
    total_squares = lax.psum(shard_squares, ("dp", "fsdp")) + jnp.sum(grad_gains * grad_gains)
    norm = jnp.sqrt(total_squares)
    factor = CLIP_AT / jnp.maximum(norm, CLIP_AT)
    groups_all = [
        (w_pixel, moment_pixel, second_pixel, grad_pixel),
        (w_res, moment_res, second_res, grad_res),
        (w_scale, moment_scale, second_scale, grad_scale),
        (w_latent, moment_latent, second_latent, grad_latent),
    ]
    outputs = [jnp.stack([smooth_sum, total_valid, commit_sum]), norm.reshape(1)]
    for weight, moment, second, grad in groups_all:
        weight_new, moment_new, second_new = adam_step(
            weight, moment, second, grad * factor, WEIGHT_RATE
        )
        outputs += [weight_new, moment_new, second_new, weight_new.astype(jnp.bfloat16)]
    outputs += list(
        adam_step(norm_gains, moment_gains, second_gains, grad_gains * factor, GAIN_RATE)
    )
    prev = jnp.concatenate([jnp.zeros_like(q_cum[:1]), q_cum[:-1]], axis=0)
    resid = (latent[None] - prev).astype(jnp.bfloat16).reshape(-1, ZD)
    block_len = min(K, 2048)

    def code_block(start):
        onehot = (
            flat_codes[:, None] == start + jnp.arange(block_len, dtype=jnp.int32)[None, :]
        ).astype(jnp.bfloat16)
        return (along_rows(onehot, resid), jnp.sum(onehot, axis=0, dtype=jnp.float32))

    sums_all, counts_all = lax.map(code_block, jnp.arange(0, K, block_len, dtype=jnp.int32))
    sums_all = sums_all.reshape(K, ZD)
    counts_all = counts_all.reshape(K)
    sums_total, counts_total = lax.psum((sums_all, counts_all), ("dp", "fsdp"))
    start_row = lax.axis_index(("dp", "fsdp")) * rows
    my_sums = lax.dynamic_slice_in_dim(sums_total, start_row, rows, 0)
    my_counts = lax.dynamic_slice_in_dim(counts_total, start_row, rows, 0)
    counts_new = EMA_DECAY * ema_counts + (1.0 - EMA_DECAY) * my_counts
    sums_new = EMA_DECAY * ema_sums + (1.0 - EMA_DECAY) * my_sums
    book_new = sums_new / counts_new[:, None]
    outputs += [counts_new, sums_new, book_new, book_new.astype(jnp.bfloat16)]
    return tuple(outputs)


def solution(mesh):
    placed = (
        P(("dp", "fsdp"), None),
        P(("dp", "fsdp"), None),
        P(("dp", "fsdp")),
        P(None, ("dp", "fsdp")),
        P(None, "fsdp", "dp"),
        P(None, "fsdp", "dp"),
        P(None, "fsdp", "dp"),
        P(None, "fsdp", "dp"),
        P(),
        P(None, "fsdp", "dp"),
        P(None, "fsdp", "dp"),
        P(None, "fsdp", "dp"),
        P(None, "fsdp", "dp"),
        P(),
        P(None, "fsdp", "dp"),
        P(None, "fsdp", "dp"),
        P(None, "fsdp", "dp"),
        P(None, "fsdp", "dp"),
        P(),
        P(("dp", "fsdp")),
        P(("dp", "fsdp"), None),
    )
    return jax.shard_map(
        on_device,
        mesh=mesh,
        in_specs=placed,
        out_specs=(
            P(),
            P(),
            P(None, "fsdp", "dp"),
            P(None, "fsdp", "dp"),
            P(None, "fsdp", "dp"),
            P(None, "fsdp", "dp"),
            P(None, "fsdp", "dp"),
            P(None, "fsdp", "dp"),
            P(None, "fsdp", "dp"),
            P(None, "fsdp", "dp"),
            P(None, "fsdp", "dp"),
            P(None, "fsdp", "dp"),
            P(None, "fsdp", "dp"),
            P(None, "fsdp", "dp"),
            P(None, "fsdp", "dp"),
            P(None, "fsdp", "dp"),
            P(None, "fsdp", "dp"),
            P(None, "fsdp", "dp"),
            P(),
            P(),
            P(),
            P(("dp", "fsdp")),
            P(("dp", "fsdp"), None),
            P(("dp", "fsdp"), None),
            P(("dp", "fsdp"), None),
        ),
        check_vma=False,
    )
```

profile of v0, /device:TPU:0, one launch (start us, length us, event | category | flops | bytes accessed | tf_op | source)
XLA Modules:
  0.0 1943.9 jit_solution(17899605121491176382)
XLA Ops:
  11.5 24.1 %all-gather.31.cloned.1.call-done = bf16[1,1152,512]{1,2,0:T(8,128)(2,1)} async-done(((bf16[1,1152,64]{1,2,0:T(8,128)(2,1)}), bf16[1,1152,512]{1,2,0:T(8,128)(2,1)}) %all-gather.31.cloned.1.call-update) | async-done | bytes 1179664 | tf_op jit(solution)/shard_map/all_gather | solution.py:152
  38.1 22.2 %all-gather.35.cloned.1.call-done = bf16[1,1152,512]{1,2,0:T(8,128)(2,1)} async-done(((bf16[1,1152,64]{1,2,0:T(8,128)(2,1)}), bf16[1,1152,512]{1,2,0:T(8,128)(2,1)}) %all-gather.35.cloned.1.call-update) | async-done | bytes 1179664 | tf_op jit(solution)/shard_map/all_gather | solution.py:152
  62.8 17.3 all-gather.6
  80.2 15.8 all-gather.12
  121.8 15.9 fusion.437
  210.5 30.8 %all-gather.10 = bf16[1,128,256]{1,2,0:T(8,128)(2,1)S(1)} all-gather(bf16[1,128,32]{1,2,0:T(8,128)(2,1)S(1)} %get-tuple-element.455), channel_id=12, replica_groups=mesh['dp'=8,'fsdp'=4] {'dp'}, dimensions={2}, use_global_device_ids=true | all-gather | bytes 73728 | tf_op jit(solution)/shard_map/all_gather | solution.py:152
  474.4 39.1 %psum.50 = f32[]{:T(128)} all-reduce(f32[]{:T(128)} %get-tuple-element.298), channel_id=1, replica_groups=mesh['dp'=8,'fsdp'=4] {'dp','fsdp'}, use_global_device_ids=true, to_apply=%region_27.30 | all-reduce | flops 1 | bytes 8 | tf_op jit(solution)/shard_map/psum | solution.py:219
  795.8 49.7 %while.36 = (s32[]{:T(128)}, f32[8,2048,256]{2,1,0:T(8,128)}, f32[8,2048]{1,0:T(8,128)S(1)}, s32[4,256]{1,0:T(4,128)S(1)}, s32[8]{0:T(128)S(1)}, /*index=5*/bf16[1024,256]{1,0:T(8,128)(2,1)S(1)}, s32[]{:T(128)}, s32[]{:T(128)}) while((s32[]{:T(128)}, f32[8,2048,256]{2,1,0:T(8,128)}, f32[8,2048]{1,0:T(8,128)S(1)}, s32[4,256]{1,0:T(4,128)S(1)}, ...), condition=%wide.region_84.87_spmd, body=%wide.region_82.86_spmd.sunk | while | flops 1084227584 | bytes 2687093 | solution.py:357
  853.5 95.4 %reduce-scatter.45.cloned.1.call-done = f32[1152,512]{1,0:T(8,128)} async-done(((f32[4608,512]{1,0:T(8,128)}), f32[1152,512]{1,0:T(8,128)}) %reduce-scatter.45.cloned.1.call-update) | async-done | bytes 2359312 | tf_op jit(solution)/shard_map/reduce_scatter | solution.py:161
  952.1 94.9 %reduce-scatter.47.cloned.1.call-done = f32[1152,512]{1,0:T(8,128)} async-done(((f32[4608,512]{1,0:T(8,128)}), f32[1152,512]{1,0:T(8,128)}) %reduce-scatter.47.cloned.1.call-update) | async-done | bytes 2359312 | tf_op jit(solution)/shard_map/reduce_scatter | solution.py:161
  1050.1 95.0 %reduce-scatter.49.cloned.1.call-done = f32[1152,512]{1,0:T(8,128)} async-done(((f32[4608,512]{1,0:T(8,128)}), f32[1152,512]{1,0:T(8,128)}) %reduce-scatter.49.cloned.1.call-update) | async-done | bytes 2359312 | tf_op jit(solution)/shard_map/reduce_scatter | solution.py:161
  1148.3 94.9 %reduce-scatter.51.cloned.1.call-done = f32[1152,512]{1,0:T(8,128)} async-done(((f32[4608,512]{1,0:T(8,128)}), f32[1152,512]{1,0:T(8,128)}) %reduce-scatter.51.cloned.1.call-update) | async-done | bytes 2359312 | tf_op jit(solution)/shard_map/reduce_scatter | solution.py:161
  1247.7 28.4 %reduce-scatter.77.cloned.1.call-done = f32[32,128]{1,0:T(8,128)} async-done(((f32[256,128]{1,0:T(8,128)}), f32[32,128]{1,0:T(8,128)}) %reduce-scatter.77.cloned.1.call-update) | async-done | bytes 16400
  1277.0 30.4 %reduce-scatter.79.cloned.1.call-done = f32[32,128]{1,0:T(8,128)} async-done(((f32[256,128]{1,0:T(8,128)}), f32[32,128]{1,0:T(8,128)}) %reduce-scatter.79.cloned.1.call-update) | async-done | bytes 16400
  1308.9 30.5 %reduce-scatter.43.cloned.1.call-done = f32[192,64]{0,1:T(8,128)} async-done(((f32[192,512]{0,1:T(8,128)}), f32[192,64]{0,1:T(8,128)}) %reduce-scatter.43.cloned.1.call-update) | async-done | bytes 49168 | tf_op jit(solution)/shard_map/reduce_scatter | solution.py:162
  1339.4 31.9 %reduce-scatter.41.cloned.1.call-done = f32[192,64]{0,1:T(8,128)} async-done(((f32[192,512]{0,1:T(8,128)}), f32[192,64]{0,1:T(8,128)}) %reduce-scatter.41.cloned.1.call-update) | async-done | bytes 49168 | tf_op jit(solution)/shard_map/reduce_scatter | solution.py:162
  1372.8 285.5 %all-reduce.41.cloned.1.call-done = (f32[16384]{0:T(1024)}, f32[16384,256]{1,0:T(8,128)}) async-done(((f32[16384]{0:T(1024)}, f32[16384,256]{1,0:T(8,128)}), (f32[16384]{0:T(1024)}, f32[16384,256]{1,0:T(8,128)})) %all-reduce.41.cloned.1.call-update) | async-done | bytes 16842768 | tf_op jit(solution)/shard_map/psum | solution.py:360
  1661.2 31.3 %reduce-scatter.75.cloned.1.call-done = f32[64,512]{1,0:T(8,128)} async-done(((f32[512,512]{1,0:T(8,128)}), f32[64,512]{1,0:T(8,128)}) %reduce-scatter.75.cloned.1.call-update) | async-done | bytes 131088
  1692.5 33.3 %reduce-scatter.73.cloned.1.call-done = f32[64,512]{1,0:T(8,128)} async-done(((f32[512,512]{1,0:T(8,128)}), f32[64,512]{1,0:T(8,128)}) %reduce-scatter.73.cloned.1.call-update) | async-done | bytes 131088
  1727.5 35.5 %reduce-scatter.65.cloned.1.call-done = f32[64,1152]{1,0:T(8,128)} async-done(((f32[512,1152]{1,0:T(8,128)}), f32[64,1152]{1,0:T(8,128)}) %reduce-scatter.65.cloned.1.call-update) | async-done | bytes 294928
  1763.0 37.8 %reduce-scatter.67.cloned.1.call-done = f32[64,1152]{1,0:T(8,128)} async-done(((f32[512,1152]{1,0:T(8,128)}), f32[64,1152]{1,0:T(8,128)}) %reduce-scatter.67.cloned.1.call-update) | async-done | bytes 294928
  1800.8 37.7 %reduce-scatter.69.cloned.1.call-done = f32[64,1152]{1,0:T(8,128)} async-done(((f32[512,1152]{1,0:T(8,128)}), f32[64,1152]{1,0:T(8,128)}) %reduce-scatter.69.cloned.1.call-update) | async-done | bytes 294928
  1838.5 37.8 %reduce-scatter.71.cloned.1.call-done = f32[64,1152]{1,0:T(8,128)} async-done(((f32[512,1152]{1,0:T(8,128)}), f32[64,1152]{1,0:T(8,128)}) %reduce-scatter.71.cloned.1.call-update) | async-done | bytes 294928
  1881.3 38.5 %all-reduce.37 = (f32[1]{0:T(128)}, f32[1]{0:T(128)}, f32[]{:T(128)}, f32[8,512]{1,0:T(8,128)}) all-reduce(f32[1]{0:T(128)} %bitcast.179, f32[1]{0:T(128)} %bitcast.177, f32[]{:T(128)S(6)} %add.1351, f32[8,512]{1,0:T(8,128)} %stack.107), channel_id=1, replica_groups=mesh['dp'=8,'fsdp'=4] {'dp','fsdp'}, use_global_device_ids=true, to_apply=%region_29.32 | all-reduce | flops 4099 | bytes 32792 | tf_op jit(solution)/shard_map/psum | solution.py:324
  (1059 shorter events, 723.4 us)
Async XLA Ops:
  10.9 317.6 %all-gather.47.cloned.1.call-start = ((), (), s32[]{:S(2)}) async-start(), calls=%async_computation.42 | async-start | bytes 1327104 | tf_op jit(solution)/shard_map/all_gather | solution.py:152
  11.5 324.9 %all-gather.33.cloned.1.call-start = ((), (), s32[]{:S(2)}) async-start(), calls=%async_computation.35 | async-start | bytes 5898240 | tf_op jit(solution)/shard_map/all_gather | solution.py:153
  38.0 334.7 %all-gather.37.cloned.1.call-start = ((), (), s32[]{:S(2)}) async-start(), calls=%async_computation.37 | async-start | bytes 5898240 | tf_op jit(solution)/shard_map/all_gather | solution.py:153
  62.7 324.6 %all-gather.39.cloned.1.call-start = ((), (), s32[]{:S(2)}) async-start(), calls=%async_computation.38 | async-start | bytes 2621440 | tf_op jit(solution)/shard_map/all_gather | solution.py:153
  80.1 311.3 %all-gather.41.cloned.1.call-start = ((), (), s32[]{:S(2)}) async-start(), calls=%async_computation.39 | async-start | bytes 2621440 | tf_op jit(solution)/shard_map/all_gather | solution.py:153
  96.0 331.4 %all-gather.45.cloned.1.call-start = ((), (), s32[]{:S(2)}) async-start(), calls=%async_computation.41 | async-start | bytes 5898240 | tf_op jit(solution)/shard_map/all_gather | solution.py:153
  268.0 185.9 %all-gather.49.cloned.1.call-start = ((), (), s32[]{:S(2)}) async-start(), calls=%async_computation.43 | async-start | bytes 5898240 | tf_op jit(solution)/shard_map/all_gather | solution.py:153
  328.6 459.2 %reduce-scatter.57.cloned.1.call-start = ((), (), s32[]{:S(2)}) async-start(), calls=%async_computation.32 | async-start | bytes 655360 | tf_op jit(solution)/shard_map/reduce_scatter | solution.py:161
  608.5 181.1 %reduce-scatter.59.cloned.1.call-start = ((), (), s32[]{:S(2)}) async-start(), calls=%async_computation.33 | async-start | bytes 655360 | tf_op jit(solution)/shard_map/reduce_scatter | solution.py:161
  714.6 234.4 %reduce-scatter.45.cloned.1.call-start = ((), (), s32[]{:S(2)}) async-start(), calls=%async_computation.26 | async-start | bytes 11796480 | tf_op jit(solution)/shard_map/reduce_scatter | solution.py:161
  731.5 315.5 %reduce-scatter.47.cloned.1.call-start = ((), (), s32[]{:S(2)}) async-start(), calls=%async_computation.27 | async-start | bytes 11796480 | tf_op jit(solution)/shard_map/reduce_scatter | solution.py:161
  748.9 396.3 %reduce-scatter.49.cloned.1.call-start = ((), (), s32[]{:S(2)}) async-start(), calls=%async_computation.28 | async-start | bytes 11796480 | tf_op jit(solution)/shard_map/reduce_scatter | solution.py:161
  770.7 472.5 %reduce-scatter.51.cloned.1.call-start = ((), (), s32[]{:S(2)}) async-start(), calls=%async_computation.29 | async-start | bytes 11796480 | tf_op jit(solution)/shard_map/reduce_scatter | solution.py:161
  787.8 488.4 %reduce-scatter.77.cloned.1.call-start = ((), (), s32[]{:S(2)}) async-start(), calls=%async_computation.52 | async-start | bytes 147456
  789.6 517.9 %reduce-scatter.79.cloned.1.call-start = ((), (), s32[]{:S(2)}) async-start(), calls=%async_computation.53 | async-start | bytes 147456
  791.3 548.0 %reduce-scatter.43.cloned.1.call-start = ((), (), s32[]{:S(2)}) async-start(), calls=%async_computation.25 | async-start | bytes 589824 | tf_op jit(solution)/shard_map/reduce_scatter | solution.py:162
  793.4 577.8 %reduce-scatter.41.cloned.1.call-start = ((), (), s32[]{:S(2)}) async-start(), calls=%async_computation.24 | async-start | bytes 589824 | tf_op jit(solution)/shard_map/reduce_scatter | solution.py:162
  795.6 862.7 %all-reduce.41.cloned.1.call-start = ((), (), s32[]{:S(2)}) async-start(), calls=%async_computation.54 | async-start | bytes 33685504 | tf_op jit(solution)/shard_map/psum | solution.py:360
  846.2 846.3 %reduce-scatter.75.cloned.1.call-start = ((), (), s32[]{:S(2)}) async-start(), calls=%async_computation.51 | async-start | bytes 1179648
  848.9 877.0 %reduce-scatter.73.cloned.1.call-start = ((), (), s32[]{:S(2)}) async-start(), calls=%async_computation.50 | async-start | bytes 1179648
  853.5 909.5 %reduce-scatter.65.cloned.1.call-start = ((), (), s32[]{:S(2)}) async-start(), calls=%async_computation.46 | async-start | bytes 2654208
  952.0 848.8 %reduce-scatter.67.cloned.1.call-start = ((), (), s32[]{:S(2)}) async-start(), calls=%async_computation.47 | async-start | bytes 2654208
  1050.1 788.4 %reduce-scatter.69.cloned.1.call-start = ((), (), s32[]{:S(2)}) async-start(), calls=%async_computation.48 | async-start | bytes 2654208
  1148.3 728.1 %reduce-scatter.71.cloned.1.call-start = ((), (), s32[]{:S(2)}) async-start(), calls=%async_computation.49 | async-start | bytes 2654208
  (236 other events, 3958.6 us)
Sparse Core Ops, SparseCore 0:
  113.5 56.7 all-gather.32
  172.6 57.1 all-gather.36
  231.6 35.1 all-gather.38
  268.6 40.9 all-gather.40
  312.0 57.1 all-gather.44
  370.9 57.0 all-gather.48
  669.2 30.8 reduce-scatter.62
  707.6 31.8 reduce-scatter.60
  742.4 52.6 reduce-scatter.54
  798.2 52.6 reduce-scatter.52
  853.9 95.0 reduce-scatter.44
  951.9 95.0 reduce-scatter.46
  1050.1 95.0 reduce-scatter.48
  1148.1 95.0 reduce-scatter.50
  1246.0 30.1 reduce-scatter.76
  1310.3 29.0 reduce-scatter.42
  1342.2 29.0 reduce-scatter.40
  1378.2 279.9 all-reduce.40
  1660.9 31.5 reduce-scatter.74
  1695.2 30.5 reduce-scatter.72
  1728.2 34.7 reduce-scatter.64
  1765.3 35.4 reduce-scatter.66
  1803.0 35.4 reduce-scatter.68
  1840.8 35.4 reduce-scatter.70
  (7 shorter events, 173.6 us)
where the time goes:
time: 1960 us; the launch traced here: 1940 us
  waiting for transfers between devices  1050 us (54%)
  matrix products  257 us (13%)
  blocking collectives  232 us (12%)
  local copies, waits for them, and re-layouts  188 us (10%)
  other arithmetic  170 us (9%)
  between operations  24 us (1%)
    reduce_scatter x8, waiting for transfers between devices, reduce_grad(): rows = lax.psum_scatter(full, 'fsdp', scatter_dimension=0, tiled=True)  382 us
    psum x1, waiting for transfers between devices, on_device(): sums_total, counts_total = lax.psum((sums_all, counts_all), ('dp', 'fsdp'))  285 us
    unnamed x41, waiting for transfers between devices  275 us
    all_gather x6, blocking collectives, fetch(): cols = lax.all_gather(shard.astype(jnp.bfloat16), 'dp', axis=1, tiled=True)  108 us
    dot_general x49, matrix products, along_rows(): lax.dot_general(left, right, (((0,), (0,)), ((), ())), preferred_element_...  103 us
    dot_general x41, matrix products, along_cols(): lax.dot_general(left, right, (((1,), (1,)), ((), ())), preferred_element_...  88.3 us
    reduce_scatter x2, waiting for transfers between devices, reduce_grad(): return lax.psum_scatter(rows, 'dp', scatter_dimension=1, tiled=True)  62.3 us
    unnamed x467, local copies, waits for them, and re-layouts  60.7 us
  transfers between devices with their start and end apart: 35, of which 19 were waited for; matrix products, arithmetic and copies ran while one was open for 24% of the time, Pallas kernels for 0%

commit v1 on v0

v1 whole, which is shorter than its diff:
```python
import functools
import jax
import jax.numpy as jnp
from jax import lax
from jax.experimental import pallas as pl
from jax.experimental.pallas import tpu as pltpu
from jax.sharding import PartitionSpec as P

C = 512
ZD = 256
GROUPS = 32
SIDE = 32
STEP = 5
COMMIT_WEIGHT = 0.25
CLIP_AT = 1e-05
EMA_DECAY = 0.8
WEIGHT_RATE = 0.03
GAIN_RATE = 0.4
ROWS = SIDE * SIDE
PAD = SIDE
HIGH = lax.Precision.HIGHEST
F32 = jnp.float32
BF16 = jnp.bfloat16
VMEM_LIMIT = 60 * 1024 * 1024


def sigmoid(v):
    return 1.0 / (1.0 + jnp.exp(-v))


def nt(left, right):
    return lax.dot_general(left, right, (((1,), (1,)), ((), ())), preferred_element_type=F32)


def nn(left, right):
    return lax.dot_general(left, right, (((1,), (0,)), ((), ())), preferred_element_type=F32)


def image_mean(sums, group):
    width = C // GROUPS
    row = lax.broadcasted_iota(jnp.int32, (C, C), 0) // width
    col = lax.broadcasted_iota(jnp.int32, (C, C), 1) // width
    same_group = (row == col).astype(F32)
    left = lax.broadcasted_iota(jnp.int32, (16, 16), 0)
    right = lax.broadcasted_iota(jnp.int32, (16, 16), 1)
    same_image = (((left >> 2) >> group) == ((right >> 2) >> group)) & (
        ((left & 3) >> group) == ((right & 3) >> group)
    )
    side = 8 << group
    count = (side * side * width).astype(F32)
    spread = lax.dot_general(
        sums, same_group, (((1,), (0,)), ((), ())), precision=HIGH, preferred_element_type=F32
    )
    total = lax.dot_general(
        same_image.astype(F32), spread, (((1,), (0,)), ((), ())), precision=HIGH, preferred_element_type=F32
    )
    return total / count


def tile_rows(block):
    return jnp.sum(block.reshape(4, 8, C), axis=1)


def spread_rows(ref, tiles):
    for ty in range(4):
        for tx in range(4):
            t = 4 * ty + tx
            ref[ty, 8 * tx : 8 * tx + 8, :] = jnp.broadcast_to(tiles[t : t + 1, :], (8, C))


def norm_stats(x_ref, group, mean_ref, rstd_ref):
    parts = []
    for ty in range(4):
        acc = x_ref[pl.ds(ty * 256, 32), :]
        for y in range(1, 8):
            acc = acc + x_ref[pl.ds(ty * 256 + y * 32, 32), :]
        parts.append(tile_rows(acc))
    spread_rows(mean_ref, image_mean(jnp.concatenate(parts, axis=0), group))
    parts = []
    for ty in range(4):
        mu = mean_ref[ty]
        acc = jnp.zeros((32, C), F32)
        for y in range(8):
            cen = x_ref[pl.ds(ty * 256 + y * 32, 32), :] - mu
            acc = acc + cen * cen
        parts.append(tile_rows(acc))
    var = image_mean(jnp.concatenate(parts, axis=0), group)
    spread_rows(rstd_ref, lax.rsqrt(var + 1e-05))


def store_shifts(ref, y, val, side):
    x = lax.broadcasted_iota(jnp.int32, (32, C), 0) & (side - 1)
    zero = jnp.zeros((32, C), F32)
    left = jnp.where(x != 0, pltpu.roll(val, 1, 0), zero)
    right = jnp.where(x != side - 1, pltpu.roll(val, 31, 0), zero)
    rows = pl.ds(pl.multiple_of(PAD + y * 32, 32), 32)
    ref[rows, 0:C] = left.astype(BF16)
    ref[rows, C : 2 * C] = val.astype(BF16)
    ref[rows, 2 * C : 3 * C] = right.astype(BF16)


def clear_pads(ref):
    ref[0:PAD, :] = jnp.zeros((PAD, 3 * C), BF16)
    ref[PAD + ROWS : 2 * PAD + ROWS, :] = jnp.zeros((PAD, 3 * C), BF16)


def row_mask(shape, dim, dy, side):
    y = (lax.broadcasted_iota(jnp.int32, shape, dim) // 32) & (side - 1)
    return y != 0 if dy < 0 else y != side - 1


def conv_fwd_kernel(has_res, sg_ref, x_ref, gain_ref, wt_hbm, *rest):
    if has_res:
        res_ref, t_ref, a3_ref, wt_ref, mean_ref, rstd_ref, sem = rest
    else:
        t_ref, a3_ref, wt_ref, mean_ref, rstd_ref, sem = rest
    copy = pltpu.make_async_copy(wt_hbm, wt_ref, sem)
    copy.start()
    group = sg_ref[0]
    side = 8 << group
    norm_stats(x_ref, group, mean_ref, rstd_ref)
    clear_pads(a3_ref)
    gamma = gain_ref[0:1, :]
    beta = gain_ref[1:2, :]

    def body(y, carry):
        ty = y // 8
        v = (x_ref[pl.ds(pl.multiple_of(y * 32, 32), 32), :] - mean_ref[ty]) * rstd_ref[ty] * gamma + beta
        store_shifts(a3_ref, y, v * sigmoid(v), side)
        return carry

    lax.fori_loop(0, 32, body, 0, unroll=2)
    copy.wait()
    out = nt(a3_ref[PAD : PAD + ROWS, :], wt_ref[:, 3 * C : 6 * C])
    if has_res:
        out = out + res_ref[...]
    t_ref[...] = out
    for dy in (-1, 1):
        part = nt(a3_ref[PAD + 32 * dy : PAD + 32 * dy + ROWS, :], wt_ref[:, (dy + 1) * 3 * C : (dy + 2) * 3 * C])
        t_ref[...] += jnp.where(row_mask((ROWS, 1), 0, dy, side), part, 0.0)


SMEM = pl.BlockSpec(memory_space=pltpu.SMEM)
VM = pl.BlockSpec(memory_space=pltpu.VMEM)
ANY = pl.BlockSpec(memory_space=pl.ANY)
PARAMS = pltpu.CompilerParams(vmem_limit_bytes=VMEM_LIMIT)


def conv_fwd(group, x, gains, wt, res=None):
    args = [group, x, gains, wt] + ([] if res is None else [res])
    return pl.pallas_call(
        functools.partial(conv_fwd_kernel, res is not None),
        out_shape=(
            jax.ShapeDtypeStruct((ROWS, C), F32),
            jax.ShapeDtypeStruct((ROWS + 2 * PAD, 3 * C), BF16),
        ),
        in_specs=[SMEM, VM, VM, ANY] + ([] if res is None else [VM]),
        out_specs=(VM, VM),
        scratch_shapes=[
            pltpu.VMEM((C, 9 * C), BF16),
            pltpu.VMEM((4, 32, C), F32),
            pltpu.VMEM((4, 32, C), F32),
            pltpu.SemaphoreType.DMA,
        ],
        compiler_params=PARAMS,
        name="conv_fwd",
    )(*args)


def conv_bwd_kernel(has_res, out_low, sg_ref, dt_ref, a3_ref, x_ref, gain_ref, wt_hbm, *rest):
    if has_res:
        res_ref, *rest = rest
    dw_ref, dx_ref, dgain_ref, wt_ref, d3_ref, dtt_ref, mean_ref, rstd_ref, ds_ref, sem = rest
    copy = pltpu.make_async_copy(wt_hbm, wt_ref, sem)
    copy.start()
    group = sg_ref[0]
    side = 8 << group
    clear_pads(d3_ref)

    def body(y, carry):
        val = dt_ref[pl.ds(pl.multiple_of(y * 32, 32), 32), :].astype(F32)
        store_shifts(d3_ref, y, val, side)
        return carry

    lax.fori_loop(0, 32, body, 0, unroll=2)
    dtt_ref[1] = dt_ref[...].astype(F32).T.astype(BF16)
    flat = dtt_ref[1]
    for dy in (-1, 1):
        keep = row_mask((1, ROWS), 1, dy, side).astype(BF16)
        dtt_ref[dy + 1] = flat * keep
    for dy in (-1, 0, 1):
        dw = nn(dtt_ref[dy + 1], a3_ref[PAD + 32 * dy : PAD + 32 * dy + ROWS, :])
        dw_ref[:, (dy + 1) * 3 * C : (dy + 2) * 3 * C] = dw.astype(dw_ref.dtype)
    copy.wait()
    for dy in (0, -1, 1):
        part = None
        for dx in (-1, 0, 1):
            t = 3 * (dy + 1) + dx + 1
            one = nn(
                d3_ref[PAD - 32 * dy : PAD - 32 * dy + ROWS, (1 - dx) * C : (2 - dx) * C],
                wt_ref[:, t * C : (t + 1) * C],
            )
            part = one if part is None else part + one
        if dy == 0:
            ds_ref[...] = part
        else:
            ds_ref[...] += jnp.where(row_mask((ROWS, 1), 0, -dy, side), part, 0.0)
    norm_stats(x_ref, group, mean_ref, rstd_ref)
    gamma = gain_ref[0:1, :]
    beta = gain_ref[1:2, :]
    first, second = [], []
    for ty in range(4):
        mu, rs = mean_ref[ty], rstd_ref[ty]

        def step(y, carry, ty=ty, mu=mu, rs=rs):
            one, two = carry
            rows = pl.ds(pl.multiple_of(ty * 256 + y * 32, 32), 32)
            xh = (x_ref[rows, :] - mu) * rs
            v = xh * gamma + beta
            sg = sigmoid(v)
            ds = ds_ref[rows, :] * (sg * (1.0 + v * (1.0 - sg)))
            ds_ref[rows, :] = ds
            return (one + ds, two + ds * xh)

        zero = jnp.zeros((32, C), F32)
        one, two = lax.fori_loop(0, 8, step, (zero, zero))
        first.append(tile_rows(one))
        second.append(tile_rows(two))
    first = jnp.concatenate(first, axis=0)
    second = jnp.concatenate(second, axis=0)
    dgain_ref[0:1, :] = jnp.sum(second, axis=0, keepdims=True)
    dgain_ref[1:2, :] = jnp.sum(first, axis=0, keepdims=True)
    m_one = image_mean(first * gamma, group)
    m_two = image_mean(second * gamma, group)
    for ty in range(4):
        mu, rs = mean_ref[ty], rstd_ref[ty]
        one = jnp.concatenate([jnp.broadcast_to(m_one[4 * ty + tx : 4 * ty + tx + 1, :], (8, C)) for tx in range(4)], axis=0)
        two = jnp.concatenate([jnp.broadcast_to(m_two[4 * ty + tx : 4 * ty + tx + 1, :], (8, C)) for tx in range(4)], axis=0)

        def step(y, carry, ty=ty, mu=mu, rs=rs, one=one, two=two):
            rows = pl.ds(pl.multiple_of(ty * 256 + y * 32, 32), 32)
            xh = (x_ref[rows, :] - mu) * rs
            dx = rs * (ds_ref[rows, :] * gamma - one - xh * two)
            if has_res:
                dx = dx + res_ref[rows, :]
            dx_ref[rows, :] = dx.astype(dx_ref.dtype)
            return carry

        lax.fori_loop(0, 8, step, 0)


def conv_bwd(group, dt, a3, x, gains, wt, res=None, low=True, grad_type=BF16):
    args = [group, dt, a3, x, gains, wt] + ([] if res is None else [res])
    return pl.pallas_call(
        functools.partial(conv_bwd_kernel, res is not None, low),
        out_shape=(
            jax.ShapeDtypeStruct((C, 9 * C), grad_type),
            jax.ShapeDtypeStruct((ROWS, C), BF16 if low else F32),
            jax.ShapeDtypeStruct((2, C), F32),
        ),
        in_specs=[SMEM, VM, VM, VM, VM, ANY] + ([] if res is None else [VM]),
        out_specs=(VM, VM, VM),
        scratch_shapes=[
            pltpu.VMEM((C, 9 * C), BF16),
            pltpu.VMEM((ROWS + 2 * PAD, 3 * C), BF16),
            pltpu.VMEM((3, C, ROWS), BF16),
            pltpu.VMEM((4, 32, C), F32),
            pltpu.VMEM((4, 32, C), F32),
            pltpu.VMEM((ROWS, C), F32),
            pltpu.SemaphoreType.DMA,
        ],
        compiler_params=PARAMS,
        name="conv_bwd",
    )(*args)


def silu_slope(value):
    gate = sigmoid(value)
    return gate * (1.0 + value * (1.0 - gate))


def transposed(value):
    return value.astype(F32).T.astype(BF16)


HALF = SIDE // 2
LAT = HALF * HALF


def to_depth(src_ref, lanes_ref, dst_ref):
    for k in range(C // 128):
        lanes_ref[k] = src_ref[:, k * 128 : (k + 1) * 128]
    for k in range(C // 128):
        for b in range(2):
            block = lanes_ref[k, pl.ds(b, ROWS // 2, stride=2), :].reshape(HALF, 2, HALF, 128)
            for a in range(2):
                at = (2 * a + b) * C + k * 128
                dst_ref[:, at : at + 128] = block[:, a].reshape(LAT, 128).astype(dst_ref.dtype)


def from_depth(src_ref, lanes_ref, dst_ref):
    for k in range(C // 128):
        for b in range(2):
            pair = [
                src_ref[:, (2 * a + b) * C + k * 128 : (2 * a + b) * C + (k + 1) * 128].reshape(HALF, 1, HALF, 128)
                for a in range(2)
            ]
            lanes_ref[k, pl.ds(b, ROWS // 2, stride=2), :] = jnp.concatenate(pair, axis=1).reshape(ROWS // 2, 128)
    for k in range(C // 128):
        dst_ref[:, k * 128 : (k + 1) * 128] = lanes_ref[k]


def mid_fwd_kernel(
    h_ref, ws0_ref, wl0_ref, code_ref, wl1_ref, ws1_ref,
    e_ref, d_ref, s_ref, q_ref, y_ref, s2_ref, g_ref, commit_ref, dcom_ref, resid_ref, u_ref, lanes_ref,
):
    to_depth(h_ref, lanes_ref, e_ref)
    d = nt(e_ref[...], ws0_ref[...])
    d_ref[...] = d
    s = (d * sigmoid(d)).astype(BF16)
    s_ref[...] = s
    z = nt(s, wl0_ref[...])
    q = jnp.zeros((LAT, ZD), F32)
    commit = jnp.zeros((LAT, ZD), F32)
    dcom = jnp.zeros((LAT, ZD), F32)
    for k in range(4):
        resid_ref[k * LAT : (k + 1) * LAT, :] = (z - q).astype(BF16)
        q = q + code_ref[k * LAT : (k + 1) * LAT, :].astype(F32)
        diff = z - q
        commit = commit + diff * diff
        dcom = dcom + diff
    commit_ref[...] = jnp.sum(commit, axis=0, keepdims=True)
    dcom_ref[...] = dcom
    quant = (z + (q - z)).astype(BF16)
    q_ref[...] = quant
    y = nn(quant, wl1_ref[...])
    y_ref[...] = y
    s2 = (y * sigmoid(y)).astype(BF16)
    s2_ref[...] = s2
    u_ref[...] = nn(s2, ws1_ref[...])
    from_depth(u_ref, lanes_ref, g_ref)


def mid_fwd(h, ws0, wl0, codes, wl1, ws1):
    shape = jax.ShapeDtypeStruct
    return pl.pallas_call(
        mid_fwd_kernel,
        out_shape=(
            shape((LAT, 4 * C), BF16),
            shape((LAT, C), F32),
            shape((LAT, C), BF16),
            shape((LAT, ZD), BF16),
            shape((LAT, C), F32),
            shape((LAT, C), BF16),
            shape((ROWS, C), F32),
            shape((1, ZD), F32),
            shape((LAT, ZD), F32),
            shape((4 * LAT, ZD), BF16),
        ),
        in_specs=[VM] * 6,
        out_specs=(VM,) * 10,
        scratch_shapes=[pltpu.VMEM((LAT, 4 * C), F32), pltpu.VMEM((C // 128, ROWS, 128), F32)],
        compiler_params=PARAMS,
        name="mid_fwd",
    )(h, ws0, wl0, codes, wl1, ws1)


def mid_bwd_kernel(
    scale, dg_ref, e_ref, d_ref, s_ref, q_ref, y_ref, s2_ref, dcom_ref, ws0_ref, wl0_ref, wl1_ref, ws1_ref,
    dws0_ref, dws1_ref, dwl0_ref, dwl1_ref, dh_ref, du_ref, de_ref, lanes_ref,
):
    to_depth(dg_ref, lanes_ref, du_ref)
    out = dws0_ref.dtype
    ds2 = nt(du_ref[...], ws1_ref[...])
    dy = (ds2 * silu_slope(y_ref[...])).astype(BF16)
    dws1_ref[...] = nn(transposed(s2_ref[...]), du_ref[...]).astype(out)
    dwl1_ref[...] = nn(transposed(q_ref[...]), dy).astype(out)
    dz = (nt(dy, wl1_ref[...]) + scale * dcom_ref[...]).astype(BF16)
    dwl0_ref[...] = nn(transposed(dz), s_ref[...]).astype(out)
    ds = nn(dz, wl0_ref[...])
    dd = (ds * silu_slope(d_ref[...])).astype(BF16)
    dws0_ref[...] = nn(transposed(dd), e_ref[...]).astype(out)
    de_ref[...] = nn(dd, ws0_ref[...])
    from_depth(de_ref, lanes_ref, dh_ref)


def mid_bwd(scale, dg, e, d, s, q, y, s2, dcom, ws0, wl0, wl1, ws1, grad_type=BF16):
    shape = jax.ShapeDtypeStruct
    return pl.pallas_call(
        functools.partial(mid_bwd_kernel, scale),
        out_shape=(
            shape((C, 4 * C), grad_type),
            shape((C, 4 * C), grad_type),
            shape((ZD, C), grad_type),
            shape((ZD, C), grad_type),
            shape((ROWS, C), F32),
        ),
        in_specs=[VM] * 12,
        out_specs=(VM,) * 5,
        scratch_shapes=[
            pltpu.VMEM((LAT, 4 * C), BF16),
            pltpu.VMEM((LAT, 4 * C), F32),
            pltpu.VMEM((C // 128, ROWS, 128), F32),
        ],
        compiler_params=PARAMS,
        name="mid_bwd",
    )(dg, e, d, s, q, y, s2, dcom, ws0, wl0, wl1, ws1)


def head_kernel(total_ref, g_ref, wp_ref, pix_ref, mask_ref, dw_ref, dg_ref, loss_ref, o_ref, dr_ref):
    inv = total_ref[0]
    loss = jnp.zeros((1, pix_ref.shape[1]), F32)
    for i in range(4):
        rows = pl.ds(i * 256, 256)
        g = g_ref[rows, :]
        gate = sigmoid(g)
        o = (g * gate).astype(BF16)
        o_ref[rows, :] = o
        err = nn(o, wp_ref[...]) - pix_ref[rows, :].astype(F32)
        keep = mask_ref[rows, :].astype(F32)
        smooth = jnp.sqrt(err * err + 1.0)
        loss = loss + jnp.sum(keep * (smooth - 1.0), axis=0, keepdims=True)
        dr = (keep * err / smooth / inv).astype(BF16)
        dr_ref[rows, :] = dr
        do = nt(dr, wp_ref[...])
        dg_ref[rows, :] = do * (gate * (1.0 + g * (1.0 - gate)))
    loss_ref[...] = loss
    dw_ref[...] = nn(transposed(o_ref[...]), dr_ref[...]).astype(dw_ref.dtype)


def head(total, g, wp, pix, mask, grad_type=BF16):
    shape = jax.ShapeDtypeStruct
    width = pix.shape[1]
    return pl.pallas_call(
        head_kernel,
        out_shape=(shape((C, width), grad_type), shape((ROWS, C), F32), shape((1, width), F32)),
        in_specs=[SMEM, VM, VM, VM, VM],
        out_specs=(VM,) * 3,
        scratch_shapes=[pltpu.VMEM((ROWS, C), BF16), pltpu.VMEM((ROWS, width), BF16)],
        compiler_params=PARAMS,
        name="head",
    )(total, g, wp, pix, mask)


BOTH = ("dp", "fsdp")
RES_W, PIX_W, SC_W, LAT_W = 9 * C, 768, 4 * C, C


def swap(shard):
    return jnp.swapaxes(shard, -1, -2).astype(BF16)


def exchange(x, axis, mask):
    n = lax.axis_size(axis)
    return lax.ppermute(x, axis, [(i, i ^ mask) for i in range(n)])


def everyone(x):
    n = lax.axis_size("dp") * lax.axis_size("fsdp")
    return lax.all_to_all(jnp.broadcast_to(x[None], (n,) + x.shape), BOTH, 0, 0, tiled=True)


STREAM_MASKS = ((2, 1), (1, 2))


def part_shapes(kind, lanes, blocks, dtype):
    if kind == "mat":
        return [jax.ShapeDtypeStruct((32 * 2 * blocks, 4 * lanes), dtype)]
    if kind == "lat":
        return [jax.ShapeDtypeStruct((32 * blocks, 4 * lanes), dtype)] * 2
    return [jax.ShapeDtypeStruct((4, 32 * 2 * blocks, lanes), dtype)]


def part_place(kind, refs, lanes, stream, dp, f):
    if kind == "lat":
        rows = pl.ds(pl.multiple_of(dp * 32, 32), 32)
        return refs[stream].at[rows, pl.ds(pl.multiple_of(f * lanes, 128), lanes)]
    rows = pl.ds(pl.multiple_of(dp * 64 + stream * 32, 32), 32)
    if kind == "mat":
        return refs[0].at[rows, pl.ds(pl.multiple_of(f * lanes, 128), lanes)]
    return refs[0].at[f, rows, :]


def part_count(kind):
    return 2 if kind == "lat" else 1


def assemble_kernel(parts, z_size, me_ref, *rest):
    pieces = rest[:8]
    outs = rest[8:-1]
    sems = rest[-1]
    dp, f = me_ref[0], me_ref[1]
    copies = []
    for stream in range(2):
        near, far = STREAM_MASKS[stream]
        for far_bit in range(2):
            for core_bit in range(2):
                piece = pieces[stream * 4 + core_bit * 2 + far_bit]
                for near_bit in range(2):
                    for z in range(z_size):
                        at_dp = dp ^ (2 * z + core_bit)
                        at_f = f ^ (near * near_bit + far * far_bit)
                        lane, first = 0, 0
                        for kind, lanes in parts:
                            refs = outs[first : first + part_count(kind)]
                            copies.append(
                                pltpu.make_async_copy(
                                    piece.at[near_bit * z_size + z, :, pl.ds(lane, lanes)],
                                    part_place(kind, refs, lanes, stream, at_dp, at_f),
                                    sems.at[len(copies)],
                                )
                            )
                            lane += lanes
                            first += part_count(kind)
    for copy in copies:
        copy.start()
    for copy in copies:
        copy.wait()


def my_place():
    return jnp.stack([lax.axis_index("dp"), lax.axis_index("fsdp")]).astype(jnp.int32)


def gather_chunk(shard, parts):
    z_size = lax.axis_size("dp") // 2
    lanes = shard.shape[1]
    got = [shard] + [exchange(shard, "dp", 2 * k) for k in range(1, z_size)]
    pieces = []
    for stream in range(2):
        near, far = STREAM_MASKS[stream]
        a = jnp.stack([g[stream * 32 : stream * 32 + 32] for g in got])
        b = jnp.concatenate([a, exchange(a, "fsdp", near)], axis=0)
        c = exchange(b, "fsdp", far)
        pieces += [b, c, exchange(b, "dp", 1), exchange(c, "dp", 1)]
    blocks = 2 * z_size
    shapes = [s for kind, width in parts for s in part_shapes(kind, width, blocks, BF16)]
    return pl.pallas_call(
        functools.partial(assemble_kernel, parts, z_size),
        out_shape=tuple(shapes),
        in_specs=[SMEM] + [ANY] * 8,
        out_specs=(ANY,) * len(shapes),
        scratch_shapes=[pltpu.SemaphoreType.DMA((32 * z_size // 2 * 2 * len(parts),))],
        compiler_params=PARAMS,
        name="assemble",
    )(my_place(), *pieces)


def split_kernel(parts, z_size, me_ref, *rest):
    count = sum(part_count(kind) for kind, _ in parts)
    ins = rest[:count]
    outs = rest[count : count + 2]
    sems = rest[-1]
    dp, f = me_ref[0], me_ref[1]
    copies = []
    for core_bit in range(2):
        for stream in range(2):
            near, far = STREAM_MASKS[stream]
            for far_bit in range(2):
                for near_bit in range(2):
                    for z in range(z_size):
                        at_dp = dp ^ (2 * z + core_bit)
                        at_f = f ^ (near * near_bit + far * far_bit)
                        lane, first = 0, 0
                        for kind, lanes in parts:
                            refs = ins[first : first + part_count(kind)]
                            copies.append(
                                pltpu.make_async_copy(
                                    part_place(kind, refs, lanes, stream, at_dp, at_f),
                                    outs[core_bit].at[
                                        stream, (2 * far_bit + near_bit) * z_size + z, :, pl.ds(lane, lanes)
                                    ],
                                    sems.at[len(copies)],
                                )
                            )
                            lane += lanes
                            first += part_count(kind)
    for copy in copies:
        copy.start()
    for copy in copies:
        copy.wait()


def scatter_chunk(grads, parts):
    z_size = lax.axis_size("dp") // 2
    lanes = sum(width for _, width in parts)
    block = jax.ShapeDtypeStruct((2, 4 * z_size, 32, lanes), BF16)
    keep, send = pl.pallas_call(
        functools.partial(split_kernel, parts, z_size),
        out_shape=(block, block),
        in_specs=[SMEM] + [ANY] * len(grads),
        out_specs=(ANY, ANY),
        scratch_shapes=[pltpu.SemaphoreType.DMA((32 * z_size // 2 * 2 * len(parts),))],
        compiler_params=PARAMS,
        name="split",
    )(my_place(), *grads)
    got = exchange(send, "dp", 1)
    totals = []
    for stream in range(2):
        near, far = STREAM_MASKS[stream]
        a = keep[stream].astype(F32) + got[stream].astype(F32)
        r = exchange(a[2 * z_size :].astype(BF16), "fsdp", far)
        a = a[: 2 * z_size] + r.astype(F32)
        r = exchange(a[z_size:].astype(BF16), "fsdp", near)
        totals.append(a[:z_size] + r.astype(F32))
    both = jnp.concatenate(totals, axis=1)
    total = both[0]
    for k in range(1, z_size):
        total = total + exchange(both[k].astype(BF16), "dp", 2 * k).astype(F32)
    return total


def fetch_whole(shard):
    cols = lax.all_gather(shard.astype(BF16), "dp", axis=1, tiled=True)
    return jnp.swapaxes(lax.all_gather(cols, "fsdp", axis=0, tiled=True), 0, 1)


def reduce_whole(grad):
    rows = lax.psum_scatter(jnp.swapaxes(grad, 0, 1), "fsdp", scatter_dimension=0, tiled=True)
    return jnp.swapaxes(lax.psum_scatter(rows, "dp", scatter_dimension=1, tiled=True), 0, 1)


MIX = (("mat", 512), ("mat", 512), ("lat", 128))
RES = (("mat", 1152),)
RES_PIX = (("mat", 1152), ("pix", 384))


def fetch_all(w_pixel, w_res, w_scale, w_latent, paired):
    if not paired:
        pix = [fetch_whole(w_pixel[i]) for i in range(2)]
        res = [fetch_whole(w_res[i]) for i in range(4)]
        scale = [fetch_whole(w_scale[i]) for i in range(2)]
        latent = [fetch_whole(w_latent[i]) for i in range(2)]
        return pix, res, scale, latent
    res_t, pix_t, scale_t, lat_t = swap(w_res), swap(w_pixel), swap(w_scale), swap(w_latent)
    res0, pix = gather_chunk(jnp.concatenate([res_t[0], pix_t[0], pix_t[1]], axis=1), RES_PIX)
    (res1,) = gather_chunk(res_t[1], RES)
    mix = jnp.concatenate([scale_t[0], scale_t[1], lat_t.reshape(-1, lat_t.shape[2])], axis=1)
    scale0, scale1, lat0, lat1 = gather_chunk(mix, MIX)
    (res2,) = gather_chunk(res_t[2], RES)
    (res3,) = gather_chunk(res_t[3], RES)
    half = pix.shape[2] // 2
    pixs = [pix[:, :, i * half : (i + 1) * half].transpose(1, 0, 2).reshape(C, 4 * half) for i in range(2)]
    return pixs, [res0, res1, res2, res3], [scale0, scale1], [lat0, lat1]


def adam_step(weight, moment, second, grad, rate):
    moment_new = 0.5 * moment + 0.5 * grad
    second_new = 0.5 * second + 0.5 * grad * grad
    fix = 1.0 - 0.5**STEP
    weight_new = weight - rate * (
        moment_new / fix / (jnp.sqrt(second_new / fix) + 1e-12) + 0.01 * weight
    )
    return (weight_new, moment_new, second_new)


def exact(left, right, dims):
    return lax.dot_general(left, right, (dims, ((), ())), preferred_element_type=F32)


def code_slots(codes, devices, capacity, rows):
    n = codes.shape[0]
    owner = codes // rows
    hot = (owner[:, None] == jnp.arange(devices, dtype=jnp.int32)[None, :]).astype(BF16)
    at = jnp.arange(n, dtype=jnp.int32)
    before = (at[None, :] < at[:, None]).astype(BF16)
    rank = exact(before, hot, ((1,), (0,)))
    place = jnp.sum(rank * hot.astype(F32), axis=1).astype(jnp.int32)
    slot = owner * capacity + place
    return (jnp.arange(devices * capacity, dtype=jnp.int32)[:, None] == slot[None, :]).astype(BF16)


def on_device(
    pixels,
    valid_mask,
    size_groups,
    code_index,
    w_pixel,
    w_res,
    w_scale,
    w_latent,
    norm_gains,
    moment_pixel,
    moment_res,
    moment_scale,
    moment_latent,
    moment_gains,
    second_pixel,
    second_res,
    second_scale,
    second_latent,
    second_gains,
    ema_counts,
    ema_sums,
):
    n_outer = lax.axis_size("dp")
    n_inner = lax.axis_size("fsdp")
    devices = n_outer * n_inner
    latent_all = code_index.shape[1] * devices
    rows = ema_sums.shape[0]
    paired = n_inner == 4 and w_res.shape[1] == 1152 and w_res.shape[2] == 64
    grad_type = BF16 if paired else F32

    pix_w, res_w, scale_w, lat_w = fetch_all(w_pixel, w_res, w_scale, w_latent, paired)

    valid = everyone(jnp.sum(valid_mask.astype(F32).reshape(-1, 128), axis=0, keepdims=True))
    total_valid = jnp.sum(valid)

    codes = code_index.reshape(-1)
    capacity = max(2, 2 * codes.shape[0] // devices)
    pick = code_slots(codes, devices, capacity, rows)
    local = codes % rows
    cols = jnp.stack([local // 16, local % 16, jnp.ones_like(local)], axis=1).astype(BF16)
    want = exact(pick, cols, ((1,), (0,)))
    wanted = jnp.where(want[:, 2] > 0.5, want[:, 0] * 16.0 + want[:, 1], -1.0).astype(jnp.int32)
    asked = lax.all_to_all(wanted.reshape(devices, 1, capacity), BOTH, 0, 0, tiled=True).reshape(-1)
    hot_rows = (asked[:, None] == jnp.arange(rows, dtype=jnp.int32)[None, :]).astype(BF16)
    book = (ema_sums / ema_counts[:, None]).astype(BF16)
    answer = exact(hot_rows, book, ((1,), (0,))).astype(BF16)
    replies = lax.all_to_all(answer.reshape(devices, capacity, ZD), BOTH, 0, 0, tiled=True).reshape(-1, ZD)
    picked = exact(pick, replies, ((0,), (0,))).astype(BF16)

    gains = [jnp.stack([norm_gains[j], norm_gains[4 + j]]) for j in range(4)]
    h0 = nt(pixels, pix_w[0])
    t1, a1 = conv_fwd(size_groups, h0, gains[0], res_w[0])
    h1, a2 = conv_fwd(size_groups, t1, gains[1], res_w[1], h0)
    e, d, s, quant, y, s2, g0, commit, dcom, resid = mid_fwd(h1, scale_w[0], lat_w[0], picked, lat_w[1], scale_w[1])
    t3, a3 = conv_fwd(size_groups, g0, gains[2], res_w[2])
    g1, a4 = conv_fwd(size_groups, t3, gains[3], res_w[3], g0)

    sent = exact(pick, resid, ((1,), (0,))).astype(BF16)
    held = lax.all_to_all(sent.reshape(devices, capacity, ZD), BOTH, 0, 0, tiled=True).reshape(-1, ZD)
    my_sums = exact(hot_rows, held, ((0,), (0,)))
    my_counts = jnp.sum(hot_rows.astype(F32), axis=0)
    counts_new = EMA_DECAY * ema_counts + (1.0 - EMA_DECAY) * my_counts
    sums_new = EMA_DECAY * ema_sums + (1.0 - EMA_DECAY) * my_sums
    book_new = sums_new / counts_new[:, None]

    d_head, dg1, loss = head(total_valid.reshape(1), g1, pix_w[1], pixels, valid_mask, grad_type)
    d_res3, dt3, dn3 = conv_bwd(size_groups, dg1, a4, t3, gains[3], res_w[3], None, True, grad_type)
    d_res2, dg0, dn2 = conv_bwd(size_groups, dt3, a3, g0, gains[2], res_w[2], dg1, False, grad_type)
    scale = 2.0 * COMMIT_WEIGHT / (latent_all * ZD)
    d_scale0, d_scale1, d_lat0, d_lat1, dh1 = mid_bwd(
        scale, dg0, e, d, s, quant, y, s2, dcom, scale_w[0], lat_w[0], lat_w[1], scale_w[1], grad_type
    )
    d_res1, dt1, dn1 = conv_bwd(size_groups, dh1, a2, t1, gains[1], res_w[1], None, True, grad_type)
    d_res0, dh0, dn0 = conv_bwd(size_groups, dt1, a1, h0, gains[0], res_w[0], dh1, True, grad_type)
    d_patch = exact(dh0, pixels, ((0,), (0,))).astype(grad_type)

    if paired:
        g_res3 = scatter_chunk([d_res3], RES)
        g_res2 = scatter_chunk([d_res2], RES)
        g_mix = scatter_chunk([d_scale0, d_scale1, d_lat0, d_lat1], MIX)
        g_res1 = scatter_chunk([d_res1], RES)
        d_pix = [g.reshape(C, 4, -1).transpose(1, 0, 2) for g in (d_patch, d_head)]
        g_last = scatter_chunk([d_res0, jnp.concatenate(d_pix, axis=2)], RES_PIX)
        wide = w_res.shape[1]
        g_pix = g_last[:, wide:]
        half = g_pix.shape[1] // 2
        grad_pixel = jnp.stack([g_pix[:, :half], g_pix[:, half:]])
        grad_res = jnp.stack([g_last[:, :wide], g_res1, g_res2, g_res3])
        grad_scale = jnp.stack([g_mix[:, :512], g_mix[:, 512:1024]])
        grad_latent = g_mix[:, 1024:].reshape(2, 32, -1)
    else:
        grad_pixel = jnp.stack([reduce_whole(g) for g in (d_patch, d_head)])
        grad_res = jnp.stack([reduce_whole(g) for g in (d_res0, d_res1, d_res2, d_res3)])
        grad_scale = jnp.stack([reduce_whole(g) for g in (d_scale0, d_scale1)])
        grad_latent = jnp.stack([reduce_whole(g) for g in (d_lat0, d_lat1)])

    gain_local = jnp.stack([dn0[0], dn1[0], dn2[0], dn3[0], dn0[1], dn1[1], dn2[1], dn3[1]])
    sums_local = jnp.concatenate(
        [
            gain_local.reshape(-1, 128),
            jnp.sum(loss.reshape(-1, 128), axis=0, keepdims=True),
            jnp.sum(commit.reshape(-1, 128), axis=0, keepdims=True),
        ]
    )
    sums_all = jnp.sum(everyone(sums_local), axis=0)
    grad_gains = sums_all[:-2].reshape(8, C)
    smooth_sum = jnp.sum(sums_all[-2])
    commit_sum = jnp.sum(sums_all[-1])

    squares = jnp.sum(grad_pixel * grad_pixel) + jnp.sum(grad_res * grad_res)
    squares = squares + jnp.sum(grad_scale * grad_scale) + jnp.sum(grad_latent * grad_latent)
    total_squares = jnp.sum(everyone(jnp.broadcast_to(squares, (1, 128)))[:, 0, 0]) + jnp.sum(grad_gains * grad_gains)
    norm = jnp.sqrt(total_squares)
    factor = CLIP_AT / jnp.maximum(norm, CLIP_AT)
    groups_all = [
        (w_pixel, moment_pixel, second_pixel, grad_pixel),
        (w_res, moment_res, second_res, grad_res),
        (w_scale, moment_scale, second_scale, grad_scale),
        (w_latent, moment_latent, second_latent, grad_latent),
    ]
    outputs = [jnp.stack([smooth_sum, total_valid, commit_sum]), norm.reshape(1)]
    for weight, moment, second, grad in groups_all:
        grad = jnp.swapaxes(grad * factor, 1, 2)
        weight_new, moment_new, second_new = adam_step(weight, moment, second, grad, WEIGHT_RATE)
        outputs += [weight_new, moment_new, second_new, weight_new.astype(BF16)]
    outputs += list(adam_step(norm_gains, moment_gains, second_gains, grad_gains * factor, GAIN_RATE))
    outputs += [counts_new, sums_new, book_new, book_new.astype(BF16)]
    return tuple(outputs)


def solution(mesh):
    placed = (
        P(("dp", "fsdp"), None),
        P(("dp", "fsdp"), None),
        P(("dp", "fsdp")),
        P(None, ("dp", "fsdp")),
        P(None, "fsdp", "dp"),
        P(None, "fsdp", "dp"),
        P(None, "fsdp", "dp"),
        P(None, "fsdp", "dp"),
        P(),
        P(None, "fsdp", "dp"),
        P(None, "fsdp", "dp"),
        P(None, "fsdp", "dp"),
        P(None, "fsdp", "dp"),
        P(),
        P(None, "fsdp", "dp"),
        P(None, "fsdp", "dp"),
        P(None, "fsdp", "dp"),
        P(None, "fsdp", "dp"),
        P(),
        P(("dp", "fsdp")),
        P(("dp", "fsdp"), None),
    )
    return jax.shard_map(
        on_device,
        mesh=mesh,
        in_specs=placed,
        out_specs=(
            P(),
            P(),
            P(None, "fsdp", "dp"),
            P(None, "fsdp", "dp"),
            P(None, "fsdp", "dp"),
            P(None, "fsdp", "dp"),
            P(None, "fsdp", "dp"),
            P(None, "fsdp", "dp"),
            P(None, "fsdp", "dp"),
            P(None, "fsdp", "dp"),
            P(None, "fsdp", "dp"),
            P(None, "fsdp", "dp"),
            P(None, "fsdp", "dp"),
            P(None, "fsdp", "dp"),
            P(None, "fsdp", "dp"),
            P(None, "fsdp", "dp"),
            P(None, "fsdp", "dp"),
            P(None, "fsdp", "dp"),
            P(),
            P(),
            P(),
            P(("dp", "fsdp")),
            P(("dp", "fsdp"), None),
            P(("dp", "fsdp"), None),
            P(("dp", "fsdp"), None),
        ),
        check_vma=False,
    )
```

time: 1960 us -> 2210 us (1.13)
  Pallas kernels: 0 us -> 1730 us
  waiting for transfers between devices: 1050 us -> 234 us
  matrix products: 257 us -> 21.8 us
  blocking collectives: 232 us -> 0 us
  local copies, waits for them, and re-layouts: 188 us -> 39 us
  other arithmetic: 170 us -> 41.4 us
  starting transfers between devices: 18.2 us -> 125 us
    pallas_call x0 -> x21, Pallas kernels: none -> 1730 us  [the longest x5 781 us: scatter_chunk(): pl.pallas_call(functools.partial(split_kernel, parts, z_size), out_shape=...]
    reduce_scatter x10 -> x0, waiting for transfers between devices: 445 us -> none  [the longest x8 382 us: reduce_grad(): rows = lax.psum_scatter(full, 'fsdp', scatter_dimension=0, tiled=True)]
    psum x1 -> x0, waiting for transfers between devices: 285 us -> none  [on_device(): sums_total, counts_total = lax.psum((sums_all, counts_all), ('dp', 'fsdp'))]
    unnamed x41 -> x0, waiting for transfers between devices: 275 us -> none
    dot_general x164 -> x8, matrix products: 252 us -> 21.8 us  [the longest x7 18.1 us: exact(): lax.dot_general(left, right, (dims, ((), ())), preferred_element_type=F32)]
    ppermute x0 -> x95, waiting for transfers between devices: none -> 225 us  [exchange(): return lax.ppermute(x, axis, [(i, i ^ mask) for i in range(n)])]
    all_gather x10 -> x0, blocking collectives: 154 us -> none  [the longest x6 108 us: fetch(): cols = lax.all_gather(shard.astype(jnp.bfloat16), 'dp', axis=1, tiled=True)]
    ppermute x0 -> x95, starting transfers between devices: none -> 99.8 us  [exchange(): return lax.ppermute(x, axis, [(i, i ^ mask) for i in range(n)])]
  transfers between devices with their start and end apart: 35 -> 101, of which waited for: 19 -> 47; matrix products, arithmetic and copies ran while one was open for 24% -> 4% of each run, Pallas kernels for 0% -> 56%
where the time goes in v1:
time: 2210 us; the launch traced here: 2200 us
  Pallas kernels  1730 us (78%)
  waiting for transfers between devices  234 us (11%)
  starting transfers between devices  125 us (6%)
  other arithmetic  41.4 us (2%)
  local copies, waits for them, and re-layouts  39 us (2%)
    pallas_call x5, Pallas kernels, scatter_chunk(): pl.pallas_call(functools.partial(split_kernel, parts, z_size), out_shape=...  781 us
    pallas_call x5, Pallas kernels, gather_chunk(): pl.pallas_call(functools.partial(assemble_kernel, parts, z_size), out_sha...  780 us
    ppermute x95, waiting for transfers between devices, exchange(): return lax.ppermute(x, axis, [(i, i ^ mask) for i in range(n)])  225 us
    ppermute x95, starting transfers between devices, exchange(): return lax.ppermute(x, axis, [(i, i ^ mask) for i in range(n)])  99.8 us
    pallas_call x4, Pallas kernels, conv_bwd(): pl.pallas_call(functools.partial(conv_bwd_kernel, res is not None, low),...  92.5 us
    pallas_call x4, Pallas kernels, conv_fwd(): pl.pallas_call(functools.partial(conv_fwd_kernel, res is not None), out_s...  47.3 us
  transfers between devices with their start and end apart: 101, of which 47 were waited for; matrix products, arithmetic and copies ran while one was open for 4% of the time, Pallas kernels for 56%

profile of v1, /device:TPU:0, one launch (start us, length us, event | category | flops | bytes accessed | tf_op | source)
XLA Modules:
  0.0 2196.5 jit_solution(13949319495059046455)
XLA Ops:
  145.8 10.1 collective-permute-done.15.rest_1_
  158.4 10.1 collective-permute-done.26.rest_1_
  188.3 10.0 collective-permute-done.48.rest_1_
  206.4 12.3 collective-permute-done.4.rest_1_
  235.6 145.9 %assemble.6.wt_hbm = bf16[512,4608]{1,0:T(8,128)(2,1)} custom-call(s32[2]{0:T(128)} %pad_add_fusion.me_ref, bf16[8,32,1152]{2,1,0:T(8,128)(2,1)} %copy-done.25, bf16[8,32,1152]{2,1,0:T(8,128)(2,1)} %copy-done.28, bf16[8,32,1152]{2,1,0:T(8,128)(2,1)} %copy-done.29, bf16[8,32,1152]{2,1,0:T(8,128)(2,1)} %copy-done.39, bf16[8,32,1152]{2,1,0:T(8,128)(2,1)} %copy-done.27, ...), custom_call_target="tpu_custom_call" | custom-call | tf_op jit(solution)/shard_map/assemble/pallas_call | solution.py:538
  381.6 148.2 %assemble.7 = (bf16[512,2048]{1,0:T(8,128)(2,1)}, bf16[512,2048]{1,0:T(8,128)(2,1)}, bf16[256,512]{1,0:T(8,128)(2,1)}, bf16[256,512]{1,0:T(8,128)(2,1)}) custom-call(s32[2]{0:T(128)} %pad_add_fusion.me_ref, bf16[8,32,1152]{2,1,0:T(8,128)(2,1)} %copy-done.19, bf16[8,32,1152]{2,1,0:T(8,128)(2,1)} %copy-done.31, bf16[8,32,1152]{2,1,0:T(8,128)(2,1)} %copy-done.33, ...), custom_call_target="tpu_custom_call" | custom-call | tf_op jit(solution)/shard_map/assemble/pallas_call | solution.py:538
  529.7 145.9 %assemble.8.wt_hbm = bf16[512,4608]{1,0:T(8,128)(2,1)} custom-call(s32[2]{0:T(128)} %pad_add_fusion.me_ref, bf16[8,32,1152]{2,1,0:T(8,128)(2,1)} %copy-done.21, bf16[8,32,1152]{2,1,0:T(8,128)(2,1)} %copy-done.36, bf16[8,32,1152]{2,1,0:T(8,128)(2,1)} %copy-done.37, bf16[8,32,1152]{2,1,0:T(8,128)(2,1)} %collective-permute-done.39.rest_3_, ...), custom_call_target="tpu_custom_call" | custom-call | tf_op jit(solution)/shard_map/assemble/pallas_call | solution.py:538
  675.6 145.9 %assemble.9.wt_hbm = bf16[512,4608]{1,0:T(8,128)(2,1)} custom-call(s32[2]{0:T(128)} %pad_add_fusion.me_ref, bf16[8,32,1152]{2,1,0:T(8,128)(2,1)} %constant_dynamic-update-slice_fusion.40.rest_0_, bf16[8,32,1152]{2,1,0:T(8,128)(2,1)} %collective-permute-done.48.rest_1_, bf16[8,32,1152]{2,1,0:T(8,128)(2,1)} %collective-permute-done.49.rest_2_, ...), custom_call_target="tpu_custom_call" | custom-call | tf_op jit(solution)/shard_map/assemble/pallas_call | solution.py:538
  824.7 194.7 %assemble.5 = (bf16[512,4608]{1,0:T(8,128)(2,1)}, bf16[4,512,384]{2,1,0:T(8,128)(2,1)}) custom-call(s32[2]{0:T(128)} %pad_add_fusion.me_ref, bf16[8,32,1536]{2,1,0:T(8,128)(2,1)} %copy-done.12, bf16[8,32,1536]{2,1,0:T(8,128)(2,1)} %copy-done.13, bf16[8,32,1536]{2,1,0:T(8,128)(2,1)} %collective-permute-done.5.rest_2_, ...), custom_call_target="tpu_custom_call" | custom-call | tf_op jit(solution)/shard_map/assemble/pallas_call | solution.py:538
  1025.6 11.5 conv_fwd.4
  1037.1 12.0 conv_fwd.5
  1058.2 11.8 conv_fwd.6
  1070.0 12.0 conv_fwd.7
  1091.3 22.8 %conv_bwd.4 = (bf16[512,4608]{1,0:T(8,128)(2,1)}, bf16[1024,512]{1,0:T(8,128)(2,1)}, f32[2,512]{1,0:T(2,128)}) custom-call(s32[1]{0:T(128)S(6)} %copy.134.sg_ref, f32[1024,512]{1,0:T(8,128)} %get-tuple-element.90.dt_ref.rest_0_, bf16[1088,1536]{1,0:T(8,128)(2,1)} %get-tuple-element.91.a3_ref, f32[1024,512]{1,0:T(8,128)} %get-tuple-element.88.x_ref, ...), custom_call_target="tpu_custom_call" | custom-call | tf_op jit(solution)/shard_map/conv_bwd/pallas_call | solution.py:254
  1114.2 23.7 %conv_bwd.5 = (bf16[512,4608]{1,0:T(8,128)(2,1)}, f32[1024,512]{1,0:T(8,128)}, f32[2,512]{1,0:T(2,128)}) custom-call(s32[1]{0:T(128)S(6)} %copy.134.sg_ref, bf16[1024,512]{1,0:T(8,128)(2,1)} %get-tuple-element.92.dt_ref, bf16[1088,1536]{1,0:T(8,128)(2,1)} %get-tuple-element.93.a3_ref, f32[1024,512]{1,0:T(8,128)} %get-tuple-element.87.x_ref.rest_0_, ...), custom_call_target="tpu_custom_call" | custom-call | tf_op jit(solution)/shard_map/conv_bwd/pallas_call | solution.py:254
  1146.6 22.8 %conv_bwd.6 = (bf16[512,4608]{1,0:T(8,128)(2,1)}, bf16[1024,512]{1,0:T(8,128)(2,1)}, f32[2,512]{1,0:T(2,128)}) custom-call(s32[1]{0:T(128)S(6)} %copy.134.sg_ref, f32[1024,512]{1,0:T(8,128)} %get-tuple-element.102.dt_ref.rest_0_, bf16[1088,1536]{1,0:T(8,128)(2,1)} %get-tuple-element.103.a3_ref, f32[1024,512]{1,0:T(8,128)} %get-tuple-element.81.x_ref, ...), custom_call_target="tpu_custom_call" | custom-call | tf_op jit(solution)/shard_map/conv_bwd/pallas_call | solution.py:254
  1169.5 23.2 %conv_bwd.7 = (bf16[512,4608]{1,0:T(8,128)(2,1)}, bf16[1024,512]{1,0:T(8,128)(2,1)}, f32[2,512]{1,0:T(2,128)}) custom-call(s32[1]{0:T(128)S(6)} %copy.134.sg_ref, bf16[1024,512]{1,0:T(8,128)(2,1)} %get-tuple-element.104.dt_ref, bf16[1088,1536]{1,0:T(8,128)(2,1)} %get-tuple-element.105.a3_ref, f32[1024,512]{1,0:T(8,128)} %convolution_bitcast_fusion.x_ref.rest_0_, ...), custom_call_target="tpu_custom_call" | custom-call | tf_op jit(solution)/shard_map/conv_bwd/pallas_call | solution.py:254
  1193.4 146.0 %split.8 = (bf16[2,16,32,1152]{3,2,1,0:T(8,128)(2,1)}, bf16[2,16,32,1152]{3,2,1,0:T(8,128)(2,1)}) custom-call(s32[2]{0:T(128)} %pad_add_fusion.me_ref, bf16[512,4608]{1,0:T(8,128)(2,1)} %get-tuple-element.123.rest_0_), custom_call_target="tpu_custom_call" | custom-call | tf_op jit(solution)/shard_map/split/pallas_call | solution.py:588
  1355.6 194.7 %split.5 = (bf16[2,16,32,1536]{3,2,1,0:T(8,128)(2,1)}, bf16[2,16,32,1536]{3,2,1,0:T(8,128)(2,1)}) custom-call(s32[2]{0:T(128)} %pad_add_fusion.me_ref, bf16[512,4608]{1,0:T(8,128)(2,1)} %get-tuple-element.112.rest_0_, bf16[4,512,384]{2,1,0:T(8,128)(2,1)} %pad_maximum_fusion.1.rest_1_), custom_call_target="tpu_custom_call" | custom-call | tf_op jit(solution)/shard_map/split/pallas_call | solution.py:588
  1550.7 145.9 %split.7 = (bf16[2,16,32,1152]{3,2,1,0:T(8,128)(2,1)}, bf16[2,16,32,1152]{3,2,1,0:T(8,128)(2,1)}) custom-call(s32[2]{0:T(128)} %pad_add_fusion.me_ref, bf16[512,4608]{1,0:T(8,128)(2,1)} %get-tuple-element.120.rest_0_), custom_call_target="tpu_custom_call" | custom-call | tf_op jit(solution)/shard_map/split/pallas_call | solution.py:588
  1696.8 145.9 %split.6 = (bf16[2,16,32,1152]{3,2,1,0:T(8,128)(2,1)}, bf16[2,16,32,1152]{3,2,1,0:T(8,128)(2,1)}) custom-call(s32[2]{0:T(128)} %pad_add_fusion.me_ref, bf16[512,4608]{1,0:T(8,128)(2,1)} %get-tuple-element.117.rest_0_), custom_call_target="tpu_custom_call" | custom-call | tf_op jit(solution)/shard_map/split/pallas_call | solution.py:588
  1843.1 148.3 %split.9 = (bf16[2,16,32,1152]{3,2,1,0:T(8,128)(2,1)}, bf16[2,16,32,1152]{3,2,1,0:T(8,128)(2,1)}) custom-call(s32[2]{0:T(128)} %pad_add_fusion.me_ref, bf16[512,2048]{1,0:T(8,128)(2,1)} %get-tuple-element.126.rest_0_, bf16[512,2048]{1,0:T(8,128)(2,1)} %get-tuple-element.127.rest_1_, bf16[256,512]{1,0:T(8,128)(2,1)} %get-tuple-element.128.rest_2_, ...), custom_call_target="tpu_custom_call" | custom-call | tf_op jit(solution)/shard_map/split/pallas_call | solution.py:588
  2032.0 9.8 collective-permute-done.72
  2099.0 11.0 collective-permute-done.85
  (541 shorter events, 423.1 us)
Async XLA Ops:
  3.0 110.9 %collective-permute-start = (bf16[64,1536]{1,0:T(8,128)(2,1)S(1)}, bf16[64,1536]{1,0:T(8,128)(2,1)}, u32[]{:S(2)}, u32[]{:S(2)}) collective-permute-start(bf16[64,1536]{1,0:T(8,128)(2,1)S(1)} %concatenate.67), channel_id=1, source_target_pairs={{0,8},{4,12},{8,0},{12,4},{16,24},{20,28},{24,16},{28,20},{1,9},{5... | collective-permute-start | bytes 589832 | tf_op jit(solution)/shard_map/ppermute | solution.py:455
  6.1 106.2 %collective-permute-start.1 = (bf16[64,1536]{1,0:T(8,128)(2,1)S(1)}, bf16[64,1536]{1,0:T(8,128)(2,1)}, u32[]{:S(2)}, u32[]{:S(2)}) collective-permute-start(bf16[64,1536]{1,0:T(8,128)(2,1)S(1)} %concatenate.67), channel_id=1, source_target_pairs={{0,16},{4,20},{8,24},{12,28},{16,0},{20,4},{24,8},{28,12},{1,17},{... | collective-permute-start | bytes 589832 | tf_op jit(solution)/shard_map/ppermute | solution.py:455
  8.6 102.1 %collective-permute-start.2 = (bf16[64,1536]{1,0:T(8,128)(2,1)S(1)}, bf16[64,1536]{1,0:T(8,128)(2,1)}, u32[]{:S(2)}, u32[]{:S(2)}) collective-permute-start(bf16[64,1536]{1,0:T(8,128)(2,1)S(1)} %concatenate.67), channel_id=1, source_target_pairs={{0,24},{4,28},{8,16},{12,20},{16,8},{20,12},{24,0},{28,4},{1,25},{... | collective-permute-start | bytes 589832 | tf_op jit(solution)/shard_map/ppermute | solution.py:455
  8.6 44.9 %collective-permute-start.11 = (bf16[64,1152]{1,0:T(8,128)(2,1)}, bf16[64,1152]{1,0:T(8,128)(2,1)}, u32[]{:S(2)}, u32[]{:S(2)}) collective-permute-start(bf16[64,1152]{1,0:T(8,128)(2,1)} %get-tuple-element.199), channel_id=1, source_target_pairs={{0,8},{4,12},{8,0},{12,4},{16,24},{20,28},{24,16},{28,20},{1,9},{5... | collective-permute-start | bytes 442376 | tf_op jit(solution)/shard_map/ppermute | solution.py:455
  9.5 32.8 %collective-permute-start.13 = (bf16[64,1152]{1,0:T(8,128)(2,1)}, bf16[64,1152]{1,0:T(8,128)(2,1)}, u32[]{:S(2)}, u32[]{:S(2)}) collective-permute-start(bf16[64,1152]{1,0:T(8,128)(2,1)} %get-tuple-element.199), channel_id=1, source_target_pairs={{0,24},{4,28},{8,16},{12,20},{16,8},{20,12},{24,0},{28,4},{1,25},{... | collective-permute-start | bytes 442376 | tf_op jit(solution)/shard_map/ppermute | solution.py:455
  35.2 147.2 %all-to-all-start = ((f32[32,1,128]{2,1,0:T(1,128)}), f32[32,1,128]{2,1,0:T(1,128)S(1)}, u32[]{:S(2)}, u32[]{:S(2)}) async-start(f32[32,1,128]{2,1,0:T(1,128)} %broadcast_in_dim.12), calls=%async_computation | async-start | bytes 32768 | tf_op jit(solution)/shard_map/all_to_all | solution.py:460
  128.5 27.4 %collective-permute-start.15 = (bf16[8,32,1152]{2,1,0:T(8,128)(2,1)S(1)}, bf16[8,32,1152]{2,1,0:T(8,128)(2,1)S(1)}, u32[]{:S(2)}, u32[]{:S(2)}) collective-permute-start(bf16[8,32,1152]{2,1,0:T(8,128)(2,1)S(1)} %constant_dynamic-update-slice_fusion.10.rest_0_), channel_id=1, source_target_pairs={{0,1},{1,0},{2,3},{3,2},{4,5},{5,4},{6,7},{7,6},{8,9},{9,8},{10,11... | collective-permute-start | bytes 1769480 | tf_op jit(solution)/shard_map/ppermute | solution.py:455
  182.4 639.1 %all-to-all-start.2 = ((bf16[32,64,256]{2,1,0:T(8,128)(2,1)}), bf16[32,64,256]{2,1,0:T(8,128)(2,1)S(1)}, u32[]{:S(2)}, u32[]{:S(2)}) async-start(bf16[32,64,256]{2,1,0:T(8,128)(2,1)} %bitcast.41), calls=%async_computation.2 | async-start | bytes 2097152 | tf_op jit(solution)/shard_map/all_to_all | solution.py:720
  186.6 32.2 %collective-permute-start.4 = (bf16[8,32,1536]{2,1,0:T(8,128)(2,1)S(1)}, bf16[8,32,1536]{2,1,0:T(8,128)(2,1)S(1)}, u32[]{:S(2)}, u32[]{:S(2)}) collective-permute-start(bf16[8,32,1536]{2,1,0:T(8,128)(2,1)S(1)} %constant_dynamic-update-slice_fusion.rest_0_), channel_id=1, source_target_pairs={{0,1},{1,0},{2,3},{3,2},{4,5},{5,4},{6,7},{7,6},{8,9},{9,8},{10,11... | collective-permute-start | bytes 2359304 | tf_op jit(solution)/shard_map/ppermute | solution.py:455
  198.7 27.3 %collective-permute-start.17 = (bf16[8,32,1152]{2,1,0:T(8,128)(2,1)}, bf16[8,32,1152]{2,1,0:T(8,128)(2,1)S(1)}, u32[]{:S(2)}, u32[]{:S(2)}) collective-permute-start(bf16[8,32,1152]{2,1,0:T(8,128)(2,1)} %copy-done.28), channel_id=1, source_target_pairs={{0,4},{4,0},{8,12},{12,8},{16,20},{20,16},{24,28},{28,24},{1,5},{5... | collective-permute-start | bytes 1769480 | tf_op jit(solution)/shard_map/ppermute | solution.py:455
  227.4 448.2 %collective-permute-start.54 = (bf16[8,32,1152]{2,1,0:T(8,128)(2,1)}, bf16[8,32,1152]{2,1,0:T(8,128)(2,1)}, u32[]{:S(2)}, u32[]{:S(2)}) collective-permute-start(bf16[8,32,1152]{2,1,0:T(8,128)(2,1)} %collective-permute-done.52.rest_5_), channel_id=1, source_target_pairs={{0,4},{4,0},{8,12},{12,8},{16,20},{20,16},{24,28},{28,24},{1,5},{5... | collective-permute-start | bytes 1769480 | tf_op jit(solution)/shard_map/ppermute | solution.py:455
  227.9 596.8 %collective-permute-start.5 = (bf16[8,32,1536]{2,1,0:T(8,128)(2,1)S(1)}, bf16[8,32,1536]{2,1,0:T(8,128)(2,1)}, u32[]{:S(2)}, u32[]{:S(2)}) collective-permute-start(bf16[8,32,1536]{2,1,0:T(8,128)(2,1)S(1)} %constant_dynamic-update-slice_fusion.rest_0_), channel_id=1, source_target_pairs={{0,4},{4,0},{8,12},{12,8},{16,20},{20,16},{24,28},{28,24},{1,5},{5... | collective-permute-start | bytes 2359304 | tf_op jit(solution)/shard_map/ppermute | solution.py:455
  228.4 596.3 %collective-permute-start.9 = (bf16[8,32,1536]{2,1,0:T(8,128)(2,1)S(1)}, bf16[8,32,1536]{2,1,0:T(8,128)(2,1)}, u32[]{:S(2)}, u32[]{:S(2)}) collective-permute-start(bf16[8,32,1536]{2,1,0:T(8,128)(2,1)S(1)} %constant_dynamic-update-slice_fusion.5.rest_4_), channel_id=1, source_target_pairs={{0,4},{4,0},{8,12},{12,8},{16,20},{20,16},{24,28},{28,24},{1,5},{5... | collective-permute-start | bytes 2359304 | tf_op jit(solution)/shard_map/ppermute | solution.py:455
  229.3 595.3 %collective-permute-start.6 = (bf16[8,32,1536]{2,1,0:T(8,128)(2,1)S(1)}, bf16[8,32,1536]{2,1,0:T(8,128)(2,1)}, u32[]{:S(2)}, u32[]{:S(2)}) collective-permute-start(bf16[8,32,1536]{2,1,0:T(8,128)(2,1)S(1)} %collective-permute-done.4.rest_1_), channel_id=1, source_target_pairs={{0,4},{4,0},{8,12},{12,8},{16,20},{20,16},{24,28},{28,24},{1,5},{5... | collective-permute-start | bytes 2359304 | tf_op jit(solution)/shard_map/ppermute | solution.py:455
  231.0 593.7 %collective-permute-start.10 = (bf16[8,32,1536]{2,1,0:T(8,128)(2,1)}, bf16[8,32,1536]{2,1,0:T(8,128)(2,1)}, u32[]{:S(2)}, u32[]{:S(2)}) collective-permute-start(bf16[8,32,1536]{2,1,0:T(8,128)(2,1)} %copy-done.14), channel_id=1, source_target_pairs={{0,4},{4,0},{8,12},{12,8},{16,20},{20,16},{24,28},{28,24},{1,5},{5... | collective-permute-start | bytes 2359304 | tf_op jit(solution)/shard_map/ppermute | solution.py:455
  1339.5 666.0 %collective-permute-start.79 = (bf16[2,16,32,1152]{3,2,1,0:T(8,128)(2,1)}, bf16[2,16,32,1152]{3,2,1,0:T(8,128)(2,1)}, u32[]{:S(2)}, u32[]{:S(2)}) collective-permute-start(bf16[2,16,32,1152]{3,2,1,0:T(8,128)(2,1)} %get-tuple-element.125), channel_id=1, source_target_pairs={{0,4},{4,0},{8,12},{12,8},{16,20},{20,16},{24,28},{28,24},{1,5},{5... | collective-permute-start | bytes 7077896 | tf_op jit(solution)/shard_map/ppermute | solution.py:455
  1340.7 653.5 %all-to-all-start.3 = ((f32[32,34,128]{2,1,0:T(8,128)}), f32[32,34,128]{2,1,0:T(8,128)}, u32[]{:S(2)}, u32[]{:S(2)}) async-start(f32[32,34,128]{2,1,0:T(8,128)} %broadcast_in_dim.16), calls=%async_computation.3 | async-start | bytes 1310720 | tf_op jit(solution)/shard_map/all_to_all | solution.py:460
  1550.3 519.7 %collective-permute-start.55 = (bf16[2,16,32,1536]{3,2,1,0:T(8,128)(2,1)}, bf16[2,16,32,1536]{3,2,1,0:T(8,128)(2,1)S(1)}, u32[]{:S(2)}, u32[]{:S(2)}) collective-permute-start(bf16[2,16,32,1536]{3,2,1,0:T(8,128)(2,1)} %get-tuple-element.116), channel_id=1, source_target_pairs={{0,4},{4,0},{8,12},{12,8},{16,20},{20,16},{24,28},{28,24},{1,5},{5... | collective-permute-start | bytes 9437192 | tf_op jit(solution)/shard_map/ppermute | solution.py:455
  1696.6 314.0 %collective-permute-start.71 = (bf16[2,16,32,1152]{3,2,1,0:T(8,128)(2,1)}, bf16[2,16,32,1152]{3,2,1,0:T(8,128)(2,1)}, u32[]{:S(2)}, u32[]{:S(2)}) collective-permute-start(bf16[2,16,32,1152]{3,2,1,0:T(8,128)(2,1)} %get-tuple-element.122), channel_id=1, source_target_pairs={{0,4},{4,0},{8,12},{12,8},{16,20},{20,16},{24,28},{28,24},{1,5},{5... | collective-permute-start | bytes 7077896 | tf_op jit(solution)/shard_map/ppermute | solution.py:455
  1842.7 171.7 %collective-permute-start.63 = (bf16[2,16,32,1152]{3,2,1,0:T(8,128)(2,1)}, bf16[2,16,32,1152]{3,2,1,0:T(8,128)(2,1)}, u32[]{:S(2)}, u32[]{:S(2)}) collective-permute-start(bf16[2,16,32,1152]{3,2,1,0:T(8,128)(2,1)} %get-tuple-element.119), channel_id=1, source_target_pairs={{0,4},{4,0},{8,12},{12,8},{16,20},{20,16},{24,28},{28,24},{1,5},{5... | collective-permute-start | bytes 7077896 | tf_op jit(solution)/shard_map/ppermute | solution.py:455
  1994.2 179.4 %all-to-all-start.5 = ((bf16[32,64,256]{2,1,0:T(8,128)(2,1)}), bf16[32,64,256]{2,1,0:T(8,128)(2,1)}, u32[]{:S(2)}, u32[]{:S(2)}) async-start(bf16[32,64,256]{2,1,0:T(8,128)(2,1)} %bitcast.379), calls=%async_computation.5 | async-start | bytes 2097152 | tf_op jit(solution)/shard_map/all_to_all | solution.py:732
  2014.4 27.4 %collective-permute-start.72 = (bf16[8,32,1152]{2,1,0:T(8,128)(2,1)S(1)}, bf16[8,32,1152]{2,1,0:T(8,128)(2,1)S(1)}, u32[]{:S(2)}, u32[]{:S(2)}) collective-permute-start(bf16[8,32,1152]{2,1,0:T(8,128)(2,1)S(1)} %fusion.39), channel_id=1, source_target_pairs={{0,1},{1,0},{2,3},{3,2},{4,5},{5,4},{6,7},{7,6},{8,9},{9,8},{10,11... | collective-permute-start | bytes 1769480 | tf_op jit(solution)/shard_map/ppermute | solution.py:455
  2081.3 61.2 %collective-permute-start.56 = (bf16[8,32,1536]{2,1,0:T(8,128)(2,1)S(1)}, bf16[8,32,1536]{2,1,0:T(8,128)(2,1)S(1)}, u32[]{:S(2)}, u32[]{:S(2)}) collective-permute-start(bf16[8,32,1536]{2,1,0:T(8,128)(2,1)S(1)} %fusion.35), channel_id=1, source_target_pairs={{0,1},{1,0},{2,3},{3,2},{4,5},{5,4},{6,7},{7,6},{8,9},{9,8},{10,11... | collective-permute-start | bytes 2359304 | tf_op jit(solution)/shard_map/ppermute | solution.py:455
  2087.5 56.3 %collective-permute-start.58 = (bf16[8,32,1536]{2,1,0:T(8,128)(2,1)S(1)}, bf16[8,32,1536]{2,1,0:T(8,128)(2,1)S(1)}, u32[]{:S(2)}, u32[]{:S(2)}) collective-permute-start(bf16[8,32,1536]{2,1,0:T(8,128)(2,1)S(1)} %fusion.36), channel_id=1, source_target_pairs={{0,2},{1,3},{2,0},{3,1},{4,6},{5,7},{6,4},{7,5},{8,10},{9,11},{10,... | collective-permute-start | bytes 2359304 | tf_op jit(solution)/shard_map/ppermute | solution.py:455
  (149 other events, 4203.7 us)

commit v2 on v1

v2 whole, which is shorter than its diff:
```python
import functools
import jax
import jax.numpy as jnp
from jax import lax
from jax.experimental import pallas as pl
from jax.experimental.pallas import tpu as pltpu
from jax.sharding import Mesh
from jax.sharding import PartitionSpec as P

C = 512
ZD = 256
GROUPS = 32
SIDE = 32
STEP = 5
COMMIT_WEIGHT = 0.25
CLIP_AT = 1e-05
EMA_DECAY = 0.8
WEIGHT_RATE = 0.03
GAIN_RATE = 0.4
ROWS = SIDE * SIDE
PAD = SIDE
HIGH = lax.Precision.HIGHEST
F32 = jnp.float32
BF16 = jnp.bfloat16
VMEM_LIMIT = 60 * 1024 * 1024


def sigmoid(v):
    return 1.0 / (1.0 + jnp.exp(-v))


def nt(left, right):
    return lax.dot_general(left, right, (((1,), (1,)), ((), ())), preferred_element_type=F32)


def nn(left, right):
    return lax.dot_general(left, right, (((1,), (0,)), ((), ())), preferred_element_type=F32)


def image_mean(sums, group):
    width = C // GROUPS
    row = lax.broadcasted_iota(jnp.int32, (C, C), 0) // width
    col = lax.broadcasted_iota(jnp.int32, (C, C), 1) // width
    same_group = (row == col).astype(F32)
    left = lax.broadcasted_iota(jnp.int32, (16, 16), 0)
    right = lax.broadcasted_iota(jnp.int32, (16, 16), 1)
    same_image = (((left >> 2) >> group) == ((right >> 2) >> group)) & (
        ((left & 3) >> group) == ((right & 3) >> group)
    )
    side = 8 << group
    count = (side * side * width).astype(F32)
    spread = lax.dot_general(
        sums, same_group, (((1,), (0,)), ((), ())), precision=HIGH, preferred_element_type=F32
    )
    total = lax.dot_general(
        same_image.astype(F32), spread, (((1,), (0,)), ((), ())), precision=HIGH, preferred_element_type=F32
    )
    return total / count


def tile_rows(block):
    return jnp.sum(block.reshape(4, 8, C), axis=1)


def spread_rows(ref, tiles):
    for ty in range(4):
        for tx in range(4):
            t = 4 * ty + tx
            ref[ty, 8 * tx : 8 * tx + 8, :] = jnp.broadcast_to(tiles[t : t + 1, :], (8, C))


def norm_stats(x_ref, group, mean_ref, rstd_ref):
    parts = []
    for ty in range(4):
        acc = x_ref[pl.ds(ty * 256, 32), :]
        for y in range(1, 8):
            acc = acc + x_ref[pl.ds(ty * 256 + y * 32, 32), :]
        parts.append(tile_rows(acc))
    spread_rows(mean_ref, image_mean(jnp.concatenate(parts, axis=0), group))
    parts = []
    for ty in range(4):
        mu = mean_ref[ty]
        acc = jnp.zeros((32, C), F32)
        for y in range(8):
            cen = x_ref[pl.ds(ty * 256 + y * 32, 32), :] - mu
            acc = acc + cen * cen
        parts.append(tile_rows(acc))
    var = image_mean(jnp.concatenate(parts, axis=0), group)
    spread_rows(rstd_ref, lax.rsqrt(var + 1e-05))


def store_shifts(ref, y, val, side):
    x = lax.broadcasted_iota(jnp.int32, (32, C), 0) & (side - 1)
    zero = jnp.zeros((32, C), F32)
    left = jnp.where(x != 0, pltpu.roll(val, 1, 0), zero)
    right = jnp.where(x != side - 1, pltpu.roll(val, 31, 0), zero)
    rows = pl.ds(pl.multiple_of(PAD + y * 32, 32), 32)
    ref[rows, 0:C] = left.astype(BF16)
    ref[rows, C : 2 * C] = val.astype(BF16)
    ref[rows, 2 * C : 3 * C] = right.astype(BF16)


def clear_pads(ref):
    ref[0:PAD, :] = jnp.zeros((PAD, 3 * C), BF16)
    ref[PAD + ROWS : 2 * PAD + ROWS, :] = jnp.zeros((PAD, 3 * C), BF16)


def row_mask(shape, dim, dy, side):
    y = (lax.broadcasted_iota(jnp.int32, shape, dim) // 32) & (side - 1)
    return y != 0 if dy < 0 else y != side - 1


SHARD = 64
RES = (("mat", 0, 1152),)
MIX = (("mat", 0, 512), ("mat", 512, 512), ("lat", 1024, 128))


def part_shapes(kind, lanes, z_size, dtype):
    rows = 2 * SHARD * z_size
    if kind == "mat":
        return [((rows, 4 * lanes), dtype)]
    if kind == "lat":
        return [((rows // 2, 4 * lanes), dtype)] * 2
    return [((4, rows, lanes), dtype)]


def part_blocks(kind, refs, lanes, dp, f):
    cols = pl.ds(pl.multiple_of(f * lanes, 128), lanes)
    if kind == "lat":
        half = SHARD // 2
        at = pl.ds(pl.multiple_of(dp * half, half), half)
        return [(pl.ds(i * half, half), refs[i].at[at, cols]) for i in range(2)]
    at = pl.ds(pl.multiple_of(dp * SHARD, SHARD), SHARD)
    where = refs[0].at[at, cols] if kind == "mat" else refs[0].at[f, at, :]
    return [(pl.ds(0, SHARD), where)]


def part_count(kind):
    return 2 if kind == "lat" else 1


def copy_count(parts, z_size):
    return 8 * z_size * sum(part_count(kind) for kind, _, _ in parts)


def block_copies(parts, info_ref, pieces, wholes, sems, inward):
    core, f, my_z = info_ref[1], info_ref[2], info_ref[3]
    z_size = pieces[0].shape[0] // 4
    copies = []
    for side in range(2):
        owner = core if side == 0 else 1 - core
        for far in range(2):
            for near in range(2):
                for z in range(z_size):
                    at_f = f ^ ((2 - owner) * near) ^ ((1 + owner) * far)
                    at_dp = 2 * (z if inward else my_z ^ z) + owner
                    first = 0
                    for kind, lane, lanes in parts:
                        refs = wholes[first : first + part_count(kind)]
                        for rows, where in part_blocks(kind, refs, lanes, at_dp, at_f):
                            piece = pieces[side].at[(2 * far + near) * z_size + z, rows, pl.ds(lane, lanes)]
                            ends = (piece, where) if inward else (where, piece)
                            copies.append(pltpu.make_async_copy(*ends, sems.at[len(copies)]))
                        first += part_count(kind)
    return copies


def weight_copies(info_ref, refs, dst_ref, sems):
    if len(refs) == 1:
        return [pltpu.make_async_copy(refs[0], dst_ref, sems.at[0])]
    return block_copies(RES, info_ref, refs, (dst_ref,), sems, True)


def weight_sems(weight):
    return pltpu.SemaphoreType.DMA((1 if len(weight) == 1 else copy_count(RES, weight[0].shape[0] // 4),))


def conv_fwd_kernel(n_weight, has_res, info_ref, x_ref, gain_ref, *rest):
    weight, rest = rest[:n_weight], rest[n_weight:]
    if has_res:
        res_ref, *rest = rest
    t_ref, a3_ref, wt_ref, mean_ref, rstd_ref, sems = rest
    copies = weight_copies(info_ref, weight, wt_ref, sems)
    for copy in copies:
        copy.start()
    group = info_ref[0]
    side = 8 << group
    norm_stats(x_ref, group, mean_ref, rstd_ref)
    clear_pads(a3_ref)
    gamma = gain_ref[0:1, :]
    beta = gain_ref[1:2, :]

    def body(y, carry):
        ty = y // 8
        v = (x_ref[pl.ds(pl.multiple_of(y * 32, 32), 32), :] - mean_ref[ty]) * rstd_ref[ty] * gamma + beta
        store_shifts(a3_ref, y, v * sigmoid(v), side)
        return carry

    lax.fori_loop(0, 32, body, 0, unroll=2)
    for copy in copies:
        copy.wait()
    out = nt(a3_ref[PAD : PAD + ROWS, :], wt_ref[:, 3 * C : 6 * C])
    if has_res:
        out = out + res_ref[...]
    t_ref[...] = out
    for dy in (-1, 1):
        part = nt(a3_ref[PAD + 32 * dy : PAD + 32 * dy + ROWS, :], wt_ref[:, (dy + 1) * 3 * C : (dy + 2) * 3 * C])
        t_ref[...] += jnp.where(row_mask((ROWS, 1), 0, dy, side), part, 0.0)


SMEM = pl.BlockSpec(memory_space=pltpu.SMEM)
VM = pl.BlockSpec(memory_space=pltpu.VMEM)
ANY = pl.BlockSpec(memory_space=pl.ANY)
PARAMS = pltpu.CompilerParams(vmem_limit_bytes=VMEM_LIMIT)
CONV_FLOPS = 2 * ROWS * 9 * C * C


def cost(flops, size):
    return pl.CostEstimate(flops=flops, bytes_accessed=size, transcendentals=0)


def conv_fwd(info, x, gains, weight, res=None):
    args = [info, x, gains, *weight] + ([] if res is None else [res])
    return pl.pallas_call(
        functools.partial(conv_fwd_kernel, len(weight), res is not None),
        out_shape=(
            jax.ShapeDtypeStruct((ROWS, C), F32),
            jax.ShapeDtypeStruct((ROWS + 2 * PAD, 3 * C), BF16),
        ),
        in_specs=[SMEM, VM, VM] + [ANY] * len(weight) + ([] if res is None else [VM]),
        out_specs=(VM, VM),
        scratch_shapes=[
            pltpu.VMEM((C, 9 * C), BF16),
            pltpu.VMEM((4, 32, C), F32),
            pltpu.VMEM((4, 32, C), F32),
            weight_sems(weight),
        ],
        compiler_params=PARAMS,
        cost_estimate=cost(2 * CONV_FLOPS, 12 << 20),
        name="conv_fwd",
    )(*args)


def conv_dw_kernel(split, info_ref, dt_ref, a3_ref, *rest):
    if split:
        keep_ref, send_ref, dw_ref, dtt_ref, sems = rest
    else:
        dw_ref, dtt_ref = rest
    side = 8 << info_ref[0]
    dtt_ref[1] = dt_ref[...].astype(F32).T.astype(BF16)
    flat = dtt_ref[1]
    for dy in (-1, 1):
        keep = row_mask((1, ROWS), 1, dy, side).astype(BF16)
        dtt_ref[dy + 1] = flat * keep
    for dy in (-1, 0, 1):
        dw = nn(dtt_ref[dy + 1], a3_ref[PAD + 32 * dy : PAD + 32 * dy + ROWS, :])
        dw_ref[:, (dy + 1) * 3 * C : (dy + 2) * 3 * C] = dw.astype(dw_ref.dtype)
    if split:
        copies = block_copies(RES, info_ref, (keep_ref, send_ref), (dw_ref,), sems, False)
        for copy in copies:
            copy.start()
        for copy in copies:
            copy.wait()


def conv_dw(info, dt, a3, z_size):
    scratch = [pltpu.VMEM((3, C, ROWS), BF16)]
    if z_size:
        block = jax.ShapeDtypeStruct((4 * z_size, SHARD, 9 * C // 4), BF16)
        shapes, specs = (block, block), (ANY, ANY)
        scratch = [pltpu.VMEM((C, 9 * C), BF16)] + scratch + [pltpu.SemaphoreType.DMA((copy_count(RES, z_size),))]
    else:
        shapes, specs = jax.ShapeDtypeStruct((C, 9 * C), F32), VM
    return pl.pallas_call(
        functools.partial(conv_dw_kernel, z_size),
        out_shape=shapes,
        in_specs=[SMEM, VM, VM],
        out_specs=specs,
        scratch_shapes=scratch,
        compiler_params=PARAMS,
        cost_estimate=cost(2 * CONV_FLOPS, 12 << 20),
        name="conv_dw",
    )(info, dt, a3)


def conv_dx_kernel(n_weight, has_res, info_ref, dt_ref, x_ref, gain_ref, *rest):
    weight, rest = rest[:n_weight], rest[n_weight:]
    if has_res:
        res_ref, *rest = rest
    dx_ref, dgain_ref, wt_ref, d3_ref, mean_ref, rstd_ref, ds_ref, sems = rest
    copies = weight_copies(info_ref, weight, wt_ref, sems)
    for copy in copies:
        copy.start()
    group = info_ref[0]
    side = 8 << group
    clear_pads(d3_ref)

    def body(y, carry):
        val = dt_ref[pl.ds(pl.multiple_of(y * 32, 32), 32), :].astype(F32)
        store_shifts(d3_ref, y, val, side)
        return carry

    lax.fori_loop(0, 32, body, 0, unroll=2)
    norm_stats(x_ref, group, mean_ref, rstd_ref)
    for copy in copies:
        copy.wait()
    for dy in (0, -1, 1):
        part = None
        for dx in (-1, 0, 1):
            t = 3 * (dy + 1) + dx + 1
            one = nn(
                d3_ref[PAD - 32 * dy : PAD - 32 * dy + ROWS, (1 - dx) * C : (2 - dx) * C],
                wt_ref[:, t * C : (t + 1) * C],
            )
            part = one if part is None else part + one
        if dy == 0:
            ds_ref[...] = part
        else:
            ds_ref[...] += jnp.where(row_mask((ROWS, 1), 0, -dy, side), part, 0.0)
    gamma = gain_ref[0:1, :]
    beta = gain_ref[1:2, :]
    first, second = [], []
    for ty in range(4):
        mu, rs = mean_ref[ty], rstd_ref[ty]

        def step(y, carry, ty=ty, mu=mu, rs=rs):
            one, two = carry
            rows = pl.ds(pl.multiple_of(ty * 256 + y * 32, 32), 32)
            xh = (x_ref[rows, :] - mu) * rs
            v = xh * gamma + beta
            sg = sigmoid(v)
            ds = ds_ref[rows, :] * (sg * (1.0 + v * (1.0 - sg)))
            ds_ref[rows, :] = ds
            return (one + ds, two + ds * xh)

        zero = jnp.zeros((32, C), F32)
        one, two = lax.fori_loop(0, 8, step, (zero, zero))
        first.append(tile_rows(one))
        second.append(tile_rows(two))
    first = jnp.concatenate(first, axis=0)
    second = jnp.concatenate(second, axis=0)
    dgain_ref[0:1, :] = jnp.sum(second, axis=0, keepdims=True)
    dgain_ref[1:2, :] = jnp.sum(first, axis=0, keepdims=True)
    m_one = image_mean(first * gamma, group)
    m_two = image_mean(second * gamma, group)
    for ty in range(4):
        mu, rs = mean_ref[ty], rstd_ref[ty]
        one = jnp.concatenate([jnp.broadcast_to(m_one[4 * ty + tx : 4 * ty + tx + 1, :], (8, C)) for tx in range(4)], axis=0)
        two = jnp.concatenate([jnp.broadcast_to(m_two[4 * ty + tx : 4 * ty + tx + 1, :], (8, C)) for tx in range(4)], axis=0)

        def step(y, carry, ty=ty, mu=mu, rs=rs, one=one, two=two):
            rows = pl.ds(pl.multiple_of(ty * 256 + y * 32, 32), 32)
            xh = (x_ref[rows, :] - mu) * rs
            dx = rs * (ds_ref[rows, :] * gamma - one - xh * two)
            if has_res:
                dx = dx + res_ref[rows, :]
            dx_ref[rows, :] = dx.astype(dx_ref.dtype)
            return carry

        lax.fori_loop(0, 8, step, 0)


def conv_dx(info, dt, x, gains, weight, res=None, low=True):
    args = [info, dt, x, gains, *weight] + ([] if res is None else [res])
    return pl.pallas_call(
        functools.partial(conv_dx_kernel, len(weight), res is not None),
        out_shape=(
            jax.ShapeDtypeStruct((ROWS, C), BF16 if low else F32),
            jax.ShapeDtypeStruct((2, C), F32),
        ),
        in_specs=[SMEM, VM, VM, VM] + [ANY] * len(weight) + ([] if res is None else [VM]),
        out_specs=(VM, VM),
        scratch_shapes=[
            pltpu.VMEM((C, 9 * C), BF16),
            pltpu.VMEM((ROWS + 2 * PAD, 3 * C), BF16),
            pltpu.VMEM((4, 32, C), F32),
            pltpu.VMEM((4, 32, C), F32),
            pltpu.VMEM((ROWS, C), F32),
            weight_sems(weight),
        ],
        compiler_params=PARAMS,
        cost_estimate=cost(3 * CONV_FLOPS, 12 << 20),
        name="conv_dx",
    )(*args)


def silu_slope(value):
    gate = sigmoid(value)
    return gate * (1.0 + value * (1.0 - gate))


def transposed(value):
    return value.astype(F32).T.astype(BF16)


HALF = SIDE // 2
LAT = HALF * HALF


def to_depth(src_ref, lanes_ref, dst_ref):
    for k in range(C // 128):
        lanes_ref[k] = src_ref[:, k * 128 : (k + 1) * 128]
    for k in range(C // 128):
        for b in range(2):
            block = lanes_ref[k, pl.ds(b, ROWS // 2, stride=2), :].reshape(HALF, 2, HALF, 128)
            for a in range(2):
                at = (2 * a + b) * C + k * 128
                dst_ref[:, at : at + 128] = block[:, a].reshape(LAT, 128).astype(dst_ref.dtype)


def from_depth(src_ref, lanes_ref, dst_ref):
    for k in range(C // 128):
        for b in range(2):
            pair = [
                src_ref[:, (2 * a + b) * C + k * 128 : (2 * a + b) * C + (k + 1) * 128].reshape(HALF, 1, HALF, 128)
                for a in range(2)
            ]
            lanes_ref[k, pl.ds(b, ROWS // 2, stride=2), :] = jnp.concatenate(pair, axis=1).reshape(ROWS // 2, 128)
    for k in range(C // 128):
        dst_ref[:, k * 128 : (k + 1) * 128] = lanes_ref[k]


def mid_fwd_kernel(
    h_ref, ws0_ref, wl0_ref, code_ref, wl1_ref, ws1_ref,
    e_ref, d_ref, s_ref, q_ref, y_ref, s2_ref, g_ref, commit_ref, dcom_ref, resid_ref, u_ref, lanes_ref,
):
    to_depth(h_ref, lanes_ref, e_ref)
    d = nt(e_ref[...], ws0_ref[...])
    d_ref[...] = d
    s = (d * sigmoid(d)).astype(BF16)
    s_ref[...] = s
    z = nt(s, wl0_ref[...])
    q = jnp.zeros((LAT, ZD), F32)
    commit = jnp.zeros((LAT, ZD), F32)
    dcom = jnp.zeros((LAT, ZD), F32)
    for k in range(4):
        resid_ref[k * LAT : (k + 1) * LAT, :] = (z - q).astype(BF16)
        q = q + code_ref[k * LAT : (k + 1) * LAT, :].astype(F32)
        diff = z - q
        commit = commit + diff * diff
        dcom = dcom + diff
    commit_ref[...] = jnp.sum(commit, axis=0, keepdims=True)
    dcom_ref[...] = dcom
    quant = (z + (q - z)).astype(BF16)
    q_ref[...] = quant
    y = nn(quant, wl1_ref[...])
    y_ref[...] = y
    s2 = (y * sigmoid(y)).astype(BF16)
    s2_ref[...] = s2
    u_ref[...] = nn(s2, ws1_ref[...])
    from_depth(u_ref, lanes_ref, g_ref)


def mid_fwd(h, ws0, wl0, codes, wl1, ws1):
    shape = jax.ShapeDtypeStruct
    return pl.pallas_call(
        mid_fwd_kernel,
        out_shape=(
            shape((LAT, 4 * C), BF16),
            shape((LAT, C), F32),
            shape((LAT, C), BF16),
            shape((LAT, ZD), BF16),
            shape((LAT, C), F32),
            shape((LAT, C), BF16),
            shape((ROWS, C), F32),
            shape((1, ZD), F32),
            shape((LAT, ZD), F32),
            shape((4 * LAT, ZD), BF16),
        ),
        in_specs=[VM] * 6,
        out_specs=(VM,) * 10,
        scratch_shapes=[pltpu.VMEM((LAT, 4 * C), F32), pltpu.VMEM((C // 128, ROWS, 128), F32)],
        compiler_params=PARAMS,
        cost_estimate=cost(4 << 30, 12 << 20),
        name="mid_fwd",
    )(h, ws0, wl0, codes, wl1, ws1)


def mid_bwd_kernel(
    split, scale, info_ref, dg_ref, e_ref, d_ref, s_ref, q_ref, y_ref, s2_ref, dcom_ref, ws0_ref, wl0_ref, wl1_ref,
    ws1_ref, *rest,
):
    if split:
        keep_ref, send_ref, dh_ref, *wholes, du_ref, de_ref, lanes_ref, sems = rest
    else:
        *wholes, dh_ref, du_ref, de_ref, lanes_ref = rest
    dws0_ref, dws1_ref, dwl0_ref, dwl1_ref = wholes
    to_depth(dg_ref, lanes_ref, du_ref)
    out = dws0_ref.dtype
    ds2 = nt(du_ref[...], ws1_ref[...])
    dy = (ds2 * silu_slope(y_ref[...])).astype(BF16)
    dws1_ref[...] = nn(transposed(s2_ref[...]), du_ref[...]).astype(out)
    dwl1_ref[...] = nn(transposed(q_ref[...]), dy).astype(out)
    dz = (nt(dy, wl1_ref[...]) + scale * dcom_ref[...]).astype(BF16)
    dwl0_ref[...] = nn(transposed(dz), s_ref[...]).astype(out)
    ds = nn(dz, wl0_ref[...])
    dd = (ds * silu_slope(d_ref[...])).astype(BF16)
    dws0_ref[...] = nn(transposed(dd), e_ref[...]).astype(out)
    copies = []
    if split:
        copies = block_copies(MIX, info_ref, (keep_ref, send_ref), wholes, sems, False)
    for copy in copies:
        copy.start()
    de_ref[...] = nn(dd, ws0_ref[...])
    from_depth(de_ref, lanes_ref, dh_ref)
    for copy in copies:
        copy.wait()


def mid_bwd(info, scale, dg, e, d, s, q, y, s2, dcom, ws0, wl0, wl1, ws1, z_size):
    shape = jax.ShapeDtypeStruct
    wholes = [(C, 4 * C), (C, 4 * C), (ZD, C), (ZD, C)]
    scratch = [
        pltpu.VMEM((LAT, 4 * C), BF16),
        pltpu.VMEM((LAT, 4 * C), F32),
        pltpu.VMEM((C // 128, ROWS, 128), F32),
    ]
    field = shape((ROWS, C), F32)
    if z_size:
        block = shape((4 * z_size, SHARD, 1152), BF16)
        shapes, specs = (block, block, field), (ANY, ANY, VM)
        scratch = [pltpu.VMEM(one, BF16) for one in wholes] + scratch
        scratch += [pltpu.SemaphoreType.DMA((copy_count(MIX, z_size),))]
    else:
        shapes, specs = tuple(shape(one, F32) for one in wholes) + (field,), (VM,) * 5
    out = pl.pallas_call(
        functools.partial(mid_bwd_kernel, z_size, scale),
        out_shape=shapes,
        in_specs=[SMEM] + [VM] * 12,
        out_specs=specs,
        scratch_shapes=scratch,
        compiler_params=PARAMS,
        cost_estimate=cost(4 << 30, 12 << 20),
        name="mid_bwd",
    )(info, dg, e, d, s, q, y, s2, dcom, ws0, wl0, wl1, ws1)
    return out[-1], out[:-1]


def head_kernel(total_ref, g_ref, wp_ref, pix_ref, mask_ref, dw_ref, dg_ref, loss_ref, o_ref, dr_ref):
    inv = total_ref[0]
    loss = jnp.zeros((1, pix_ref.shape[1]), F32)
    for i in range(4):
        rows = pl.ds(i * 256, 256)
        g = g_ref[rows, :]
        gate = sigmoid(g)
        o = (g * gate).astype(BF16)
        o_ref[rows, :] = o
        err = nn(o, wp_ref[...]) - pix_ref[rows, :].astype(F32)
        keep = mask_ref[rows, :].astype(F32)
        smooth = jnp.sqrt(err * err + 1.0)
        loss = loss + jnp.sum(keep * (smooth - 1.0), axis=0, keepdims=True)
        dr = (keep * err / smooth / inv).astype(BF16)
        dr_ref[rows, :] = dr
        do = nt(dr, wp_ref[...])
        dg_ref[rows, :] = do * (gate * (1.0 + g * (1.0 - gate)))
    loss_ref[...] = loss
    dw_ref[...] = nn(transposed(o_ref[...]), dr_ref[...]).astype(dw_ref.dtype)


def head(total, g, wp, pix, mask, grad_type=BF16):
    shape = jax.ShapeDtypeStruct
    width = pix.shape[1]
    return pl.pallas_call(
        head_kernel,
        out_shape=(shape((C, width), grad_type), shape((ROWS, C), F32), shape((1, width), F32)),
        in_specs=[SMEM, VM, VM, VM, VM],
        out_specs=(VM,) * 3,
        scratch_shapes=[pltpu.VMEM((ROWS, C), BF16), pltpu.VMEM((ROWS, width), BF16)],
        compiler_params=PARAMS,
        cost_estimate=cost(6 << 30, 12 << 20),
        name="head",
    )(total, g, wp, pix, mask)


BOTH = ("z", "core", "fsdp")
COLS = ("z", "core")


def swap(shard):
    return jnp.swapaxes(shard, -1, -2).astype(BF16)


def across(x, near):
    n = lax.axis_size("fsdp")
    masks = (2, 1) if near else (1, 2)
    return lax.ppermute(x, ("core", "fsdp"), [(c * n + f, c * n + (f ^ masks[c])) for c in range(2) for f in range(n)])


def partner(x):
    return lax.ppermute(x, "core", [(0, 1), (1, 0)])


def everyone(x):
    n = lax.axis_size("z") * lax.axis_size("core") * lax.axis_size("fsdp")
    return lax.all_to_all(jnp.broadcast_to(x[None], (n,) + x.shape), BOTH, 0, 0, tiled=True)


def along_z(x, step):
    n = lax.axis_size("z")
    return lax.ppermute(x, "z", [(i, i ^ step) for i in range(n)])


def shuffle(x, axis):
    return lax.all_to_all(x, axis, 0, 0, tiled=True)


def assemble_kernel(parts, info_ref, own, other, *rest):
    copies = block_copies(parts, info_ref, (own, other), rest[:-1], rest[-1], True)
    for copy in copies:
        copy.start()
    for copy in copies:
        copy.wait()


def assemble(info, pieces, parts):
    z_size = pieces[0].shape[0] // 4
    shapes = [s for kind, _, lanes in parts for s in part_shapes(kind, lanes, z_size, BF16)]
    return pl.pallas_call(
        functools.partial(assemble_kernel, parts),
        out_shape=tuple(jax.ShapeDtypeStruct(*s) for s in shapes),
        in_specs=[SMEM] + [ANY] * 2,
        out_specs=(VM,) * len(shapes),
        scratch_shapes=[pltpu.SemaphoreType.DMA((copy_count(parts, z_size),))],
        compiler_params=PARAMS,
        cost_estimate=cost(1 << 30, 10 << 20),
        name="assemble",
    )(info, *pieces)


def gather_all(shards, others):
    z_size = lax.axis_size("z")
    count = len(shards)
    shards = list(shards)
    z_done, near_done, far_done, pieces, side = {}, {}, {}, {}, {}
    for step in range(max([count + 2] + list(others)) + 1):
        new = {}
        if step < count:
            new["z"] = shuffle(jnp.broadcast_to(shards[step][None], (z_size,) + shards[step].shape), "z")
        if 0 <= step - 1 < count:
            new["near"] = across(z_done[step - 1], True)
        if 0 <= step - 2 < count:
            new["far"] = across(near_done[step - 2], False)
        if 0 <= step - 3 < count:
            new["core"] = partner(far_done[step - 3])
        if step in others:
            side = {**side, **others[step](pieces, side)}
        new, shards[step + 1 :], side = lax.optimization_barrier((new, shards[step + 1 :], side))
        if "z" in new:
            z_done[step] = new["z"]
        if "near" in new:
            near_done[step - 1] = jnp.concatenate([z_done[step - 1], new["near"]])
        if "far" in new:
            far_done[step - 2] = jnp.concatenate([near_done[step - 2], new["far"]])
        if "core" in new:
            pieces[step - 3] = (far_done[step - 3], new["core"])
    return pieces, side


def add_up(parts):
    total = parts[0].astype(F32)
    for part in parts[1:]:
        total = total + part.astype(F32)
    return total


def scatter_stages(keep, send, out):
    half = keep.shape[0] // 2
    keep, got = yield keep, partner(send)
    parts = [keep, got]
    for near in (False, True):
        *parts, got = yield *parts, across(add_up([p[half : 2 * half] for p in parts]).astype(BF16), near)
        parts.append(got)
        half = half // 2
    away = [along_z(add_up([p[k] for p in parts]).astype(BF16), k) for k in range(1, 2 * half)]
    *both, = yield *parts, *away
    out.append(add_up([p[0] for p in both[: len(parts)]] + both[len(parts) :]))


def scatter_direct(blocks, out):
    got = yield shuffle(blocks, BOTH)
    out.append(jnp.sum(got.astype(F32), axis=0))


class Overlap:
    def __init__(self):
        self.live = []

    def add(self, stages, *args, late=0):
        out = []
        stages = stages(*args, out)
        self.live.append((stages, next(stages), late))
        return out

    def step(self, values):
        due = [value for _, value, late in self.live if not late]
        values, due = lax.optimization_barrier((values, due))
        live, at = [], 0
        for stages, value, late in self.live:
            if late:
                live.append((stages, value, late - 1))
                continue
            try:
                live.append((stages, stages.send(due[at]), 0))
            except StopIteration:
                pass
            at += 1
        self.live = live
        return values


def fetch_whole(shard):
    cols = lax.all_gather(shard.astype(BF16), COLS, axis=1, tiled=True)
    return jnp.swapaxes(lax.all_gather(cols, "fsdp", axis=0, tiled=True), 0, 1)


def reduce_whole(grad):
    rows = lax.psum_scatter(jnp.swapaxes(grad, 0, 1), "fsdp", scatter_dimension=0, tiled=True)
    return jnp.swapaxes(lax.psum_scatter(rows, COLS, scatter_dimension=1, tiled=True), 0, 1)


def widen(block, width):
    return jnp.pad(block, ((0, 0),) * (block.ndim - 1) + ((0, width - block.shape[-1]),))


def pix_matrix(blocks, width):
    return blocks[:, :, :width].transpose(1, 0, 2).reshape(C, 4 * width)


def pix_blocks(matrix, shard):
    rows, cols = shard
    return matrix.reshape(-1, cols, matrix.shape[1] // rows, rows).transpose(0, 2, 1, 3).reshape(-1, cols, rows)


def adam_step(weight, moment, second, grad, rate):
    moment_new = 0.5 * moment + 0.5 * grad
    second_new = 0.5 * second + 0.5 * grad * grad
    fix = 1.0 - 0.5**STEP
    weight_new = weight - rate * (
        moment_new / fix / (jnp.sqrt(second_new / fix) + 1e-12) + 0.01 * weight
    )
    return (weight_new, moment_new, second_new)


def exact(left, right, dims):
    return lax.dot_general(left, right, (dims, ((), ())), preferred_element_type=F32)


def code_slots(codes, devices, capacity, rows):
    n = codes.shape[0]
    owner = codes // rows
    hot = (owner[:, None] == jnp.arange(devices, dtype=jnp.int32)[None, :]).astype(BF16)
    at = jnp.arange(n, dtype=jnp.int32)
    before = (at[None, :] < at[:, None]).astype(BF16)
    rank = exact(before, hot, ((1,), (0,)))
    place = jnp.sum(rank * hot.astype(F32), axis=1).astype(jnp.int32)
    slot = owner * capacity + place
    return (jnp.arange(devices * capacity, dtype=jnp.int32)[:, None] == slot[None, :]).astype(BF16)


def on_device(
    pixels,
    valid_mask,
    size_groups,
    code_index,
    w_pixel,
    w_res,
    w_scale,
    w_latent,
    norm_gains,
    moment_pixel,
    moment_res,
    moment_scale,
    moment_latent,
    moment_gains,
    second_pixel,
    second_res,
    second_scale,
    second_latent,
    second_gains,
    ema_counts,
    ema_sums,
):
    n_inner = lax.axis_size("fsdp")
    z_size = lax.axis_size("z")
    devices = 2 * z_size * n_inner
    latent_all = code_index.shape[1] * devices
    rows = ema_sums.shape[0]
    paired = n_inner == 4 and w_res.shape[1] == 1152 and w_res.shape[2] == SHARD
    blocks = z_size if paired else 0
    place = [lax.axis_index("core"), lax.axis_index("fsdp"), lax.axis_index("z")]
    info = jnp.stack([size_groups[0]] + [one.astype(jnp.int32) for one in place])

    codes = code_index.reshape(-1)
    capacity = max(2, 2 * codes.shape[0] // devices)
    pick = code_slots(codes, devices, capacity, rows)
    local = codes % rows
    cols = jnp.stack([local // 16, local % 16, jnp.ones_like(local)], axis=1).astype(BF16)
    want = exact(pick, cols, ((1,), (0,)))
    wanted = jnp.where(want[:, 2] > 0.5, want[:, 0] * 16.0 + want[:, 1], -1.0).astype(jnp.int32)
    book = (ema_sums / ema_counts[:, None]).astype(BF16)
    valid = jnp.sum(valid_mask.astype(F32).reshape(-1, 128), axis=0, keepdims=True)

    def row_hot(asked):
        return (asked[:, None] == jnp.arange(rows, dtype=jnp.int32)[None, :]).astype(BF16)

    def ask(pieces, side):
        wide = -(-capacity // 128) * 128
        request = widen(wanted.astype(F32).reshape(devices, 1, capacity), wide)
        count = jnp.broadcast_to(widen(valid, wide)[None], (devices, 1, wide))
        got = shuffle(jnp.concatenate([request, count], axis=1), BOTH)
        return {"asked": got[:, 0, :capacity].reshape(-1).astype(jnp.int32), "count": jnp.sum(got[:, 1])}

    def reply(pieces, side):
        answer = exact(row_hot(side["asked"]), book, ((1,), (0,))).astype(BF16)
        return {"replies": shuffle(answer.reshape(devices, capacity, ZD), BOTH)}

    gains = [jnp.stack([norm_gains[j], norm_gains[4 + j]]) for j in range(4)]
    width = w_pixel.shape[1]

    def run_conv0(pieces, side):
        if paired:
            (pix,) = assemble(info, pieces[0], (("pix", RES[0][2], 256),))
            h0 = nt(pixels, pix_matrix(pix, width))
            weight = pieces[0]
        else:
            h0 = nt(pixels, fetch_whole(w_pixel[0]))
            weight = (fetch_whole(w_res[0]),)
        t1, a1 = conv_fwd(info, h0, gains[0], weight)
        return {"h0": h0, "t1": t1, "a1": a1, "res0": weight}

    def run_conv1(pieces, side):
        weight = pieces[1] if paired else (fetch_whole(w_res[1]),)
        h1, a2 = conv_fwd(info, side["t1"], gains[1], weight, side["h0"])
        return {"h1": h1, "a2": a2, "res1": weight, **reply(pieces, side)}

    def run_mid(pieces, side):
        if paired:
            mats = assemble(info, pieces[2], MIX)
        else:
            mats = [fetch_whole(w_scale[i]) for i in range(2)] + [fetch_whole(w_latent[i]) for i in range(2)]
        scale0, scale1, lat0, lat1 = mats
        picked = exact(pick, side["replies"].reshape(-1, ZD), ((0,), (0,))).astype(BF16)
        return {"mid": mid_fwd(side["h1"], scale0, lat0, picked, lat1, scale1), "mats": mats}

    def run_conv2(pieces, side):
        weight = pieces[3] if paired else (fetch_whole(w_res[2]),)
        t3, a3 = conv_fwd(info, side["mid"][6], gains[2], weight)
        return {"t3": t3, "a3": a3, "res2": weight}

    def run_conv3(pieces, side):
        sent = exact(pick, side["mid"][9], ((1,), (0,))).astype(BF16)
        held = shuffle(sent.reshape(devices, capacity, ZD), BOTH)
        if paired:
            (pix,) = assemble(info, pieces[4], (("pix", RES[0][2], 256),))
            pix = pix_matrix(pix, width)
            weight = pieces[4]
        else:
            pix, weight = fetch_whole(w_pixel[1]), (fetch_whole(w_res[3]),)
        g1, a4 = conv_fwd(info, side["t3"], gains[3], weight, side["mid"][6])
        out = BF16 if paired else F32
        d_head, dg1, loss = head(side["count"].reshape(1), g1, pix, pixels, valid_mask, out)
        return {"held": held, "a4": a4, "res3": weight, "d_head": d_head, "dg1": dg1, "loss": loss}

    others = {2: ask, 4: run_conv0, 5: run_conv1, 6: run_mid, 7: run_conv2, 8: run_conv3}
    shards = []
    if paired:
        res_t, pix_t, scale_t, lat_t = swap(w_res), swap(w_pixel), swap(w_scale), swap(w_latent)
        mix = jnp.concatenate([scale_t[0], scale_t[1], lat_t.reshape(-1, lat_t.shape[2])], axis=1)
        first, last = [jnp.concatenate([res_t[3 * i], widen(pix_t[i], 256)], axis=1) for i in range(2)]
        shards = [first, res_t[1], mix, res_t[2], last]
    _, side = gather_all(shards, others)
    total_valid = side["count"]
    e, d, s, quant, y, s2, g0, commit, dcom, _ = side["mid"]
    h0, t1, a1, h1, a2, t3, a3, a4 = [side[name] for name in ("h0", "t1", "a1", "h1", "a2", "t3", "a3", "a4")]
    res_w = [side["res0"], side["res1"], side["res2"], side["res3"]]
    scale0, scale1, lat0, lat1 = side["mats"]
    d_head, dg1, loss = side["d_head"], side["dg1"], side["loss"]

    hot_rows = row_hot(side["asked"])
    held = side["held"].reshape(-1, ZD)
    my_sums = exact(hot_rows, held, ((0,), (0,)))
    my_counts = jnp.sum(hot_rows.astype(F32), axis=0)
    counts_new = EMA_DECAY * ema_counts + (1.0 - EMA_DECAY) * my_counts
    sums_new = EMA_DECAY * ema_sums + (1.0 - EMA_DECAY) * my_sums
    book_new = sums_new / counts_new[:, None]

    scale = 2.0 * COMMIT_WEIGHT / (latent_all * ZD)
    if paired:
        overlap = Overlap()
        shard = w_pixel.shape[1:]
        sum_head = overlap.add(scatter_direct, pix_blocks(d_head, shard), late=1)
        dw, dg1 = overlap.step((conv_dw(info, dg1, a4, z_size), dg1))
        sum_res3 = overlap.add(scatter_stages, *dw)
        dt3, dn3 = overlap.step(conv_dx(info, dg1, t3, gains[3], res_w[3]))
        dw, dt3 = overlap.step((conv_dw(info, dt3, a3, z_size), dt3))
        sum_res2 = overlap.add(scatter_stages, *dw)
        dg0, dn2 = overlap.step(conv_dx(info, dt3, g0, gains[2], res_w[2], dg1, False))
        dh1, dw = overlap.step(
            mid_bwd(info, scale, dg0, e, d, s, quant, y, s2, dcom, scale0, lat0, lat1, scale1, z_size)
        )
        sum_mix = overlap.add(scatter_stages, *dw)
        dw, dh1 = overlap.step((conv_dw(info, dh1, a2, z_size), dh1))
        sum_res1 = overlap.add(scatter_stages, *dw)
        dt1, dn1 = overlap.step(conv_dx(info, dh1, t1, gains[1], res_w[1]))
        dw, dt1 = overlap.step((conv_dw(info, dt1, a1, z_size), dt1))
        sum_res0 = overlap.add(scatter_stages, *dw)
        dh0, dn0 = overlap.step(conv_dx(info, dt1, h0, gains[0], res_w[0], dh1))
        d_patch = exact(dh0, pixels, ((0,), (0,))).astype(BF16)
        d_patch = overlap.step(pix_blocks(d_patch, shard))
        sum_patch = overlap.add(scatter_direct, d_patch)
        overlap.step(())
        overlap.step(())
        grad_pixel = jnp.stack([sum_patch[0], sum_head[0]])
        grad_res = jnp.stack([sum_res0[0], sum_res1[0], sum_res2[0], sum_res3[0]])
        grad_scale = jnp.stack([sum_mix[0][:, :512], sum_mix[0][:, 512:1024]])
        grad_latent = sum_mix[0][:, 1024:].reshape(2, SHARD // 2, -1)
    else:
        d_res3 = conv_dw(info, dg1, a4, 0)
        dt3, dn3 = conv_dx(info, dg1, t3, gains[3], res_w[3])
        d_res2 = conv_dw(info, dt3, a3, 0)
        dg0, dn2 = conv_dx(info, dt3, g0, gains[2], res_w[2], dg1, False)
        dh1, (d_scale0, d_scale1, d_lat0, d_lat1) = mid_bwd(
            info, scale, dg0, e, d, s, quant, y, s2, dcom, scale0, lat0, lat1, scale1, 0
        )
        d_res1 = conv_dw(info, dh1, a2, 0)
        dt1, dn1 = conv_dx(info, dh1, t1, gains[1], res_w[1])
        d_res0 = conv_dw(info, dt1, a1, 0)
        dh0, dn0 = conv_dx(info, dt1, h0, gains[0], res_w[0], dh1)
        d_patch = exact(dh0, pixels, ((0,), (0,)))
        grad_pixel = jnp.stack([reduce_whole(g) for g in (d_patch, d_head)])
        grad_res = jnp.stack([reduce_whole(g) for g in (d_res0, d_res1, d_res2, d_res3)])
        grad_scale = jnp.stack([reduce_whole(g) for g in (d_scale0, d_scale1)])
        grad_latent = jnp.stack([reduce_whole(g) for g in (d_lat0, d_lat1)])

    gain_local = jnp.stack([dn0[0], dn1[0], dn2[0], dn3[0], dn0[1], dn1[1], dn2[1], dn3[1]])
    sums_local = jnp.concatenate(
        [
            gain_local.reshape(-1, 128),
            jnp.sum(loss.reshape(-1, 128), axis=0, keepdims=True),
            jnp.sum(commit.reshape(-1, 128), axis=0, keepdims=True),
        ]
    )
    sums_all = jnp.sum(everyone(sums_local), axis=0)
    grad_gains = sums_all[:-2].reshape(8, C)
    smooth_sum = jnp.sum(sums_all[-2])
    commit_sum = jnp.sum(sums_all[-1])

    squares = jnp.sum(grad_pixel * grad_pixel) + jnp.sum(grad_res * grad_res)
    squares = squares + jnp.sum(grad_scale * grad_scale) + jnp.sum(grad_latent * grad_latent)
    total_squares = jnp.sum(everyone(jnp.broadcast_to(squares, (1, 128)))[:, 0, 0]) + jnp.sum(grad_gains * grad_gains)
    norm = jnp.sqrt(total_squares)
    factor = CLIP_AT / jnp.maximum(norm, CLIP_AT)
    groups_all = [
        (w_pixel, moment_pixel, second_pixel, grad_pixel),
        (w_res, moment_res, second_res, grad_res),
        (w_scale, moment_scale, second_scale, grad_scale),
        (w_latent, moment_latent, second_latent, grad_latent),
    ]
    outputs = [jnp.stack([smooth_sum, total_valid, commit_sum]), norm.reshape(1)]
    for weight, moment, second, grad in groups_all:
        grad = jnp.swapaxes(grad * factor, 1, 2)
        weight_new, moment_new, second_new = adam_step(weight, moment, second, grad, WEIGHT_RATE)
        outputs += [weight_new, moment_new, second_new, weight_new.astype(BF16)]
    outputs += list(adam_step(norm_gains, moment_gains, second_gains, grad_gains * factor, GAIN_RATE))
    outputs += [counts_new, sums_new, book_new, book_new.astype(BF16)]
    return tuple(outputs)


def solution(mesh):
    outer, inner = mesh.shape["dp"], mesh.shape["fsdp"]
    fine = Mesh(mesh.devices.reshape(outer // 2, 2, inner), BOTH)
    placed = (
        P(BOTH, None),
        P(BOTH, None),
        P(BOTH),
        P(None, BOTH),
        P(None, "fsdp", COLS),
        P(None, "fsdp", COLS),
        P(None, "fsdp", COLS),
        P(None, "fsdp", COLS),
        P(),
        P(None, "fsdp", COLS),
        P(None, "fsdp", COLS),
        P(None, "fsdp", COLS),
        P(None, "fsdp", COLS),
        P(),
        P(None, "fsdp", COLS),
        P(None, "fsdp", COLS),
        P(None, "fsdp", COLS),
        P(None, "fsdp", COLS),
        P(),
        P(BOTH),
        P(BOTH, None),
    )
    return jax.shard_map(
        on_device,
        mesh=fine,
        in_specs=placed,
        out_specs=(
            P(),
            P(),
            P(None, "fsdp", COLS),
            P(None, "fsdp", COLS),
            P(None, "fsdp", COLS),
            P(None, "fsdp", COLS),
            P(None, "fsdp", COLS),
            P(None, "fsdp", COLS),
            P(None, "fsdp", COLS),
            P(None, "fsdp", COLS),
            P(None, "fsdp", COLS),
            P(None, "fsdp", COLS),
            P(None, "fsdp", COLS),
            P(None, "fsdp", COLS),
            P(None, "fsdp", COLS),
            P(None, "fsdp", COLS),
            P(None, "fsdp", COLS),
            P(None, "fsdp", COLS),
            P(),
            P(),
            P(),
            P(BOTH),
            P(BOTH, None),
            P(BOTH, None),
            P(BOTH, None),
        ),
        check_vma=False,
    )
```

time: 2210 us -> 587 us (0.27)
  Pallas kernels: 1730 us -> 194 us
  waiting for transfers between devices: 234 us -> 138 us
  other arithmetic: 41.4 us -> 70 us
  starting transfers between devices: 125 us -> 98.1 us
    pallas_call x19 -> x16, Pallas kernels: 1710 us -> 178 us  [the longest x4 64.1 us: conv_dx(): pl.pallas_call(functools.partial(conv_dx_kernel, len(weight), res is not...]
    ppermute x95 -> x45, waiting for transfers between devices: 225 us -> 87.7 us  [the longest x20 66 us: across(): lax.ppermute(x, ('core', 'fsdp'), [(c * n + f, c * n + (f ^ masks[c])) fo...]
    ppermute x95 -> x45, starting transfers between devices: 99.8 us -> 50.1 us  [the longest x20 25.2 us: across(): lax.ppermute(x, ('core', 'fsdp'), [(c * n + f, c * n + (f ^ masks[c])) fo...]
    all_to_all x3 -> x9, waiting for transfers between devices: 6.65 us -> 45.8 us  [shuffle(): return lax.all_to_all(x, axis, 0, 0, tiled=True)]
    all_to_all x3 -> x9, starting transfers between devices: 12.5 us -> 41.3 us  [shuffle(): return lax.all_to_all(x, axis, 0, 0, tiled=True)]
  transfers between devices with their start and end apart: 101 -> 56, of which waited for: 47 -> 19; matrix products, arithmetic and copies ran while one was open for 4% -> 15% of each run, Pallas kernels for 56% -> 32%
where the time goes in v2:
time: 587 us; the launch traced here: 580 us
  Pallas kernels  194 us (33%)
  waiting for transfers between devices  138 us (24%)
  starting transfers between devices  98.1 us (17%)
  other arithmetic  70 us (12%)
  local copies, waits for them, and re-layouts  43.1 us (7%)
  matrix products  18.6 us (3%)
  blocking collectives  9.94 us (2%)
  between operations  8.1 us (1%)
    ppermute x20, waiting for transfers between devices, across(): lax.ppermute(x, ('core', 'fsdp'), [(c * n + f, c * n + (f ^ masks[c])) fo...  66 us
    pallas_call x4, Pallas kernels, conv_dx(): pl.pallas_call(functools.partial(conv_dx_kernel, len(weight), res is not...  64.1 us
    pallas_call x4, Pallas kernels, conv_fwd(): pl.pallas_call(functools.partial(conv_fwd_kernel, len(weight), res is not...  48.9 us
    all_to_all x9, waiting for transfers between devices, shuffle(): return lax.all_to_all(x, axis, 0, 0, tiled=True)  45.8 us
    all_to_all x9, starting transfers between devices, shuffle(): return lax.all_to_all(x, axis, 0, 0, tiled=True)  41.3 us
    pallas_call x4, Pallas kernels, conv_dw(): pl.pallas_call(functools.partial(conv_dw_kernel, z_size), out_shape=shape...  40.3 us
    ppermute x20, starting transfers between devices, across(): lax.ppermute(x, ('core', 'fsdp'), [(c * n + f, c * n + (f ^ masks[c])) fo...  25.2 us
    ppermute x15, starting transfers between devices, along_z(): return lax.ppermute(x, 'z', [(i, i ^ step) for i in range(n)])  22.2 us
  transfers between devices with their start and end apart: 56, of which 19 were waited for; matrix products, arithmetic and copies ran while one was open for 15% of the time, Pallas kernels for 32%

profile of v2, /device:TPU:0, one launch (start us, length us, event | category | flops | bytes accessed | tf_op | source)
XLA Modules:
  0.0 579.6 jit_solution(11002661895137320912)
XLA Ops:
  11.2 17.9 %all-to-all-done = bf16[4,64,1408]{2,1,0:T(8,128)(2,1)S(1)} async-done(((bf16[4,64,1408]{2,1,0:T(8,128)(2,1)}), bf16[4,64,1408]{2,1,0:T(8,128)(2,1)S(1)}, u32[]{:S(2)}, u32[]{:S(2)}) %all-to-all-start) | async-done | bytes 720928 | tf_op jit(solution)/shard_map/all_to_all | solution.py:604
  35.8 9.1 %collective-permute-done = bf16[4,64,1408]{2,1,0:T(8,128)(2,1)S(1)} collective-permute-done((bf16[4,64,1408]{2,1,0:T(8,128)(2,1)S(1)}, bf16[4,64,1408]{2,1,0:T(8,128)(2,1)S(1)}, u32[]{:S(2)}, u32[]{:S(2)}) %collective-permute-start) | collective-permute-done | bytes 720928 | tf_op jit(solution)/shard_map/ppermute | solution.py:586
  60.7 9.9 %all_to_all.60 = f32[32,2,128]{2,1,0:T(2,128)S(1)} all-to-all(f32[32,2,128]{2,1,0:T(2,128)S(1)} %fusion.59), channel_id=1, replica_groups=mesh['z'=4,'core'=2,'fsdp'=4] {'z','core','fsdp'}, dimensions={0} | all-to-all | bytes 65536 | tf_op jit(solution)/shard_map/all_to_all | solution.py:604
  78.2 6.8 %collective-permute-done.2 = bf16[4,64,1152]{2,1,0:T(8,128)(2,1)S(1)} collective-permute-done((bf16[4,64,1152]{2,1,0:T(8,128)(2,1)S(1)}, bf16[4,64,1152]{2,1,0:T(8,128)(2,1)S(1)}, u32[]{:S(2)}, u32[]{:S(2)}) %collective-permute-start.2) | collective-permute-done | bytes 589856 | tf_op jit(solution)/shard_map/ppermute | solution.py:586
  105.8 11.7 %collective-permute-done.5 = bf16[4,64,1152]{2,1,0:T(8,128)(2,1)S(1)} collective-permute-done((bf16[4,64,1152]{2,1,0:T(8,128)(2,1)S(1)}, bf16[4,64,1152]{2,1,0:T(8,128)(2,1)S(1)}, u32[]{:S(2)}, u32[]{:S(2)}) %collective-permute-start.5) | collective-permute-done | bytes 589856 | tf_op jit(solution)/shard_map/ppermute | solution.py:586
  139.7 11.7 %conv_fwd.4 = (f32[1024,512]{1,0:T(8,128)}, bf16[1088,1536]{1,0:T(8,128)(2,1)}) custom-call(s32[4]{0:T(128)} %pad_add_fusion.info_ref, f32[1024,512]{1,0:T(8,128)} %convolution_bitcast_fusion.x_ref.rest_2_, f32[2,512]{1,0:T(2,128)} %get-tuple-element.670.gain_ref, bf16[16,64,1408]{2,1,0:T(8,128)(2,1)} %constant_dynamic-update-slice_fusion.own.rest_0_, ...), custom_call_target="tpu_custom_call" | custom-call | flops 9663676416 | bytes 12582912 | tf_op jit(solution)/shard_map/conv_fwd/pallas_call | solution.py:224
  168.5 12.6 %conv_fwd.5 = (f32[1024,512]{1,0:T(8,128)}, bf16[1088,1536]{1,0:T(8,128)(2,1)}) custom-call(s32[4]{0:T(128)} %pad_add_fusion.info_ref, f32[1024,512]{1,0:T(8,128)} %get-tuple-element.505.x_ref, f32[2,512]{1,0:T(2,128)} %get-tuple-element.671.gain_ref, bf16[16,64,1152]{2,1,0:T(8,128)(2,1)} %constant_dynamic-update-slice_fusion.3.rest_0_, ...), custom_call_target="tpu_custom_call" | custom-call | flops 9663676416 | bytes 12582912 | tf_op jit(solution)/shard_map/conv_fwd/pallas_call | solution.py:224
  181.1 10.4 %collective-permute-done.11 = bf16[4,64,1408]{2,1,0:T(8,128)(2,1)S(1)} collective-permute-done((bf16[4,64,1408]{2,1,0:T(8,128)(2,1)S(1)}, bf16[4,64,1408]{2,1,0:T(8,128)(2,1)S(1)}, u32[]{:S(2)}, u32[]{:S(2)}) %collective-permute-start.11) | collective-permute-done | bytes 720928 | tf_op jit(solution)/shard_map/ppermute | solution.py:586
  222.6 12.2 %conv_fwd.6 = (f32[1024,512]{1,0:T(8,128)}, bf16[1088,1536]{1,0:T(8,128)(2,1)}) custom-call(s32[4]{0:T(128)} %pad_add_fusion.info_ref, f32[1024,512]{1,0:T(8,128)} %get-tuple-element.464.x_ref.rest_2_, f32[2,512]{1,0:T(2,128)} %get-tuple-element.672.gain_ref, bf16[16,64,1152]{2,1,0:T(8,128)(2,1)} %constant_dynamic-update-slice_fusion.9.rest_0_, ...), custom_call_target="tpu_custom_call" | custom-call | flops 9663676416 | bytes 12582912 | tf_op jit(solution)/shard_map/conv_fwd/pallas_call | solution.py:224
  247.9 12.4 %conv_fwd.7 = (f32[1024,512]{1,0:T(8,128)}, bf16[1088,1536]{1,0:T(8,128)(2,1)}) custom-call(s32[4]{0:T(128)} %pad_add_fusion.info_ref, f32[1024,512]{1,0:T(8,128)} %get-tuple-element.449.x_ref, f32[2,512]{1,0:T(2,128)} %get-tuple-element.673.gain_ref, bf16[16,64,1408]{2,1,0:T(8,128)(2,1)} %copy-done.6, ...), custom_call_target="tpu_custom_call" | custom-call | flops 9663676416 | bytes 12582912 | tf_op jit(solution)/shard_map/conv_fwd/pallas_call | solution.py:224
  260.3 9.4 %head.1 = (bf16[512,768]{1,0:T(8,128)(2,1)}, f32[1024,512]{1,0:T(8,128)}, f32[1,768]{1,0:T(1,128)}) custom-call(f32[1]{0:T(128)} %bitcast.22.total_ref, f32[1024,512]{1,0:T(8,128)} %get-tuple-element.419.g_ref, bf16[512,768]{1,0:T(8,128)(2,1)} %copy.72.wp_ref, bf16[1024,768]{1,0:T(8,128)(2,1)} %pix_ref.1, s32[1024,768]{1,0:T(8,128)} %mask_ref.1), custom_call_target="tpu_custom_call" | custom-call | flops 6442450944 | bytes 12582912 | tf_op jit(solution)/shard_map/head/pallas_call | solution.py:563
  269.7 10.6 %conv_dw.4 = (bf16[16,64,1152]{2,1,0:T(8,128)(2,1)}, bf16[16,64,1152]{2,1,0:T(8,128)(2,1)}) custom-call(s32[4]{0:T(128)} %pad_add_fusion.info_ref, f32[1024,512]{1,0:T(8,128)} %get-tuple-element.448.dt_ref.rest_2_, bf16[1088,1536]{1,0:T(8,128)(2,1)} %get-tuple-element.445.a3_ref), custom_call_target="tpu_custom_call" | custom-call | flops 9663676416 | bytes 12582912 | tf_op jit(solution)/shard_map/conv_dw/pallas_call | solution.py:274
  288.9 15.6 %conv_dx.4 = (bf16[1024,512]{1,0:T(8,128)(2,1)}, f32[2,512]{1,0:T(2,128)}) custom-call(s32[4]{0:T(128)} %pad_add_fusion.info_ref, f32[1024,512]{1,0:T(8,128)} %get-tuple-element.448.dt_ref.rest_2_, f32[1024,512]{1,0:T(8,128)} %get-tuple-element.449.x_ref, f32[2,512]{1,0:T(2,128)} %get-tuple-element.673.gain_ref, bf16[16,64,1408]{2,1,0:T(8,128)(2,1)} %copy-done.6, ...), custom_call_target="tpu_custom_call" | custom-call | flops 14495514624 | bytes 12582912 | tf_op jit(solution)/shard_map/conv_dx/pallas_call | solution.py:365
  304.5 10.8 %all-to-all-done.8 = bf16[32,64,192]{2,1,0:T(8,128)(2,1)S(1)} async-done(((bf16[32,64,192]{2,1,0:T(8,128)(2,1)}), bf16[32,64,192]{2,1,0:T(8,128)(2,1)S(1)}, u32[]{:S(2)}, u32[]{:S(2)}) %all-to-all-start.8) | async-done | bytes 786464 | tf_op jit(solution)/shard_map/all_to_all | solution.py:604
  319.8 9.8 %conv_dw.5 = (bf16[16,64,1152]{2,1,0:T(8,128)(2,1)}, bf16[16,64,1152]{2,1,0:T(8,128)(2,1)}) custom-call(s32[4]{0:T(128)} %pad_add_fusion.info_ref, bf16[1024,512]{1,0:T(8,128)(2,1)} %get-tuple-element.463.dt_ref, bf16[1088,1536]{1,0:T(8,128)(2,1)} %get-tuple-element.458.a3_ref), custom_call_target="tpu_custom_call" | custom-call | flops 9663676416 | bytes 12582912 | tf_op jit(solution)/shard_map/conv_dw/pallas_call | solution.py:274
  339.1 16.4 %conv_dx.5 = (f32[1024,512]{1,0:T(8,128)}, f32[2,512]{1,0:T(2,128)}) custom-call(s32[4]{0:T(128)} %pad_add_fusion.info_ref, bf16[1024,512]{1,0:T(8,128)(2,1)} %get-tuple-element.463.dt_ref, f32[1024,512]{1,0:T(8,128)} %get-tuple-element.464.x_ref.rest_2_, f32[2,512]{1,0:T(2,128)} %get-tuple-element.672.gain_ref, ...), custom_call_target="tpu_custom_call" | custom-call | flops 14495514624 | bytes 12582912 | tf_op jit(solution)/shard_map/conv_dx/pallas_call | solution.py:365
  368.6 11.5 %mid_bwd.1 = (bf16[16,64,1152]{2,1,0:T(8,128)(2,1)}, bf16[16,64,1152]{2,1,0:T(8,128)(2,1)}, f32[1024,512]{1,0:T(8,128)}) custom-call(s32[4]{0:T(128)} %pad_add_fusion.info_ref, f32[1024,512]{1,0:T(8,128)} %get-tuple-element.474.dg_ref, bf16[256,2048]{1,0:T(8,128)(2,1)} %get-tuple-element.475.e_ref, f32[256,512]{1,0:T(8,128)} %get-tuple-element.476.d_ref, ...), custom_call_target="tpu_custom_call" | custom-call | flops 4294967296 | bytes 12582912 | tf_op jit(solution)/shard_map/mid_bwd/pallas_call | solution.py:526
  384.5 10.1 %conv_dw.6 = (bf16[16,64,1152]{2,1,0:T(8,128)(2,1)}, bf16[16,64,1152]{2,1,0:T(8,128)(2,1)}) custom-call(s32[4]{0:T(128)} %pad_add_fusion.info_ref, f32[1024,512]{1,0:T(8,128)} %get-tuple-element.504.dt_ref.rest_2_, bf16[1088,1536]{1,0:T(8,128)(2,1)} %get-tuple-element.496.a3_ref), custom_call_target="tpu_custom_call" | custom-call | flops 9663676416 | bytes 12582912 | tf_op jit(solution)/shard_map/conv_dw/pallas_call | solution.py:274
  405.4 15.7 %conv_dx.6 = (bf16[1024,512]{1,0:T(8,128)(2,1)}, f32[2,512]{1,0:T(2,128)}) custom-call(s32[4]{0:T(128)} %pad_add_fusion.info_ref, f32[1024,512]{1,0:T(8,128)} %get-tuple-element.504.dt_ref.rest_2_, f32[1024,512]{1,0:T(8,128)} %get-tuple-element.505.x_ref, f32[2,512]{1,0:T(2,128)} %get-tuple-element.671.gain_ref, ...), custom_call_target="tpu_custom_call" | custom-call | flops 14495514624 | bytes 12582912 | tf_op jit(solution)/shard_map/conv_dx/pallas_call | solution.py:365
  427.6 9.7 %conv_dw.7 = (bf16[16,64,1152]{2,1,0:T(8,128)(2,1)}, bf16[16,64,1152]{2,1,0:T(8,128)(2,1)}) custom-call(s32[4]{0:T(128)} %pad_add_fusion.info_ref, bf16[1024,512]{1,0:T(8,128)(2,1)} %get-tuple-element.527.dt_ref, bf16[1088,1536]{1,0:T(8,128)(2,1)} %get-tuple-element.519.a3_ref), custom_call_target="tpu_custom_call" | custom-call | flops 9663676416 | bytes 12582912 | tf_op jit(solution)/shard_map/conv_dw/pallas_call | solution.py:274
  454.7 16.4 %conv_dx.7 = (bf16[1024,512]{1,0:T(8,128)(2,1)}, f32[2,512]{1,0:T(2,128)}) custom-call(s32[4]{0:T(128)} %pad_add_fusion.info_ref, bf16[1024,512]{1,0:T(8,128)(2,1)} %get-tuple-element.527.dt_ref, f32[1024,512]{1,0:T(8,128)} %convolution_bitcast_fusion.x_ref.rest_2_, f32[2,512]{1,0:T(2,128)} %get-tuple-element.670.gain_ref, ...), custom_call_target="tpu_custom_call" | custom-call | flops 14495514624 | bytes 12582912 | tf_op jit(solution)/shard_map/conv_dx/pallas_call | solution.py:365
  491.5 12.1 %collective-permute-done.38 = bf16[64,1152]{1,0:T(8,128)(2,1)} collective-permute-done((bf16[64,1152]{1,0:T(8,128)(2,1)}, bf16[64,1152]{1,0:T(8,128)(2,1)}, u32[]{:S(2)}, u32[]{:S(2)}) %collective-permute-start.38) | collective-permute-done | bytes 147488 | tf_op jit(solution)/shard_map/ppermute | solution.py:600
  516.5 12.2 %collective-permute-done.41 = bf16[4,64,1152]{2,1,0:T(8,128)(2,1)} collective-permute-done((bf16[4,64,1152]{2,1,0:T(8,128)(2,1)S(1)}, bf16[4,64,1152]{2,1,0:T(8,128)(2,1)}, u32[]{:S(2)}, u32[]{:S(2)}) %collective-permute-start.41) | collective-permute-done | bytes 589856 | tf_op jit(solution)/shard_map/ppermute | solution.py:586
  544.1 8.0 %collective-permute-done.43 = bf16[64,1152]{1,0:T(8,128)(2,1)S(1)} collective-permute-done((bf16[64,1152]{1,0:T(8,128)(2,1)S(1)}, bf16[64,1152]{1,0:T(8,128)(2,1)S(1)}, u32[]{:S(2)}, u32[]{:S(2)}) %collective-permute-start.43) | collective-permute-done | bytes 147488 | tf_op jit(solution)/shard_map/ppermute | solution.py:600
  (376 shorter events, 288.4 us)
Async XLA Ops:
  4.0 25.2 %all-to-all-start = ((bf16[4,64,1408]{2,1,0:T(8,128)(2,1)}), bf16[4,64,1408]{2,1,0:T(8,128)(2,1)S(1)}, u32[]{:S(2)}, u32[]{:S(2)}) async-start(bf16[4,64,1408]{2,1,0:T(8,128)(2,1)} %broadcast_in_dim.22), calls=%async_computation | async-start | bytes 1441792 | tf_op jit(solution)/shard_map/all_to_all | solution.py:604
  50.2 41.3 %collective-permute-start.1 = (bf16[8,64,1408]{2,1,0:T(8,128)(2,1)}, bf16[8,64,1408]{2,1,0:T(8,128)(2,1)}, u32[]{:S(2)}, u32[]{:S(2)}) collective-permute-start(bf16[8,64,1408]{2,1,0:T(8,128)(2,1)} %pad_maximum_fusion), channel_id=1, source_target_pairs={{0,1},{1,0},{2,3},{3,2},{4,6},{5,7},{6,4},{7,5},{8,9},{9,8},{10,11... | collective-permute-start | bytes 4325384 | tf_op jit(solution)/shard_map/ppermute | solution.py:586
  94.1 24.0 %collective-permute-start.3 = (bf16[16,64,1408]{2,1,0:T(8,128)(2,1)}, bf16[16,64,1408]{2,1,0:T(8,128)(2,1)}, u32[]{:S(2)}, u32[]{:S(2)}) collective-permute-start(bf16[16,64,1408]{2,1,0:T(8,128)(2,1)} %constant_dynamic-update-slice_fusion.own.rest_0_), channel_id=1, source_target_pairs={{0,4},{4,0},{1,5},{5,1},{2,6},{6,2},{3,7},{7,3},{8,12},{12,8},{9,1... | collective-permute-start | bytes 8650760 | tf_op jit(solution)/shard_map/ppermute | solution.py:590
  95.2 22.8 %collective-permute-start.4 = (bf16[8,64,1152]{2,1,0:T(8,128)(2,1)}, bf16[8,64,1152]{2,1,0:T(8,128)(2,1)}, u32[]{:S(2)}, u32[]{:S(2)}) collective-permute-start(bf16[8,64,1152]{2,1,0:T(8,128)(2,1)} %pad_maximum_fusion.2), channel_id=1, source_target_pairs={{0,1},{1,0},{2,3},{3,2},{4,6},{5,7},{6,4},{7,5},{8,9},{9,8},{10,11... | collective-permute-start | bytes 3538952 | tf_op jit(solution)/shard_map/ppermute | solution.py:586
  120.4 31.1 %collective-permute-start.6 = (bf16[16,64,1152]{2,1,0:T(8,128)(2,1)}, bf16[16,64,1152]{2,1,0:T(8,128)(2,1)}, u32[]{:S(2)}, u32[]{:S(2)}) collective-permute-start(bf16[16,64,1152]{2,1,0:T(8,128)(2,1)} %constant_dynamic-update-slice_fusion.3.rest_0_), channel_id=1, source_target_pairs={{0,4},{4,0},{1,5},{5,1},{2,6},{6,2},{3,7},{7,3},{8,12},{12,8},{9,1... | collective-permute-start | bytes 7077896 | tf_op jit(solution)/shard_map/ppermute | solution.py:590
  122.5 29.0 %collective-permute-start.7 = (bf16[8,64,1152]{2,1,0:T(8,128)(2,1)}, bf16[8,64,1152]{2,1,0:T(8,128)(2,1)}, u32[]{:S(2)}, u32[]{:S(2)}) collective-permute-start(bf16[8,64,1152]{2,1,0:T(8,128)(2,1)} %pad_maximum_fusion.3), channel_id=1, source_target_pairs={{0,1},{1,0},{2,3},{3,2},{4,6},{5,7},{6,4},{7,5},{8,9},{9,8},{10,11... | collective-permute-start | bytes 3538952 | tf_op jit(solution)/shard_map/ppermute | solution.py:586
  124.0 27.5 %collective-permute-start.8 = (bf16[4,64,1152]{2,1,0:T(8,128)(2,1)S(1)}, bf16[4,64,1152]{2,1,0:T(8,128)(2,1)S(1)}, u32[]{:S(2)}, u32[]{:S(2)}) collective-permute-start(bf16[4,64,1152]{2,1,0:T(8,128)(2,1)S(1)} %all-to-all-done.4), channel_id=1, source_target_pairs={{0,2},{1,3},{2,0},{3,1},{4,5},{5,4},{6,7},{7,6},{8,10},{9,11},{10,... | collective-permute-start | bytes 1769480 | tf_op jit(solution)/shard_map/ppermute | solution.py:586
  125.6 25.9 %all-to-all-start.5 = ((bf16[4,64,1408]{2,1,0:T(8,128)(2,1)}), bf16[4,64,1408]{2,1,0:T(8,128)(2,1)S(1)}, u32[]{:S(2)}, u32[]{:S(2)}) async-start(bf16[4,64,1408]{2,1,0:T(8,128)(2,1)} %broadcast_in_dim.28), calls=%async_computation.5 | async-start | bytes 1441792 | tf_op jit(solution)/shard_map/all_to_all | solution.py:604
  154.2 41.6 %collective-permute-start.9 = (bf16[16,64,1152]{2,1,0:T(8,128)(2,1)}, bf16[16,64,1152]{2,1,0:T(8,128)(2,1)}, u32[]{:S(2)}, u32[]{:S(2)}) collective-permute-start(bf16[16,64,1152]{2,1,0:T(8,128)(2,1)} %constant_dynamic-update-slice_fusion.6.own), channel_id=1, source_target_pairs={{0,4},{4,0},{1,5},{5,1},{2,6},{6,2},{3,7},{7,3},{8,12},{12,8},{9,1... | collective-permute-start | bytes 7077896 | tf_op jit(solution)/shard_map/ppermute | solution.py:590
  156.2 39.6 %all-to-all-start.6 = ((bf16[32,64,256]{2,1,0:T(8,128)(2,1)}), bf16[32,64,256]{2,1,0:T(8,128)(2,1)}, u32[]{:S(2)}, u32[]{:S(2)}) async-start(bf16[32,64,256]{2,1,0:T(8,128)(2,1)} %bitcast.20), calls=%async_computation.6 | async-start | bytes 2097152 | tf_op jit(solution)/shard_map/all_to_all | solution.py:604
  162.5 33.3 %collective-permute-start.10 = (bf16[8,64,1152]{2,1,0:T(8,128)(2,1)}, bf16[8,64,1152]{2,1,0:T(8,128)(2,1)}, u32[]{:S(2)}, u32[]{:S(2)}) collective-permute-start(bf16[8,64,1152]{2,1,0:T(8,128)(2,1)} %pad_maximum_fusion.4), channel_id=1, source_target_pairs={{0,1},{1,0},{2,3},{3,2},{4,6},{5,7},{6,4},{7,5},{8,9},{9,8},{10,11... | collective-permute-start | bytes 3538952 | tf_op jit(solution)/shard_map/ppermute | solution.py:586
  165.1 26.4 %collective-permute-start.11 = (bf16[4,64,1408]{2,1,0:T(8,128)(2,1)S(1)}, bf16[4,64,1408]{2,1,0:T(8,128)(2,1)S(1)}, u32[]{:S(2)}, u32[]{:S(2)}) collective-permute-start(bf16[4,64,1408]{2,1,0:T(8,128)(2,1)S(1)} %all-to-all-done.5), channel_id=1, source_target_pairs={{0,2},{1,3},{2,0},{3,1},{4,5},{5,4},{6,7},{7,6},{8,10},{9,11},{10,... | collective-permute-start | bytes 2162696 | tf_op jit(solution)/shard_map/ppermute | solution.py:586
  237.5 32.2 %all-to-all-start.7 = ((bf16[32,64,256]{2,1,0:T(8,128)(2,1)}), bf16[32,64,256]{2,1,0:T(8,128)(2,1)S(1)}, u32[]{:S(2)}, u32[]{:S(2)}) async-start(bf16[32,64,256]{2,1,0:T(8,128)(2,1)} %bitcast.25), calls=%async_computation.7 | async-start | bytes 2097152 | tf_op jit(solution)/shard_map/all_to_all | solution.py:604
  280.4 35.0 %collective-permute-start.15 = (bf16[16,64,1152]{2,1,0:T(8,128)(2,1)}, bf16[16,64,1152]{2,1,0:T(8,128)(2,1)}, u32[]{:S(2)}, u32[]{:S(2)}) collective-permute-start(bf16[16,64,1152]{2,1,0:T(8,128)(2,1)} %get-tuple-element.456), channel_id=1, source_target_pairs={{0,4},{4,0},{1,5},{5,1},{2,6},{6,2},{3,7},{7,3},{8,12},{12,8},{9,1... | collective-permute-start | bytes 7077896 | tf_op jit(solution)/shard_map/ppermute | solution.py:590
  283.2 32.2 %all-to-all-start.8 = ((bf16[32,64,192]{2,1,0:T(8,128)(2,1)}), bf16[32,64,192]{2,1,0:T(8,128)(2,1)S(1)}, u32[]{:S(2)}, u32[]{:S(2)}) async-start(bf16[32,64,192]{2,1,0:T(8,128)(2,1)} %bitcast.27), calls=%async_computation.8 | async-start | bytes 2097152 | tf_op jit(solution)/shard_map/all_to_all | solution.py:604
  358.3 21.9 %collective-permute-start.22 = (bf16[8,64,1152]{2,1,0:T(8,128)(2,1)}, bf16[8,64,1152]{2,1,0:T(8,128)(2,1)}, u32[]{:S(2)}, u32[]{:S(2)}) collective-permute-start(bf16[8,64,1152]{2,1,0:T(8,128)(2,1)} %add_convert_fusion.3), channel_id=1, source_target_pairs={{0,1},{1,0},{2,3},{3,2},{4,6},{5,7},{6,4},{7,5},{8,9},{9,8},{10,11... | collective-permute-start | bytes 3538952 | tf_op jit(solution)/shard_map/ppermute | solution.py:586
  396.1 25.1 %collective-permute-start.29 = (bf16[16,64,1152]{2,1,0:T(8,128)(2,1)}, bf16[16,64,1152]{2,1,0:T(8,128)(2,1)}, u32[]{:S(2)}, u32[]{:S(2)}) collective-permute-start(bf16[16,64,1152]{2,1,0:T(8,128)(2,1)} %get-tuple-element.517), channel_id=1, source_target_pairs={{0,4},{4,0},{1,5},{5,1},{2,6},{6,2},{3,7},{7,3},{8,12},{12,8},{9,1... | collective-permute-start | bytes 7077896 | tf_op jit(solution)/shard_map/ppermute | solution.py:590
  397.9 23.2 %collective-permute-start.25 = (bf16[64,1152]{1,0:T(8,128)(2,1)S(1)}, bf16[64,1152]{1,0:T(8,128)(2,1)S(1)}, u32[]{:S(2)}, u32[]{:S(2)}) collective-permute-start(bf16[64,1152]{1,0:T(8,128)(2,1)S(1)} %get-tuple-element.639), channel_id=1, source_target_pairs={{0,8},{8,0},{16,24},{24,16},{1,9},{9,1},{17,25},{25,17},{2,10},{10... | collective-permute-start | bytes 442376 | tf_op jit(solution)/shard_map/ppermute | solution.py:600
  444.6 26.6 %collective-permute-start.36 = (bf16[16,64,1152]{2,1,0:T(8,128)(2,1)}, bf16[16,64,1152]{2,1,0:T(8,128)(2,1)}, u32[]{:S(2)}, u32[]{:S(2)}) collective-permute-start(bf16[16,64,1152]{2,1,0:T(8,128)(2,1)} %get-tuple-element.541), channel_id=1, source_target_pairs={{0,4},{4,0},{1,5},{5,1},{2,6},{6,2},{3,7},{7,3},{8,12},{12,8},{9,1... | collective-permute-start | bytes 7077896 | tf_op jit(solution)/shard_map/ppermute | solution.py:590
  448.0 23.2 %collective-permute-start.32 = (bf16[64,1152]{1,0:T(8,128)(2,1)S(1)}, bf16[64,1152]{1,0:T(8,128)(2,1)S(1)}, u32[]{:S(2)}, u32[]{:S(2)}) collective-permute-start(bf16[64,1152]{1,0:T(8,128)(2,1)S(1)} %get-tuple-element.636), channel_id=1, source_target_pairs={{0,8},{8,0},{16,24},{24,16},{1,9},{9,1},{17,25},{25,17},{2,10},{10... | collective-permute-start | bytes 442376 | tf_op jit(solution)/shard_map/ppermute | solution.py:600
  448.6 22.6 %collective-permute-start.33 = (bf16[64,1152]{1,0:T(8,128)(2,1)S(1)}, bf16[64,1152]{1,0:T(8,128)(2,1)S(1)}, u32[]{:S(2)}, u32[]{:S(2)}) collective-permute-start(bf16[64,1152]{1,0:T(8,128)(2,1)S(1)} %get-tuple-element.635), channel_id=1, source_target_pairs={{0,16},{8,24},{16,0},{24,8},{1,17},{9,25},{17,1},{25,9},{2,18},{10... | collective-permute-start | bytes 442376 | tf_op jit(solution)/shard_map/ppermute | solution.py:600
  473.0 30.5 %all-to-all-start.9 = ((f32[32,34,128]{2,1,0:T(8,128)}), f32[32,34,128]{2,1,0:T(8,128)S(1)}, u32[]{:S(2)}, u32[]{:S(2)}) async-start(f32[32,34,128]{2,1,0:T(8,128)} %broadcast_in_dim.31), calls=%async_computation.9 | async-start | bytes 1310720 | tf_op jit(solution)/shard_map/all_to_all | solution.py:595
  478.6 24.9 %collective-permute-start.40 = (bf16[8,64,1152]{2,1,0:T(8,128)(2,1)}, bf16[8,64,1152]{2,1,0:T(8,128)(2,1)}, u32[]{:S(2)}, u32[]{:S(2)}) collective-permute-start(bf16[8,64,1152]{2,1,0:T(8,128)(2,1)} %add_convert_fusion), channel_id=1, source_target_pairs={{0,1},{1,0},{2,3},{3,2},{4,6},{5,7},{6,4},{7,5},{8,9},{9,8},{10,11... | collective-permute-start | bytes 3538952 | tf_op jit(solution)/shard_map/ppermute | solution.py:586
  503.6 31.9 %all-to-all-start.10 = ((bf16[32,64,192]{2,1,0:T(8,128)(2,1)}), bf16[32,64,192]{2,1,0:T(8,128)(2,1)S(1)}, u32[]{:S(2)}, u32[]{:S(2)}) async-start(bf16[32,64,192]{2,1,0:T(8,128)(2,1)} %bitcast.44), calls=%async_computation.10 | async-start | bytes 2097152 | tf_op jit(solution)/shard_map/all_to_all | solution.py:604
  (103 other events, 1316.9 us)

commit v3 on v2

--- a/solution.py
+++ b/solution.py
@@ -26,7 +26,7 @@
 
 
 def sigmoid(v):
-    return 1.0 / (1.0 + jnp.exp(-v))
+    return 0.5 * jnp.tanh(0.5 * v) + 0.5
 
 
 def nt(left, right):
@@ -144,7 +144,7 @@
 
 
 def block_copies(parts, info_ref, pieces, wholes, sems, inward):
-    core, f, my_z = info_ref[1], info_ref[2], info_ref[3]
+    core, f = info_ref[1], info_ref[2]
     z_size = pieces[0].shape[0] // 4
     copies = []
     for side in range(2):
@@ -153,7 +153,7 @@
             for near in range(2):
                 for z in range(z_size):
                     at_f = f ^ ((2 - owner) * near) ^ ((1 + owner) * far)
-                    at_dp = 2 * (z if inward else my_z ^ z) + owner
+                    at_dp = 2 * z + owner
                     first = 0
                     for kind, lane, lanes in parts:
                         refs = wholes[first : first + part_count(kind)]
@@ -196,7 +196,7 @@
         store_shifts(a3_ref, y, v * sigmoid(v), side)
         return carry
 
-    lax.fori_loop(0, 32, body, 0, unroll=2)
+    lax.fori_loop(0, 32, body, 0, unroll=4)
     for copy in copies:
         copy.wait()
     out = nt(a3_ref[PAD : PAD + ROWS, :], wt_ref[:, 3 * C : 6 * C])
@@ -300,7 +300,7 @@
         store_shifts(d3_ref, y, val, side)
         return carry
 
-    lax.fori_loop(0, 32, body, 0, unroll=2)
+    lax.fori_loop(0, 32, body, 0, unroll=4)
     norm_stats(x_ref, group, mean_ref, rstd_ref)
     for copy in copies:
         copy.wait()
@@ -334,7 +334,7 @@
             return (one + ds, two + ds * xh)
 
         zero = jnp.zeros((32, C), F32)
-        one, two = lax.fori_loop(0, 8, step, (zero, zero))
+        one, two = lax.fori_loop(0, 8, step, (zero, zero), unroll=2)
         first.append(tile_rows(one))
         second.append(tile_rows(two))
     first = jnp.concatenate(first, axis=0)
@@ -357,7 +357,7 @@
             dx_ref[rows, :] = dx.astype(dx_ref.dtype)
             return carry
 
-        lax.fori_loop(0, 8, step, 0)
+        lax.fori_loop(0, 8, step, 0, unroll=2)
 
 
 def conv_dx(info, dt, x, gains, weight, res=None, low=True):
@@ -627,32 +627,51 @@
     )(info, *pieces)
 
 
-def gather_all(shards, others):
+def gather_all(shards, others, slow):
     z_size = lax.axis_size("z")
     count = len(shards)
     shards = list(shards)
-    z_done, near_done, far_done, pieces, side = {}, {}, {}, {}, {}
+    done = [{} for _ in shards]
+    pieces, side, waiting = {}, {}, {}
+    groups = [(1, 3), (3, count)] if count else []
+    bulks = {}
+    for first, last in groups:
+        bulks[first] = lax.all_gather(jnp.concatenate(shards[first:last], axis=1), "z")
     for step in range(max([count + 2] + list(others)) + 1):
         new = {}
-        if step < count:
-            new["z"] = shuffle(jnp.broadcast_to(shards[step][None], (z_size,) + shards[step].shape), "z")
+        if 0 <= step - 2 < count:
+            new["both", step - 2] = across(done[step - 2]["near"], False)
         if 0 <= step - 1 < count:
-            new["near"] = across(z_done[step - 1], True)
-        if 0 <= step - 2 < count:
-            new["far"] = across(near_done[step - 2], False)
+            new["far", step - 1] = across(done[step - 1]["z"], False)
+            new["near", step - 1] = across(done[step - 1]["z"], True)
+        if step < min(count, 1):
+            new["z", step] = shuffle(jnp.broadcast_to(shards[step][None], (z_size,) + shards[step].shape), "z")
+        for i, (first, last) in enumerate(groups):
+            if step == i + 1:
+                new["bulk", first] = bulks[first]
         if 0 <= step - 3 < count:
-            new["core"] = partner(far_done[step - 3])
+            own = jnp.concatenate([done[step - 3][name] for name in ("z", "near", "far", "both")])
+            new["own", step - 3] = own
+            new["core", step - 3] = partner(own)
+        if step in slow:
+            due, function = slow[step]
+            waiting[due] = function(pieces, side)
+        if step in waiting:
+            side = {**side, **waiting.pop(step)}
         if step in others:
             side = {**side, **others[step](pieces, side)}
-        new, shards[step + 1 :], side = lax.optimization_barrier((new, shards[step + 1 :], side))
-        if "z" in new:
-            z_done[step] = new["z"]
-        if "near" in new:
-            near_done[step - 1] = jnp.concatenate([z_done[step - 1], new["near"]])
-        if "far" in new:
-            far_done[step - 2] = jnp.concatenate([near_done[step - 2], new["far"]])
-        if "core" in new:
-            pieces[step - 3] = (far_done[step - 3], new["core"])
+        names = list(new)
+        values, shards[step + 1 :], side = lax.optimization_barrier((list(new.values()), shards[step + 1 :], side))
+        for (name, i), value in zip(names, values):
+            done[i][name] = value
+        for i, (first, last) in enumerate(groups):
+            if step == i + 1:
+                at = 0
+                for j in range(first, last):
+                    done[j]["z"] = done[first]["bulk"][:, :, at : at + shards[j].shape[1]]
+                    at += shards[j].shape[1]
+        if 0 <= step - 3 < count:
+            pieces[step - 3] = (done[step - 3]["own"], done[step - 3]["core"])
     return pieces, side
 
 
@@ -663,17 +682,38 @@
     return total
 
 
-def scatter_stages(keep, send, out):
+class Slow:
+    def __init__(self, value):
+        self.value = value
+
+
+def scatter_stages(keep, send, tie, bulk, out):
     half = keep.shape[0] // 2
     keep, got = yield keep, partner(send)
     parts = [keep, got]
     for near in (False, True):
-        *parts, got = yield *parts, across(add_up([p[half : 2 * half] for p in parts]).astype(BF16), near)
+        away = add_up([p[half : 2 * half] for p in parts]).astype(BF16)
+        if near and tie:
+            away, tie[0] = lax.optimization_barrier((away, tie[0]))
+        *parts, got = yield *parts, across(away, near)
         parts.append(got)
         half = half // 2
-    away = [along_z(add_up([p[k] for p in parts]).astype(BF16), k) for k in range(1, 2 * half)]
-    *both, = yield *parts, *away
-    out.append(add_up([p[0] for p in both[: len(parts)]] + both[len(parts) :]))
+    sums = add_up([p[: 2 * half] for p in parts]).astype(BF16)
+    if bulk:
+        got = yield Slow(lax.psum_scatter(sums, "z", scatter_dimension=0))
+        out.append(got.astype(F32))
+    else:
+        got = yield shuffle(sums, "z")
+        out.append(jnp.sum(got.astype(F32), axis=0))
+
+
+def scatter_pair(blocks, out):
+    got = yield shuffle(blocks, ("core", "fsdp"))
+    sums = jnp.sum(got.astype(F32), axis=0)
+    me = lax.axis_index("z")
+    away = [along_z(lax.dynamic_index_in_dim(sums, me ^ k, keepdims=False).astype(BF16), k) for k in range(1, sums.shape[0])]
+    away = yield away
+    out.append(add_up([lax.dynamic_index_in_dim(sums, me, keepdims=False)] + away))
 
 
 def scatter_direct(blocks, out):
@@ -691,16 +731,34 @@
         self.live.append((stages, next(stages), late))
         return out
 
-    def step(self, values):
+    def finish(self):
+        for stages, value, _ in self.live:
+            try:
+                while True:
+                    value = stages.send(value.value if isinstance(value, Slow) else value)
+            except StopIteration:
+                pass
+        self.live = []
+
+    def push(self, values):
+        stages, value, _ = self.live[-1]
+        values, value = lax.optimization_barrier((values, value))
+        self.live[-1] = (stages, stages.send(value), 0)
+        return values
+
+    def step(self, values, use=None):
         due = [value for _, value, late in self.live if not late]
         values, due = lax.optimization_barrier((values, due))
+        if use is not None:
+            use(values)
         live, at = [], 0
         for stages, value, late in self.live:
             if late:
                 live.append((stages, value, late - 1))
                 continue
             try:
-                live.append((stages, stages.send(due[at]), 0))
+                value = stages.send(due[at])
+                live.append((stages, value.value, 1) if isinstance(value, Slow) else (stages, value, 0))
             except StopIteration:
                 pass
             at += 1
@@ -739,6 +797,12 @@
         moment_new / fix / (jnp.sqrt(second_new / fix) + 1e-12) + 0.01 * weight
     )
     return (weight_new, moment_new, second_new)
+
+
+def small_blocks(values, devices):
+    flat = jnp.concatenate([value.reshape(-1) for value in values])
+    lanes = -(-flat.shape[0] // (128 * devices)) * 128
+    return jnp.pad(flat, (0, devices * lanes - flat.shape[0])).reshape(devices, 1, lanes)
 
 
 def exact(left, right, dims):
@@ -787,7 +851,7 @@
     rows = ema_sums.shape[0]
     paired = n_inner == 4 and w_res.shape[1] == 1152 and w_res.shape[2] == SHARD
     blocks = z_size if paired else 0
-    place = [lax.axis_index("core"), lax.axis_index("fsdp"), lax.axis_index("z")]
+    place = [lax.axis_index("core"), lax.axis_index("fsdp")]
     info = jnp.stack([size_groups[0]] + [one.astype(jnp.int32) for one in place])
 
     codes = code_index.reshape(-1)
@@ -803,11 +867,14 @@
     def row_hot(asked):
         return (asked[:, None] == jnp.arange(rows, dtype=jnp.int32)[None, :]).astype(BF16)
 
-    def ask(pieces, side):
+    def prepare(pieces, side):
         wide = -(-capacity // 128) * 128
         request = widen(wanted.astype(F32).reshape(devices, 1, capacity), wide)
         count = jnp.broadcast_to(widen(valid, wide)[None], (devices, 1, wide))
-        got = shuffle(jnp.concatenate([request, count], axis=1), BOTH)
+        return {"request": jnp.concatenate([request, count], axis=1)}
+
+    def ask(pieces, side):
+        got = shuffle(side["request"], BOTH)
         return {"asked": got[:, 0, :capacity].reshape(-1).astype(jnp.int32), "count": jnp.sum(got[:, 1])}
 
     def reply(pieces, side):
@@ -831,7 +898,7 @@
     def run_conv1(pieces, side):
         weight = pieces[1] if paired else (fetch_whole(w_res[1]),)
         h1, a2 = conv_fwd(info, side["t1"], gains[1], weight, side["h0"])
-        return {"h1": h1, "a2": a2, "res1": weight, **reply(pieces, side)}
+        return {"h1": h1, "a2": a2, "res1": weight}
 
     def run_mid(pieces, side):
         if paired:
@@ -861,14 +928,16 @@
         d_head, dg1, loss = head(side["count"].reshape(1), g1, pix, pixels, valid_mask, out)
         return {"held": held, "a4": a4, "res3": weight, "d_head": d_head, "dg1": dg1, "loss": loss}
 
-    others = {2: ask, 4: run_conv0, 5: run_conv1, 6: run_mid, 7: run_conv2, 8: run_conv3}
+    others = {0: prepare, 2: ask, 4: run_conv0, 5: run_conv1, 6: run_mid, 7: run_conv2, 8: run_conv3}
     shards = []
     if paired:
-        res_t, pix_t, scale_t, lat_t = swap(w_res), swap(w_pixel), swap(w_scale), swap(w_latent)
-        mix = jnp.concatenate([scale_t[0], scale_t[1], lat_t.reshape(-1, lat_t.shape[2])], axis=1)
-        first, last = [jnp.concatenate([res_t[3 * i], widen(pix_t[i], 256)], axis=1) for i in range(2)]
-        shards = [first, res_t[1], mix, res_t[2], last]
-    _, side = gather_all(shards, others)
+        first = jnp.concatenate([swap(w_res[0]), widen(swap(w_pixel[0]), 256)], axis=1)
+        first, res, pix, scale, latent = lax.optimization_barrier((first, w_res, w_pixel, w_scale, w_latent))
+        scale, latent = swap(scale), swap(latent)
+        mix = jnp.concatenate([scale[0], scale[1], latent.reshape(-1, latent.shape[2])], axis=1)
+        last = jnp.concatenate([swap(res[3]), widen(swap(pix[1]), 256)], axis=1)
+        shards = [first, swap(res[1]), mix, swap(res[2]), last]
+    _, side = gather_all(shards, others, {3: (4, reply)})
     total_valid = side["count"]
     e, d, s, quant, y, s2, g0, commit, dcom, _ = side["mid"]
     h0, t1, a1, h1, a2, t3, a3, a4 = [side[name] for name in ("h0", "t1", "a1", "h1", "a2", "t3", "a3", "a4")]
@@ -885,31 +954,36 @@
     book_new = sums_new / counts_new[:, None]
 
     scale = 2.0 * COMMIT_WEIGHT / (latent_all * ZD)
+    loss_rows = jnp.stack([jnp.sum(one.reshape(-1, 128), axis=0) for one in (loss, commit)])
     if paired:
         overlap = Overlap()
         shard = w_pixel.shape[1:]
-        sum_head = overlap.add(scatter_direct, pix_blocks(d_head, shard), late=1)
+        sum_head = overlap.add(scatter_direct, pix_blocks(d_head, shard), late=2)
         dw, dg1 = overlap.step((conv_dw(info, dg1, a4, z_size), dg1))
-        sum_res3 = overlap.add(scatter_stages, *dw)
+        sum_res3 = overlap.add(scatter_stages, *dw, (), True)
         dt3, dn3 = overlap.step(conv_dx(info, dg1, t3, gains[3], res_w[3]))
         dw, dt3 = overlap.step((conv_dw(info, dt3, a3, z_size), dt3))
-        sum_res2 = overlap.add(scatter_stages, *dw)
+        sum_res2 = overlap.add(scatter_stages, *dw, (), True)
         dg0, dn2 = overlap.step(conv_dx(info, dt3, g0, gains[2], res_w[2], dg1, False))
         dh1, dw = overlap.step(
             mid_bwd(info, scale, dg0, e, d, s, quant, y, s2, dcom, scale0, lat0, lat1, scale1, z_size)
         )
-        sum_mix = overlap.add(scatter_stages, *dw)
+        sum_mix = overlap.add(scatter_stages, *dw, (), True)
         dw, dh1 = overlap.step((conv_dw(info, dh1, a2, z_size), dh1))
-        sum_res1 = overlap.add(scatter_stages, *dw)
+        sum_res1 = overlap.add(scatter_stages, *dw, (), True)
+        dh1 = overlap.push(dh1)
         dt1, dn1 = overlap.step(conv_dx(info, dh1, t1, gains[1], res_w[1]))
         dw, dt1 = overlap.step((conv_dw(info, dt1, a1, z_size), dt1))
-        sum_res0 = overlap.add(scatter_stages, *dw)
-        dh0, dn0 = overlap.step(conv_dx(info, dt1, h0, gains[0], res_w[0], dh1))
-        d_patch = exact(dh0, pixels, ((0,), (0,))).astype(BF16)
-        d_patch = overlap.step(pix_blocks(d_patch, shard))
-        sum_patch = overlap.add(scatter_direct, d_patch)
-        overlap.step(())
-        overlap.step(())
+        tie = []
+        sum_res0 = overlap.add(scatter_stages, *dw, tie, True)
+        dt1 = overlap.push(dt1)
+        _, dn0 = overlap.step(conv_dx(info, dt1, h0, gains[0], res_w[0], dh1), lambda got: tie.append(got[0]))
+        d_patch = exact(tie[0], pixels, ((0,), (0,))).astype(BF16)
+        d_patch = pix_blocks(d_patch, shard).reshape(z_size, 2 * n_inner, *shard[::-1])
+        sum_patch = overlap.add(scatter_pair, d_patch.transpose(1, 0, 2, 3))
+        small = overlap.add(scatter_direct, small_blocks([dn0, dn1, dn2, dn3, loss_rows], devices))
+        overlap.finish()
+        small = small[0]
         grad_pixel = jnp.stack([sum_patch[0], sum_head[0]])
         grad_res = jnp.stack([sum_res0[0], sum_res1[0], sum_res2[0], sum_res3[0]])
         grad_scale = jnp.stack([sum_mix[0][:, :512], sum_mix[0][:, 512:1024]])
@@ -931,23 +1005,20 @@
         grad_res = jnp.stack([reduce_whole(g) for g in (d_res0, d_res1, d_res2, d_res3)])
         grad_scale = jnp.stack([reduce_whole(g) for g in (d_scale0, d_scale1)])
         grad_latent = jnp.stack([reduce_whole(g) for g in (d_lat0, d_lat1)])
-
-    gain_local = jnp.stack([dn0[0], dn1[0], dn2[0], dn3[0], dn0[1], dn1[1], dn2[1], dn3[1]])
-    sums_local = jnp.concatenate(
-        [
-            gain_local.reshape(-1, 128),
-            jnp.sum(loss.reshape(-1, 128), axis=0, keepdims=True),
-            jnp.sum(commit.reshape(-1, 128), axis=0, keepdims=True),
-        ]
-    )
-    sums_all = jnp.sum(everyone(sums_local), axis=0)
-    grad_gains = sums_all[:-2].reshape(8, C)
-    smooth_sum = jnp.sum(sums_all[-2])
-    commit_sum = jnp.sum(sums_all[-1])
+        small = shuffle(small_blocks([dn0, dn1, dn2, dn3, loss_rows], devices), BOTH)
+        small = jnp.sum(small, axis=0)
 
     squares = jnp.sum(grad_pixel * grad_pixel) + jnp.sum(grad_res * grad_res)
     squares = squares + jnp.sum(grad_scale * grad_scale) + jnp.sum(grad_latent * grad_latent)
-    total_squares = jnp.sum(everyone(jnp.broadcast_to(squares, (1, 128)))[:, 0, 0]) + jnp.sum(grad_gains * grad_gains)
+    shared = everyone(jnp.concatenate([small, jnp.full((1, small.shape[1]), squares, F32)]))
+    total_squares = jnp.sum(shared[:, -1, 0])
+    sizes = [2 * C] * 4 + [2 * 128]
+    every = shared[:, :-1].reshape(-1)[: sum(sizes)]
+    dn0, dn1, dn2, dn3, losses = jnp.split(every, [2 * C, 4 * C, 6 * C, 8 * C])
+    dn0, dn1, dn2, dn3 = [one.reshape(2, C) for one in (dn0, dn1, dn2, dn3)]
+    grad_gains = jnp.stack([dn0[0], dn1[0], dn2[0], dn3[0], dn0[1], dn1[1], dn2[1], dn3[1]])
+    smooth_sum, commit_sum = jnp.sum(losses[:128]), jnp.sum(losses[128:])
+    total_squares = total_squares + jnp.sum(grad_gains * grad_gains)
     norm = jnp.sqrt(total_squares)
     factor = CLIP_AT / jnp.maximum(norm, CLIP_AT)
     groups_all = [

time: 587 us -> 545 us (0.928)
  starting transfers between devices: 98.1 us -> 71.2 us
  waiting for transfers between devices: 138 us -> 122 us
  between operations: 8.1 us -> 21.3 us
  local copies, waits for them, and re-layouts: 43.1 us -> 31.8 us
  blocking collectives: 9.94 us -> 0 us
  other arithmetic: 70 us -> 77.5 us
    ppermute x15 -> x3, waiting for transfers between devices: 21.7 us -> 1.31 us  [along_z(): return lax.ppermute(x, 'z', [(i, i ^ step) for i in range(n)])]
    convert_element_type x11 -> x17, other arithmetic: 20.2 us -> 38 us  [the longest x10 23.7 us: scatter_stages(): away = add_up([p[half:2 * half] for p in parts]).astype(BF16)]
    ppermute x15 -> x3, starting transfers between devices: 22.2 us -> 4.45 us  [along_z(): return lax.ppermute(x, 'z', [(i, i ^ step) for i in range(n)])]
    all_gather x0 -> x2, waiting for transfers between devices: none -> 11.9 us  [gather_all(): lax.all_gather(jnp.concatenate(shards[first:last], axis=1), 'z')]
    all_to_all x9 -> x7, starting transfers between devices: 41.3 us -> 30.6 us  [shuffle(): return lax.all_to_all(x, axis, 0, 0, tiled=True)]
    ppermute x20 -> x25, waiting for transfers between devices: 66 us -> 55.5 us  [across(): lax.ppermute(x, ('core', 'fsdp'), [(c * n + f, c * n + (f ^ masks[c])) fo...]
    add x6 -> x0, other arithmetic: 10.5 us -> none  [add_up(): total = total + part.astype(F32)]
    concatenate x5 -> x2, local copies, waits for them, and re-layouts: 11.7 us -> 1.2 us  [the longest x1 1.2 us: gather_all(): jnp.concatenate([done[step - 3][name] for name in ('z', 'near', 'far', 'b...]
  transfers between devices with their start and end apart: 56 -> 53, of which waited for: 19 -> 21; matrix products, arithmetic and copies ran while one was open for 15% -> 18% of each run, Pallas kernels for 32% -> 34%
where the time goes in v3:
time: 545 us; the launch traced here: 537 us
  Pallas kernels  191 us (35%)
  waiting for transfers between devices  122 us (22%)
  other arithmetic  77.5 us (14%)
  starting transfers between devices  71.2 us (13%)
  local copies, waits for them, and re-layouts  31.8 us (6%)
  matrix products  22.8 us (4%)
  between operations  21.3 us (4%)
    pallas_call x4, Pallas kernels, conv_dx(): pl.pallas_call(functools.partial(conv_dx_kernel, len(weight), res is not...  61.3 us
    ppermute x25, waiting for transfers between devices, across(): lax.ppermute(x, ('core', 'fsdp'), [(c * n + f, c * n + (f ^ masks[c])) fo...  55.5 us
    pallas_call x4, Pallas kernels, conv_fwd(): pl.pallas_call(functools.partial(conv_fwd_kernel, len(weight), res is not...  48.6 us
    all_to_all x7, waiting for transfers between devices, shuffle(): return lax.all_to_all(x, axis, 0, 0, tiled=True)  40.8 us
    pallas_call x4, Pallas kernels, conv_dw(): pl.pallas_call(functools.partial(conv_dw_kernel, z_size), out_shape=shape...  40.5 us
    all_to_all x7, starting transfers between devices, shuffle(): return lax.all_to_all(x, axis, 0, 0, tiled=True)  30.6 us
    ppermute x25, starting transfers between devices, across(): lax.ppermute(x, ('core', 'fsdp'), [(c * n + f, c * n + (f ^ masks[c])) fo...  30.3 us
    convert_element_type x10, other arithmetic, scatter_stages(): away = add_up([p[half:2 * half] for p in parts]).astype(BF16)  23.7 us
  transfers between devices with their start and end apart: 53, of which 21 were waited for; matrix products, arithmetic and copies ran while one was open for 18% of the time, Pallas kernels for 34%

profile of v3, /device:TPU:0, one launch (start us, length us, event | category | flops | bytes accessed | tf_op | source)
XLA Modules:
  0.0 537.3 jit_solution(1973989102639442929)
XLA Ops:
  10.1 6.4 %all-to-all-start = ((bf16[4,64,1408]{2,1,0:T(8,128)(2,1)}), bf16[4,64,1408]{2,1,0:T(8,128)(2,1)}, u32[]{:S(2)}, u32[]{:S(2)}) async-start(bf16[4,64,1408]{2,1,0:T(8,128)(2,1)} %broadcast_in_dim.10), calls=%async_computation | async-start | bytes 1441792 | tf_op jit(solution)/shard_map/all_to_all | solution.py:604
  27.0 17.6 %all-to-all-done = bf16[4,64,1408]{2,1,0:T(8,128)(2,1)} async-done(((bf16[4,64,1408]{2,1,0:T(8,128)(2,1)}), bf16[4,64,1408]{2,1,0:T(8,128)(2,1)}, u32[]{:S(2)}, u32[]{:S(2)}) %all-to-all-start) | async-done | bytes 720928 | tf_op jit(solution)/shard_map/all_to_all | solution.py:604
  69.8 11.8 %all-to-all-done.1 = f32[32,2,128]{2,1,0:T(2,128)S(1)} async-done(((f32[32,2,128]{2,1,0:T(2,128)}), f32[32,2,128]{2,1,0:T(2,128)S(1)}, u32[]{:S(2)}, u32[]{:S(2)}) %all-to-all-start.1) | async-done | bytes 32800 | tf_op jit(solution)/shard_map/all_to_all | solution.py:604
  82.4 6.9 %all-gather.7.cloned.1.call-done = bf16[256,2560]{1,0:T(8,128)(2,1)} async-done(((bf16[64,2560]{1,0:T(8,128)(2,1)}), bf16[256,2560]{1,0:T(8,128)(2,1)}) %all-gather.7.cloned.1.call-update) | async-done | bytes 1310736 | tf_op jit(solution)/shard_map/all_gather | solution.py:639
  94.2 12.1 %collective-permute-done.6 = bf16[4,64,1152]{2,1,0:T(8,128)(2,1)S(1)} collective-permute-done((bf16[4,64,1152]{2,1,0:T(8,128)(2,1)S(1)}, bf16[4,64,1152]{2,1,0:T(8,128)(2,1)S(1)}, u32[]{:S(2)}, u32[]{:S(2)}) %collective-permute-start.6) | collective-permute-done | bytes 589856 | tf_op jit(solution)/shard_map/ppermute | solution.py:586
  140.1 11.6 %conv_fwd.4 = (f32[1024,512]{1,0:T(8,128)}, bf16[1088,1536]{1,0:T(8,128)(2,1)}) custom-call(s32[3]{0:T(128)} %pad_add_fusion.info_ref, f32[1024,512]{1,0:T(8,128)} %convolution_bitcast_fusion.x_ref.rest_2_, f32[2,512]{1,0:T(2,128)} %get-tuple-element.599.gain_ref, bf16[16,64,1408]{2,1,0:T(8,128)(2,1)} %copy-done.4, ...), custom_call_target="tpu_custom_call" | custom-call | flops 9663676416 | bytes 12582912 | tf_op jit(solution)/shard_map/conv_fwd/pallas_call | solution.py:224
  162.5 12.5 %conv_fwd.5 = (f32[1024,512]{1,0:T(8,128)}, bf16[1088,1536]{1,0:T(8,128)(2,1)}) custom-call(s32[3]{0:T(128)} %pad_add_fusion.info_ref, f32[1024,512]{1,0:T(8,128)} %get-tuple-element.485.x_ref, f32[2,512]{1,0:T(2,128)} %get-tuple-element.600.gain_ref, bf16[16,64,1152]{2,1,0:T(8,128)(2,1)} %pad_maximum_fusion.1.rest_0_, ...), custom_call_target="tpu_custom_call" | custom-call | flops 9663676416 | bytes 12582912 | tf_op jit(solution)/shard_map/conv_fwd/pallas_call | solution.py:224
  187.7 6.5 %assemble.4 = (bf16[512,2048]{1,0:T(8,128)(2,1)}, bf16[512,2048]{1,0:T(8,128)(2,1)}, bf16[256,512]{1,0:T(8,128)(2,1)}, bf16[256,512]{1,0:T(8,128)(2,1)}) custom-call(s32[3]{0:T(128)} %pad_add_fusion.info_ref, bf16[16,64,1152]{2,1,0:T(8,128)(2,1)} %copy-done.1, bf16[16,64,1152]{2,1,0:T(8,128)(2,1)} %collective-permute-done.16.other), custom_call_target="tpu_custom_call" | custom-call | flops 1073741824 | bytes 10485760 | tf_op jit(solution)/shard_map/assemble/pallas_call | solution.py:618
  198.1 6.8 %mid_fwd.1 = (bf16[256,2048]{1,0:T(8,128)(2,1)}, f32[256,512]{1,0:T(8,128)}, bf16[256,512]{1,0:T(8,128)(2,1)}, bf16[256,256]{1,0:T(8,128)(2,1)}, f32[256,512]{1,...) custom-call(f32[1024,512]{1,0:T(8,128)} %get-tuple-element.334.h_ref, ...), custom_call_target="tpu_custom_call" | custom-call | flops 4294967296 | bytes 12582912 | tf_op jit(solution)/shard_map/mid_fwd/pallas_call | solution.py:456
  207.8 12.1 %conv_fwd.6 = (f32[1024,512]{1,0:T(8,128)}, bf16[1088,1536]{1,0:T(8,128)(2,1)}) custom-call(s32[3]{0:T(128)} %pad_add_fusion.info_ref, f32[1024,512]{1,0:T(8,128)} %get-tuple-element.441.x_ref.rest_2_, f32[2,512]{1,0:T(2,128)} %get-tuple-element.601.gain_ref, bf16[16,64,1152]{2,1,0:T(8,128)(2,1)} %copy-done.9, ...), custom_call_target="tpu_custom_call" | custom-call | flops 9663676416 | bytes 12582912 | tf_op jit(solution)/shard_map/conv_fwd/pallas_call | solution.py:224
  233.3 12.4 %conv_fwd.7 = (f32[1024,512]{1,0:T(8,128)}, bf16[1088,1536]{1,0:T(8,128)(2,1)}) custom-call(s32[3]{0:T(128)} %pad_add_fusion.info_ref, f32[1024,512]{1,0:T(8,128)} %get-tuple-element.426.x_ref, f32[2,512]{1,0:T(2,128)} %get-tuple-element.602.gain_ref, bf16[16,64,1408]{2,1,0:T(8,128)(2,1)} %copy-done, ...), custom_call_target="tpu_custom_call" | custom-call | flops 9663676416 | bytes 12582912 | tf_op jit(solution)/shard_map/conv_fwd/pallas_call | solution.py:224
  245.7 9.3 %head.1 = (bf16[512,768]{1,0:T(8,128)(2,1)}, f32[1024,512]{1,0:T(8,128)}, f32[1,768]{1,0:T(1,128)}) custom-call(f32[1]{0:T(128)} %bitcast.29.total_ref, f32[1024,512]{1,0:T(8,128)} %get-tuple-element.396.g_ref, bf16[512,768]{1,0:T(8,128)(2,1)} %copy.74.wp_ref, bf16[1024,768]{1,0:T(8,128)(2,1)} %pix_ref.1, s32[1024,768]{1,0:T(8,128)} %mask_ref.1), custom_call_target="tpu_custom_call" | custom-call | flops 6442450944 | bytes 12582912 | tf_op jit(solution)/shard_map/head/pallas_call | solution.py:563
  255.0 10.5 %conv_dw.4 = (bf16[16,64,1152]{2,1,0:T(8,128)(2,1)}, bf16[16,64,1152]{2,1,0:T(8,128)(2,1)}) custom-call(s32[3]{0:T(128)} %pad_add_fusion.info_ref, f32[1024,512]{1,0:T(8,128)} %get-tuple-element.425.dt_ref.rest_2_, bf16[1088,1536]{1,0:T(8,128)(2,1)} %get-tuple-element.422.a3_ref), custom_call_target="tpu_custom_call" | custom-call | flops 9663676416 | bytes 12582912 | tf_op jit(solution)/shard_map/conv_dw/pallas_call | solution.py:274
  274.1 15.1 %conv_dx.4 = (bf16[1024,512]{1,0:T(8,128)(2,1)}, f32[2,512]{1,0:T(2,128)}) custom-call(s32[3]{0:T(128)} %pad_add_fusion.info_ref, f32[1024,512]{1,0:T(8,128)} %get-tuple-element.425.dt_ref.rest_2_, f32[1024,512]{1,0:T(8,128)} %get-tuple-element.426.x_ref, f32[2,512]{1,0:T(2,128)} %get-tuple-element.602.gain_ref, bf16[16,64,1408]{2,1,0:T(8,128)(2,1)} %copy-done, ...), custom_call_target="tpu_custom_call" | custom-call | flops 14495514624 | bytes 12582912 | tf_op jit(solution)/shard_map/conv_dx/pallas_call | solution.py:365
  293.5 10.0 %conv_dw.5 = (bf16[16,64,1152]{2,1,0:T(8,128)(2,1)}, bf16[16,64,1152]{2,1,0:T(8,128)(2,1)}) custom-call(s32[3]{0:T(128)} %pad_add_fusion.info_ref, bf16[1024,512]{1,0:T(8,128)(2,1)} %get-tuple-element.440.dt_ref, bf16[1088,1536]{1,0:T(8,128)(2,1)} %get-tuple-element.434.a3_ref), custom_call_target="tpu_custom_call" | custom-call | flops 9663676416 | bytes 12582912 | tf_op jit(solution)/shard_map/conv_dw/pallas_call | solution.py:274
  313.3 16.0 %conv_dx.5 = (f32[1024,512]{1,0:T(8,128)}, f32[2,512]{1,0:T(2,128)}) custom-call(s32[3]{0:T(128)} %pad_add_fusion.info_ref, bf16[1024,512]{1,0:T(8,128)(2,1)} %get-tuple-element.440.dt_ref, f32[1024,512]{1,0:T(8,128)} %get-tuple-element.441.x_ref.rest_2_, f32[2,512]{1,0:T(2,128)} %get-tuple-element.601.gain_ref, bf16[16,64,1152]{2,1,0:T(8,128)(2,1)} %copy-done.9, ...), custom_call_target="tpu_custom_call" | custom-call | flops 14495514624 | bytes 12582912 | tf_op jit(solution)/shard_map/conv_dx/pallas_call | solution.py:365
  333.4 11.4 %mid_bwd.1 = (bf16[16,64,1152]{2,1,0:T(8,128)(2,1)}, bf16[16,64,1152]{2,1,0:T(8,128)(2,1)}, f32[1024,512]{1,0:T(8,128)}) custom-call(s32[3]{0:T(128)} %pad_add_fusion.info_ref, f32[1024,512]{1,0:T(8,128)} %get-tuple-element.451.dg_ref, bf16[256,2048]{1,0:T(8,128)(2,1)} %get-tuple-element.452.e_ref, f32[256,512]{1,0:T(8,128)} %get-tuple-element.453.d_ref, ...), custom_call_target="tpu_custom_call" | custom-call | flops 4294967296 | bytes 12582912 | tf_op jit(solution)/shard_map/mid_bwd/pallas_call | solution.py:526
  354.1 10.3 %conv_dw.6 = (bf16[16,64,1152]{2,1,0:T(8,128)(2,1)}, bf16[16,64,1152]{2,1,0:T(8,128)(2,1)}) custom-call(s32[3]{0:T(128)} %pad_add_fusion.info_ref, f32[1024,512]{1,0:T(8,128)} %get-tuple-element.484.dt_ref.rest_2_, bf16[1088,1536]{1,0:T(8,128)(2,1)} %get-tuple-element.469.a3_ref), custom_call_target="tpu_custom_call" | custom-call | flops 9663676416 | bytes 12582912 | tf_op jit(solution)/shard_map/conv_dw/pallas_call | solution.py:274
  364.4 8.8 %reduce-scatter.6.cloned.1.call-done = bf16[1,64,1152]{2,1,0:T(8,128)(2,1)} async-done(((bf16[4,64,1152]{2,1,0:T(8,128)(2,1)}), bf16[1,64,1152]{2,1,0:T(8,128)(2,1)}) %reduce-scatter.6.cloned.1.call-update) | async-done | bytes 147472 | tf_op jit(solution)/shard_map/reduce_scatter | solution.py:703
  383.9 14.9 %conv_dx.6 = (bf16[1024,512]{1,0:T(8,128)(2,1)}, f32[2,512]{1,0:T(2,128)}) custom-call(s32[3]{0:T(128)} %pad_add_fusion.info_ref, f32[1024,512]{1,0:T(8,128)} %get-tuple-element.484.dt_ref.rest_2_, f32[1024,512]{1,0:T(8,128)} %get-tuple-element.485.x_ref, f32[2,512]{1,0:T(2,128)} %get-tuple-element.600.gain_ref, ...), custom_call_target="tpu_custom_call" | custom-call | flops 14495514624 | bytes 12582912 | tf_op jit(solution)/shard_map/conv_dx/pallas_call | solution.py:365
  398.8 6.1 %collective-permute-done.29 = bf16[8,64,1152]{2,1,0:T(8,128)(2,1)} collective-permute-done((bf16[8,64,1152]{2,1,0:T(8,128)(2,1)}, bf16[8,64,1152]{2,1,0:T(8,128)(2,1)}, u32[]{:S(2)}, u32[]{:S(2)}) %collective-permute-start.29) | collective-permute-done | bytes 1179680 | tf_op jit(solution)/shard_map/ppermute | solution.py:586
  411.6 9.7 %conv_dw.7 = (bf16[16,64,1152]{2,1,0:T(8,128)(2,1)}, bf16[16,64,1152]{2,1,0:T(8,128)(2,1)}) custom-call(s32[3]{0:T(128)} %pad_add_fusion.info_ref, bf16[1024,512]{1,0:T(8,128)(2,1)} %get-tuple-element.511.dt_ref, bf16[1088,1536]{1,0:T(8,128)(2,1)} %get-tuple-element.495.a3_ref), custom_call_target="tpu_custom_call" | custom-call | flops 9663676416 | bytes 12582912 | tf_op jit(solution)/shard_map/conv_dw/pallas_call | solution.py:274
  435.5 15.4 %conv_dx.7 = (bf16[1024,512]{1,0:T(8,128)(2,1)}, f32[2,512]{1,0:T(2,128)}) custom-call(s32[3]{0:T(128)} %pad_add_fusion.info_ref, bf16[1024,512]{1,0:T(8,128)(2,1)} %get-tuple-element.511.dt_ref, f32[1024,512]{1,0:T(8,128)} %convolution_bitcast_fusion.x_ref.rest_2_, f32[2,512]{1,0:T(2,128)} %get-tuple-element.599.gain_ref, bf16[16,64,1408]{2,1,0:T(8,128)(2,1)} %copy-done.4, ...), custom_call_target="tpu_custom_call" | custom-call | flops 14495514624 | bytes 12582912 | tf_op jit(solution)/shard_map/conv_dx/pallas_call | solution.py:365
  472.1 10.6 %all-to-all-done.6 = bf16[8,4,64,192]{3,2,1,0:T(8,128)(2,1)S(1)} async-done(((bf16[8,4,64,192]{3,2,1,0:T(8,128)(2,1)}), bf16[8,4,64,192]{3,2,1,0:T(8,128)(2,1)S(1)}, u32[]{:S(2)}, u32[]{:S(2)}) %all-to-all-start.6) | async-done | bytes 786464 | tf_op jit(solution)/shard_map/all_to_all | solution.py:604
  (338 shorter events, 251.3 us)
Async XLA Ops:
  10.1 34.6 %all-to-all-start = ((bf16[4,64,1408]{2,1,0:T(8,128)(2,1)}), bf16[4,64,1408]{2,1,0:T(8,128)(2,1)}, u32[]{:S(2)}, u32[]{:S(2)}) async-start(bf16[4,64,1408]{2,1,0:T(8,128)(2,1)} %broadcast_in_dim.10), calls=%async_computation | async-start | bytes 1441792 | tf_op jit(solution)/shard_map/all_to_all | solution.py:604
  16.5 38.0 %all-gather.5.cloned.1.call-start = ((), (), s32[]{:S(2)}) async-start(), calls=%async_computation.18 | async-start | bytes 1474560 | tf_op jit(solution)/shard_map/all_gather | solution.py:639
  17.5 71.8 %all-gather.7.cloned.1.call-start = ((), (), s32[]{:S(2)}) async-start(), calls=%async_computation.19 | async-start | bytes 1638400 | tf_op jit(solution)/shard_map/all_gather | solution.py:639
  61.0 28.4 %collective-permute-start.3 = (bf16[4,64,1152]{2,1,0:T(8,128)(2,1)}, bf16[4,64,1152]{2,1,0:T(8,128)(2,1)}, u32[]{:S(2)}, u32[]{:S(2)}) collective-permute-start(bf16[4,64,1152]{2,1,0:T(8,128)(2,1)} %get-tuple-element.571), channel_id=1, source_target_pairs={{0,1},{1,0},{2,3},{3,2},{4,6},{5,7},{6,4},{7,5},{8,9},{9,8},{10,11... | collective-permute-start | bytes 1769480 | tf_op jit(solution)/shard_map/ppermute | solution.py:586
  62.4 26.9 %collective-permute-start.4 = (bf16[4,64,1152]{2,1,0:T(8,128)(2,1)}, bf16[4,64,1152]{2,1,0:T(8,128)(2,1)}, u32[]{:S(2)}, u32[]{:S(2)}) collective-permute-start(bf16[4,64,1152]{2,1,0:T(8,128)(2,1)} %get-tuple-element.571), channel_id=1, source_target_pairs={{0,2},{1,3},{2,0},{3,1},{4,5},{5,4},{6,7},{7,6},{8,10},{9,11},{10,... | collective-permute-start | bytes 1769480 | tf_op jit(solution)/shard_map/ppermute | solution.py:586
  63.0 26.4 %collective-permute-start.2 = (bf16[4,64,1408]{2,1,0:T(8,128)(2,1)}, bf16[4,64,1408]{2,1,0:T(8,128)(2,1)}, u32[]{:S(2)}, u32[]{:S(2)}) collective-permute-start(bf16[4,64,1408]{2,1,0:T(8,128)(2,1)} %collective-permute-done.1), channel_id=1, source_target_pairs={{0,1},{1,0},{2,3},{3,2},{4,6},{5,7},{6,4},{7,5},{8,9},{9,8},{10,11... | collective-permute-start | bytes 2162696 | tf_op jit(solution)/shard_map/ppermute | solution.py:586
  90.6 22.7 %collective-permute-start.8 = (bf16[16,64,1408]{2,1,0:T(8,128)(2,1)S(1)}, bf16[16,64,1408]{2,1,0:T(8,128)(2,1)}, u32[]{:S(2)}, u32[]{:S(2)}) collective-permute-start(bf16[16,64,1408]{2,1,0:T(8,128)(2,1)S(1)} %constant_dynamic-update-slice_fusion.own.rest_0_), channel_id=1, source_target_pairs={{0,4},{4,0},{1,5},{5,1},{2,6},{6,2},{3,7},{7,3},{8,12},{12,8},{9,1... | collective-permute-start | bytes 8650760 | tf_op jit(solution)/shard_map/ppermute | solution.py:590
  116.4 40.3 %collective-permute-start.12 = (bf16[16,64,1152]{2,1,0:T(8,128)(2,1)}, bf16[16,64,1152]{2,1,0:T(8,128)(2,1)}, u32[]{:S(2)}, u32[]{:S(2)}) collective-permute-start(bf16[16,64,1152]{2,1,0:T(8,128)(2,1)} %pad_maximum_fusion.1.rest_0_), channel_id=1, source_target_pairs={{0,4},{4,0},{1,5},{5,1},{2,6},{6,2},{3,7},{7,3},{8,12},{12,8},{9,1... | collective-permute-start | bytes 7077896 | tf_op jit(solution)/shard_map/ppermute | solution.py:590
  120.1 31.6 %all-to-all-start.2 = ((bf16[32,64,256]{2,1,0:T(8,128)(2,1)}), bf16[32,64,256]{2,1,0:T(8,128)(2,1)S(1)}, u32[]{:S(2)}, u32[]{:S(2)}) async-start(bf16[32,64,256]{2,1,0:T(8,128)(2,1)} %bitcast.27), calls=%async_computation.2 | async-start | bytes 2097152 | tf_op jit(solution)/shard_map/all_to_all | solution.py:604
  126.5 25.2 %collective-permute-start.10 = (bf16[4,64,1152]{2,1,0:T(8,128)(2,1)S(1)}, bf16[4,64,1152]{2,1,0:T(8,128)(2,1)}, u32[]{:S(2)}, u32[]{:S(2)}) collective-permute-start(bf16[4,64,1152]{2,1,0:T(8,128)(2,1)S(1)} %slice.315), channel_id=1, source_target_pairs={{0,1},{1,0},{2,3},{3,2},{4,6},{5,7},{6,4},{7,5},{8,9},{9,8},{10,11... | collective-permute-start | bytes 1769480 | tf_op jit(solution)/shard_map/ppermute | solution.py:586
  128.4 23.3 %collective-permute-start.11 = (bf16[4,64,1152]{2,1,0:T(8,128)(2,1)S(1)}, bf16[4,64,1152]{2,1,0:T(8,128)(2,1)}, u32[]{:S(2)}, u32[]{:S(2)}) collective-permute-start(bf16[4,64,1152]{2,1,0:T(8,128)(2,1)S(1)} %slice.315), channel_id=1, source_target_pairs={{0,2},{1,3},{2,0},{3,1},{4,5},{5,4},{6,7},{7,6},{8,10},{9,11},{10,... | collective-permute-start | bytes 1769480 | tf_op jit(solution)/shard_map/ppermute | solution.py:586
  129.9 26.8 %collective-permute-start.9 = (bf16[4,64,1152]{2,1,0:T(8,128)(2,1)}, bf16[4,64,1152]{2,1,0:T(8,128)(2,1)}, u32[]{:S(2)}, u32[]{:S(2)}) collective-permute-start(bf16[4,64,1152]{2,1,0:T(8,128)(2,1)} %collective-permute-done.7), channel_id=1, source_target_pairs={{0,1},{1,0},{2,3},{3,2},{4,6},{5,7},{6,4},{7,5},{8,9},{9,8},{10,11... | collective-permute-start | bytes 1769480 | tf_op jit(solution)/shard_map/ppermute | solution.py:586
  158.8 25.8 %collective-permute-start.16 = (bf16[16,64,1152]{2,1,0:T(8,128)(2,1)S(1)}, bf16[16,64,1152]{2,1,0:T(8,128)(2,1)}, u32[]{:S(2)}, u32[]{:S(2)}) collective-permute-start(bf16[16,64,1152]{2,1,0:T(8,128)(2,1)S(1)} %pad_maximum_fusion.2.own), channel_id=1, source_target_pairs={{0,4},{4,0},{1,5},{5,1},{2,6},{6,2},{3,7},{7,3},{8,12},{12,8},{9,1... | collective-permute-start | bytes 7077896 | tf_op jit(solution)/shard_map/ppermute | solution.py:590
  161.2 23.4 %collective-permute-start.13 = (bf16[4,64,1152]{2,1,0:T(8,128)(2,1)}, bf16[4,64,1152]{2,1,0:T(8,128)(2,1)}, u32[]{:S(2)}, u32[]{:S(2)}) collective-permute-start(bf16[4,64,1152]{2,1,0:T(8,128)(2,1)} %collective-permute-done.11), channel_id=1, source_target_pairs={{0,1},{1,0},{2,3},{3,2},{4,6},{5,7},{6,4},{7,5},{8,9},{9,8},{10,11... | collective-permute-start | bytes 1769480 | tf_op jit(solution)/shard_map/ppermute | solution.py:586
  222.5 32.4 %all-to-all-start.3 = ((bf16[32,64,256]{2,1,0:T(8,128)(2,1)}), bf16[32,64,256]{2,1,0:T(8,128)(2,1)S(1)}, u32[]{:S(2)}, u32[]{:S(2)}) async-start(bf16[32,64,256]{2,1,0:T(8,128)(2,1)} %bitcast.32), calls=%async_computation.3 | async-start | bytes 2097152 | tf_op jit(solution)/shard_map/all_to_all | solution.py:604
  265.5 23.7 %collective-permute-start.20 = (bf16[16,64,1152]{2,1,0:T(8,128)(2,1)}, bf16[16,64,1152]{2,1,0:T(8,128)(2,1)}, u32[]{:S(2)}, u32[]{:S(2)}) collective-permute-start(bf16[16,64,1152]{2,1,0:T(8,128)(2,1)} %get-tuple-element.432), channel_id=1, source_target_pairs={{0,4},{4,0},{1,5},{5,1},{2,6},{6,2},{3,7},{7,3},{8,12},{12,8},{9,1... | collective-permute-start | bytes 7077896 | tf_op jit(solution)/shard_map/ppermute | solution.py:590
  268.3 35.2 %all-to-all-start.4 = ((bf16[32,64,192]{2,1,0:T(8,128)(2,1)}), bf16[32,64,192]{2,1,0:T(8,128)(2,1)S(1)}, u32[]{:S(2)}, u32[]{:S(2)}) async-start(bf16[32,64,192]{2,1,0:T(8,128)(2,1)} %bitcast.34), calls=%async_computation.4 | async-start | bytes 2097152 | tf_op jit(solution)/shard_map/all_to_all | solution.py:604
  274.0 99.1 %reduce-scatter.6.cloned.1.call-start = ((), (), s32[]{:S(2)}) async-start(), calls=%async_computation.13 | async-start | bytes 737280 | tf_op jit(solution)/shard_map/reduce_scatter | solution.py:703
  348.4 24.7 %collective-permute-start.26 = (bf16[16,64,1152]{2,1,0:T(8,128)(2,1)}, bf16[16,64,1152]{2,1,0:T(8,128)(2,1)}, u32[]{:S(2)}, u32[]{:S(2)}) collective-permute-start(bf16[16,64,1152]{2,1,0:T(8,128)(2,1)} %get-tuple-element.480), channel_id=1, source_target_pairs={{0,4},{4,0},{1,5},{5,1},{2,6},{6,2},{3,7},{7,3},{8,12},{12,8},{9,1... | collective-permute-start | bytes 7077896 | tf_op jit(solution)/shard_map/ppermute | solution.py:590
  351.2 70.3 %reduce-scatter.8.cloned.1.call-start = ((), (), s32[]{:S(2)}) async-start(), calls=%async_computation.14 | async-start | bytes 737280 | tf_op jit(solution)/shard_map/reduce_scatter | solution.py:703
  375.7 23.1 %collective-permute-start.28 = (bf16[8,64,1152]{2,1,0:T(8,128)(2,1)}, bf16[8,64,1152]{2,1,0:T(8,128)(2,1)}, u32[]{:S(2)}, u32[]{:S(2)}) collective-permute-start(bf16[8,64,1152]{2,1,0:T(8,128)(2,1)} %add_convert_fusion.2), channel_id=1, source_target_pairs={{0,1},{1,0},{2,3},{3,2},{4,6},{5,7},{6,4},{7,5},{8,9},{9,8},{10,11... | collective-permute-start | bytes 3538952 | tf_op jit(solution)/shard_map/ppermute | solution.py:586
  380.0 74.5 %reduce-scatter.14.cloned.1.call-start = ((), (), s32[]{:S(2)}) async-start(), calls=%async_computation.17 | async-start | bytes 737280 | tf_op jit(solution)/shard_map/reduce_scatter | solution.py:703
  426.3 68.7 %reduce-scatter.12.cloned.1.call-start = ((), (), s32[]{:S(2)}) async-start(), calls=%async_computation.16 | async-start | bytes 737280 | tf_op jit(solution)/shard_map/reduce_scatter | solution.py:703
  467.9 27.1 %reduce-scatter.10.cloned.1.call-start = ((), (), s32[]{:S(2)}) async-start(), calls=%async_computation.15 | async-start | bytes 737280 | tf_op jit(solution)/shard_map/reduce_scatter | solution.py:703
  (86 other events, 1118.1 us)
Sparse Core Ops, SparseCore 0:
  19.5 35.0 all-gather.4
  56.7 32.5 all-gather.6
  351.3 21.7 reduce-scatter.5
  380.1 19.4 reduce-scatter.7
  426.4 20.4 reduce-scatter.13
  449.6 20.3 reduce-scatter.11
  472.8 20.9 reduce-scatter.9

commit v4 on v3

--- a/solution.py
+++ b/solution.py
@@ -145,7 +145,7 @@
 
 def block_copies(parts, info_ref, pieces, wholes, sems, inward):
     core, f = info_ref[1], info_ref[2]
-    z_size = pieces[0].shape[0] // 4
+    z_size = pieces[0][0].shape[0]
     copies = []
     for side in range(2):
         owner = core if side == 0 else 1 - core
@@ -158,21 +158,25 @@
                     for kind, lane, lanes in parts:
                         refs = wholes[first : first + part_count(kind)]
                         for rows, where in part_blocks(kind, refs, lanes, at_dp, at_f):
-                            piece = pieces[side].at[(2 * far + near) * z_size + z, rows, pl.ds(lane, lanes)]
+                            piece = pieces[side][2 * far + near].at[z, rows, pl.ds(lane, lanes)]
                             ends = (piece, where) if inward else (where, piece)
                             copies.append(pltpu.make_async_copy(*ends, sems.at[len(copies)]))
                         first += part_count(kind)
     return copies
 
 
+def quarters(*refs):
+    return [[ref.at[pl.ds(k * (ref.shape[0] // 4), ref.shape[0] // 4)] for k in range(4)] for ref in refs]
+
+
 def weight_copies(info_ref, refs, dst_ref, sems):
     if len(refs) == 1:
         return [pltpu.make_async_copy(refs[0], dst_ref, sems.at[0])]
-    return block_copies(RES, info_ref, refs, (dst_ref,), sems, True)
+    return block_copies(RES, info_ref, (refs[:4], refs[4:]), (dst_ref,), sems, True)
 
 
 def weight_sems(weight):
-    return pltpu.SemaphoreType.DMA((1 if len(weight) == 1 else copy_count(RES, weight[0].shape[0] // 4),))
+    return pltpu.SemaphoreType.DMA((1 if len(weight) == 1 else copy_count(RES, weight[0].shape[0]),))
 
 
 def conv_fwd_kernel(n_weight, has_res, info_ref, x_ref, gain_ref, *rest):
@@ -256,7 +260,7 @@
         dw = nn(dtt_ref[dy + 1], a3_ref[PAD + 32 * dy : PAD + 32 * dy + ROWS, :])
         dw_ref[:, (dy + 1) * 3 * C : (dy + 2) * 3 * C] = dw.astype(dw_ref.dtype)
     if split:
-        copies = block_copies(RES, info_ref, (keep_ref, send_ref), (dw_ref,), sems, False)
+        copies = block_copies(RES, info_ref, quarters(keep_ref, send_ref), (dw_ref,), sems, False)
         for copy in copies:
             copy.start()
         for copy in copies:
@@ -498,7 +502,7 @@
     dws0_ref[...] = nn(transposed(dd), e_ref[...]).astype(out)
     copies = []
     if split:
-        copies = block_copies(MIX, info_ref, (keep_ref, send_ref), wholes, sems, False)
+        copies = block_copies(MIX, info_ref, quarters(keep_ref, send_ref), wholes, sems, False)
     for copy in copies:
         copy.start()
     de_ref[...] = nn(dd, ws0_ref[...])
@@ -604,8 +608,8 @@
     return lax.all_to_all(x, axis, 0, 0, tiled=True)
 
 
-def assemble_kernel(parts, info_ref, own, other, *rest):
-    copies = block_copies(parts, info_ref, (own, other), rest[:-1], rest[-1], True)
+def assemble_kernel(parts, info_ref, *rest):
+    copies = block_copies(parts, info_ref, (rest[:4], rest[4:8]), rest[8:-1], rest[-1], True)
     for copy in copies:
         copy.start()
     for copy in copies:
@@ -613,12 +617,12 @@
 
 
 def assemble(info, pieces, parts):
-    z_size = pieces[0].shape[0] // 4
+    z_size = pieces[0].shape[0]
     shapes = [s for kind, _, lanes in parts for s in part_shapes(kind, lanes, z_size, BF16)]
     return pl.pallas_call(
         functools.partial(assemble_kernel, parts),
         out_shape=tuple(jax.ShapeDtypeStruct(*s) for s in shapes),
-        in_specs=[SMEM] + [ANY] * 2,
+        in_specs=[SMEM] + [ANY] * 8,
         out_specs=(VM,) * len(shapes),
         scratch_shapes=[pltpu.SemaphoreType.DMA((copy_count(parts, z_size),))],
         compiler_params=PARAMS,
@@ -632,7 +636,7 @@
     count = len(shards)
     shards = list(shards)
     done = [{} for _ in shards]
-    pieces, side, waiting = {}, {}, {}
+    pieces, later, side, waiting, early = {}, {}, {}, {}, {}
     groups = [(1, 3), (3, count)] if count else []
     bulks = {}
     for first, last in groups:
@@ -649,10 +653,12 @@
         for i, (first, last) in enumerate(groups):
             if step == i + 1:
                 new["bulk", first] = bulks[first]
+        for j in list(early):
+            new["z", j] = early.pop(j)
         if 0 <= step - 3 < count:
-            own = jnp.concatenate([done[step - 3][name] for name in ("z", "near", "far", "both")])
-            new["own", step - 3] = own
-            new["core", step - 3] = partner(own)
+            own = [done[step - 3][name] for name in ("z", "near", "far", "both")]
+            new["core", step - 3] = [partner(one) for one in own]
+            pieces[step - 3] = (*own, *new["core", step - 3])
         if step in slow:
             due, function = slow[step]
             waiting[due] = function(pieces, side)
@@ -668,11 +674,15 @@
             if step == i + 1:
                 at = 0
                 for j in range(first, last):
-                    done[j]["z"] = done[first]["bulk"][:, :, at : at + shards[j].shape[1]]
+                    z_slice = done[first]["bulk"][:, :, at : at + shards[j].shape[1]]
                     at += shards[j].shape[1]
+                    if j <= step:
+                        done[j]["z"] = z_slice
+                    else:
+                        early[j] = z_slice
         if 0 <= step - 3 < count:
-            pieces[step - 3] = (done[step - 3]["own"], done[step - 3]["core"])
-    return pieces, side
+            later[step - 3] = (*[done[step - 3][name] for name in ("z", "near", "far", "both")], *done[step - 3]["core"])
+    return later, side
 
 
 def add_up(parts):
@@ -877,9 +887,11 @@
         got = shuffle(side["request"], BOTH)
         return {"asked": got[:, 0, :capacity].reshape(-1).astype(jnp.int32), "count": jnp.sum(got[:, 1])}
 
+    def answer(side):
+        return {"answer": exact(row_hot(side["asked"]), book, ((1,), (0,))).astype(BF16)}
+
     def reply(pieces, side):
-        answer = exact(row_hot(side["asked"]), book, ((1,), (0,))).astype(BF16)
-        return {"replies": shuffle(answer.reshape(devices, capacity, ZD), BOTH)}
+        return {"replies": shuffle(side["answer"].reshape(devices, capacity, ZD), BOTH)}
 
     gains = [jnp.stack([norm_gains[j], norm_gains[4 + j]]) for j in range(4)]
     width = w_pixel.shape[1]
@@ -893,12 +905,12 @@
             h0 = nt(pixels, fetch_whole(w_pixel[0]))
             weight = (fetch_whole(w_res[0]),)
         t1, a1 = conv_fwd(info, h0, gains[0], weight)
-        return {"h0": h0, "t1": t1, "a1": a1, "res0": weight}
+        return {**answer(side), "h0": h0, "t1": t1, "a1": a1, **({} if paired else {"res0": weight})}
 
     def run_conv1(pieces, side):
         weight = pieces[1] if paired else (fetch_whole(w_res[1]),)
         h1, a2 = conv_fwd(info, side["t1"], gains[1], weight, side["h0"])
-        return {"h1": h1, "a2": a2, "res1": weight}
+        return {"h1": h1, "a2": a2, **({} if paired else {"res1": weight})}
 
     def run_mid(pieces, side):
         if paired:
@@ -912,7 +924,7 @@
     def run_conv2(pieces, side):
         weight = pieces[3] if paired else (fetch_whole(w_res[2]),)
         t3, a3 = conv_fwd(info, side["mid"][6], gains[2], weight)
-        return {"t3": t3, "a3": a3, "res2": weight}
+        return {"t3": t3, "a3": a3, **({} if paired else {"res2": weight})}
 
     def run_conv3(pieces, side):
         sent = exact(pick, side["mid"][9], ((1,), (0,))).astype(BF16)
@@ -926,9 +938,9 @@
         g1, a4 = conv_fwd(info, side["t3"], gains[3], weight, side["mid"][6])
         out = BF16 if paired else F32
         d_head, dg1, loss = head(side["count"].reshape(1), g1, pix, pixels, valid_mask, out)
-        return {"held": held, "a4": a4, "res3": weight, "d_head": d_head, "dg1": dg1, "loss": loss}
-
-    others = {0: prepare, 2: ask, 4: run_conv0, 5: run_conv1, 6: run_mid, 7: run_conv2, 8: run_conv3}
+        return {"held": held, "a4": a4, **({} if paired else {"res3": weight}), "d_head": d_head, "dg1": dg1, "loss": loss}
+
+    others = {0: prepare, 2: ask, 3: run_conv0, 4: run_conv1, 5: run_mid, 6: run_conv2, 7: run_conv3}
     shards = []
     if paired:
         first = jnp.concatenate([swap(w_res[0]), widen(swap(w_pixel[0]), 256)], axis=1)
@@ -937,11 +949,11 @@
         mix = jnp.concatenate([scale[0], scale[1], latent.reshape(-1, latent.shape[2])], axis=1)
         last = jnp.concatenate([swap(res[3]), widen(swap(pix[1]), 256)], axis=1)
         shards = [first, swap(res[1]), mix, swap(res[2]), last]
-    _, side = gather_all(shards, others, {3: (4, reply)})
+    pieces, side = gather_all(shards, others, {4: (5, reply)})
     total_valid = side["count"]
     e, d, s, quant, y, s2, g0, commit, dcom, _ = side["mid"]
     h0, t1, a1, h1, a2, t3, a3, a4 = [side[name] for name in ("h0", "t1", "a1", "h1", "a2", "t3", "a3", "a4")]
-    res_w = [side["res0"], side["res1"], side["res2"], side["res3"]]
+    res_w = [pieces[i] for i in (0, 1, 3, 4)] if paired else [side[name] for name in ("res0", "res1", "res2", "res3")]
     scale0, scale1, lat0, lat1 = side["mats"]
     d_head, dg1, loss = side["d_head"], side["dg1"], side["loss"]
 

time: 545 us -> 522 us (0.958)
  waiting for transfers between devices: 122 us -> 111 us
  other arithmetic: 77.5 us -> 69 us
    all_gather x2, waiting for transfers between devices: 11.9 us -> 0.04 us  [gather_all(): lax.all_gather(jnp.concatenate(shards[first:last], axis=1), 'z')]
    concatenate x4 -> x0, other arithmetic: 8.78 us -> none  [gather_all(): jnp.concatenate([done[step - 3][name] for name in ('z', 'near', 'far', 'b...]
    all_to_all x7, waiting for transfers between devices: 40.8 us -> 47.4 us  [shuffle(): return lax.all_to_all(x, axis, 0, 0, tiled=True)]
  transfers between devices with their start and end apart: 53 -> 68, of which waited for: 21 -> 16; matrix products, arithmetic and copies ran while one was open for 18% -> 18% of each run, Pallas kernels for 34% -> 35%
where the time goes in v4:
time: 522 us; the launch traced here: 516 us
  Pallas kernels  190 us (36%)
  waiting for transfers between devices  111 us (21%)
  starting transfers between devices  75.6 us (14%)
  other arithmetic  69 us (13%)
  local copies, waits for them, and re-layouts  27.3 us (5%)
  between operations  21.3 us (4%)
  matrix products  21.1 us (4%)
    pallas_call x4, Pallas kernels, conv_dx(): pl.pallas_call(functools.partial(conv_dx_kernel, len(weight), res is not...  61.3 us
    ppermute x25, waiting for transfers between devices, across(): lax.ppermute(x, ('core', 'fsdp'), [(c * n + f, c * n + (f ^ masks[c])) fo...  50.1 us
    pallas_call x4, Pallas kernels, conv_fwd(): pl.pallas_call(functools.partial(conv_fwd_kernel, len(weight), res is not...  48.5 us
    all_to_all x7, waiting for transfers between devices, shuffle(): return lax.all_to_all(x, axis, 0, 0, tiled=True)  47.4 us
    pallas_call x4, Pallas kernels, conv_dw(): pl.pallas_call(functools.partial(conv_dw_kernel, z_size), out_shape=shape...  40.1 us
    ppermute x25, starting transfers between devices, across(): lax.ppermute(x, ('core', 'fsdp'), [(c * n + f, c * n + (f ^ masks[c])) fo...  32 us
    all_to_all x7, starting transfers between devices, shuffle(): return lax.all_to_all(x, axis, 0, 0, tiled=True)  29.6 us
    convert_element_type x10, other arithmetic, scatter_stages(): away = add_up([p[half:2 * half] for p in parts]).astype(BF16)  23.7 us
  transfers between devices with their start and end apart: 68, of which 16 were waited for; matrix products, arithmetic and copies ran while one was open for 18% of the time, Pallas kernels for 35%

profile of v4, /device:TPU:0, one launch (start us, length us, event | category | flops | bytes accessed | tf_op | source)
XLA Modules:
  0.0 515.6 jit_solution(6078001875418575013)
XLA Ops:
  12.3 6.4 %all-to-all-start = ((bf16[4,64,1408]{2,1,0:T(8,128)(2,1)}), bf16[4,64,1408]{2,1,0:T(8,128)(2,1)}, u32[]{:S(2)}, u32[]{:S(2)}) async-start(bf16[4,64,1408]{2,1,0:T(8,128)(2,1)} %broadcast_in_dim.10), calls=%async_computation | async-start | bytes 1441792 | tf_op jit(solution)/shard_map/all_to_all | solution.py:608
  29.2 24.4 %all-to-all-done.rest_0_ = bf16[4,64,1408]{2,1,0:T(8,128)(2,1)} async-done(((bf16[4,64,1408]{2,1,0:T(8,128)(2,1)}), bf16[4,64,1408]{2,1,0:T(8,128)(2,1)}, u32[]{:S(2)}, u32[]{:S(2)}) %all-to-all-start) | async-done | bytes 720928 | tf_op jit(solution)/shard_map/all_to_all | solution.py:608
  57.0 11.1 %collective-permute-done.rest_2_ = bf16[4,64,1408]{2,1,0:T(8,128)(2,1)S(1)} collective-permute-done((bf16[4,64,1408]{2,1,0:T(8,128)(2,1)}, bf16[4,64,1408]{2,1,0:T(8,128)(2,1)S(1)}, u32[]{:S(2)}, u32[]{:S(2)}) %collective-permute-start) | collective-permute-done | bytes 720928 | tf_op jit(solution)/shard_map/ppermute | solution.py:590
  79.1 11.5 %all-to-all-done.1 = f32[32,2,128]{2,1,0:T(2,128)S(1)} async-done(((f32[32,2,128]{2,1,0:T(2,128)}), f32[32,2,128]{2,1,0:T(2,128)S(1)}, u32[]{:S(2)}, u32[]{:S(2)}) %all-to-all-start.1) | async-done | bytes 32800 | tf_op jit(solution)/shard_map/all_to_all | solution.py:608
  111.3 11.7 %conv_fwd.4 = (f32[1024,512]{1,0:T(8,128)}, bf16[1088,1536]{1,0:T(8,128)(2,1)}) custom-call(s32[3]{0:T(128)} %pad_add_fusion.info_ref, f32[1024,512]{1,0:T(8,128)} %convolution_bitcast_fusion.x_ref.rest_8_, f32[2,512]{1,0:T(2,128)} %pad_maximum_fusion.4.gain_ref, bf16[4,64,1408]{2,1,0:T(8,128)(2,1)} %all-to-all-done.rest_0_, ...), custom_call_target="tpu_custom_call" | custom-call | flops 9663676416 | bytes 12582912 | tf_op jit(solution)/shard_map/conv_fwd/pallas_call | solution.py:228
  130.8 12.5 %conv_fwd.5 = (f32[1024,512]{1,0:T(8,128)}, bf16[1088,1536]{1,0:T(8,128)(2,1)}) custom-call(s32[3]{0:T(128)} %pad_add_fusion.info_ref, f32[1024,512]{1,0:T(8,128)} %get-tuple-element.445.x_ref, f32[2,512]{1,0:T(2,128)} %pad_maximum_fusion.5.gain_ref, bf16[4,64,1152]{2,1,0:T(8,128)(2,1)} %get-tuple-element.535.rest_0_, ...), custom_call_target="tpu_custom_call" | custom-call | flops 9663676416 | bytes 12582912 | tf_op jit(solution)/shard_map/conv_fwd/pallas_call | solution.py:228
  143.3 16.1 %collective-permute-done.13.rest_3_ = bf16[4,64,1152]{2,1,0:T(8,128)(2,1)} collective-permute-done((bf16[4,64,1152]{2,1,0:T(8,128)(2,1)}, bf16[4,64,1152]{2,1,0:T(8,128)(2,1)}, u32[]{:S(2)}, u32[]{:S(2)}) %collective-permute-start.13) | collective-permute-done | bytes 589856 | tf_op jit(solution)/shard_map/ppermute | solution.py:590
  163.5 6.5 %assemble.4 = (bf16[512,2048]{1,0:T(8,128)(2,1)}, bf16[512,2048]{1,0:T(8,128)(2,1)}, bf16[256,512]{1,0:T(8,128)(2,1)}, bf16[256,512]{1,0:T(8,128)(2,1)}) custom-call(s32[3]{0:T(128)} %pad_add_fusion.info_ref, bf16[4,64,1152]{2,1,0:T(8,128)(2,1)} %copy-done.3, bf16[4,64,1152]{2,1,0:T(8,128)(2,1)} %collective-permute-done.7.rest_1_, ...), custom_call_target="tpu_custom_call" | custom-call | flops 1073741824 | bytes 10485760 | tf_op jit(solution)/shard_map/assemble/pallas_call | solution.py:622
  173.2 6.8 %mid_fwd.1 = (bf16[256,2048]{1,0:T(8,128)(2,1)}, f32[256,512]{1,0:T(8,128)}, bf16[256,512]{1,0:T(8,128)(2,1)}, bf16[256,256]{1,0:T(8,128)(2,1)}, f32[256,512]{1,...) custom-call(f32[1024,512]{1,0:T(8,128)} %get-tuple-element.307.h_ref, ...), custom_call_target="tpu_custom_call" | custom-call | flops 4294967296 | bytes 12582912 | tf_op jit(solution)/shard_map/mid_fwd/pallas_call | solution.py:460
  187.7 12.0 %conv_fwd.6 = (f32[1024,512]{1,0:T(8,128)}, bf16[1088,1536]{1,0:T(8,128)(2,1)}) custom-call(s32[3]{0:T(128)} %pad_add_fusion.info_ref, f32[1024,512]{1,0:T(8,128)} %get-tuple-element.399.x_ref.rest_8_, f32[2,512]{1,0:T(2,128)} %pad_maximum_fusion.6.gain_ref, bf16[4,64,1152]{2,1,0:T(8,128)(2,1)} %slice.314.rest_0_, ...), custom_call_target="tpu_custom_call" | custom-call | flops 9663676416 | bytes 12582912 | tf_op jit(solution)/shard_map/conv_fwd/pallas_call | solution.py:228
  215.0 12.4 %conv_fwd.7 = (f32[1024,512]{1,0:T(8,128)}, bf16[1088,1536]{1,0:T(8,128)(2,1)}) custom-call(s32[3]{0:T(128)} %pad_add_fusion.info_ref, f32[1024,512]{1,0:T(8,128)} %get-tuple-element.382.x_ref, f32[2,512]{1,0:T(2,128)} %pad_maximum_fusion.7.gain_ref, bf16[4,64,1408]{2,1,0:T(8,128)(2,1)} %copy-done.2, bf16[4,64,1408]{2,1,0:T(8,128)(2,1)} %copy-done.17, ...), custom_call_target="tpu_custom_call" | custom-call | flops 9663676416 | bytes 12582912 | tf_op jit(solution)/shard_map/conv_fwd/pallas_call | solution.py:228
  227.4 9.3 %head.1 = (bf16[512,768]{1,0:T(8,128)(2,1)}, f32[1024,512]{1,0:T(8,128)}, f32[1,768]{1,0:T(1,128)}) custom-call(f32[1]{0:T(128)} %bitcast.29.total_ref, f32[1024,512]{1,0:T(8,128)} %get-tuple-element.358.g_ref, bf16[512,768]{1,0:T(8,128)(2,1)} %copy.74.wp_ref, bf16[1024,768]{1,0:T(8,128)(2,1)} %pix_ref.1, s32[1024,768]{1,0:T(8,128)} %mask_ref.1), custom_call_target="tpu_custom_call" | custom-call | flops 6442450944 | bytes 12582912 | tf_op jit(solution)/shard_map/head/pallas_call | solution.py:567
  236.7 10.2 %conv_dw.4 = (bf16[16,64,1152]{2,1,0:T(8,128)(2,1)}, bf16[16,64,1152]{2,1,0:T(8,128)(2,1)}) custom-call(s32[3]{0:T(128)} %pad_add_fusion.info_ref, f32[1024,512]{1,0:T(8,128)} %get-tuple-element.381.dt_ref.rest_8_, bf16[1088,1536]{1,0:T(8,128)(2,1)} %get-tuple-element.378.a3_ref), custom_call_target="tpu_custom_call" | custom-call | flops 9663676416 | bytes 12582912 | tf_op jit(solution)/shard_map/conv_dw/pallas_call | solution.py:278
  255.4 15.1 %conv_dx.4 = (bf16[1024,512]{1,0:T(8,128)(2,1)}, f32[2,512]{1,0:T(2,128)}) custom-call(s32[3]{0:T(128)} %pad_add_fusion.info_ref, f32[1024,512]{1,0:T(8,128)} %get-tuple-element.381.dt_ref.rest_8_, f32[1024,512]{1,0:T(8,128)} %get-tuple-element.382.x_ref, f32[2,512]{1,0:T(2,128)} %pad_maximum_fusion.7.gain_ref, bf16[4,64,1408]{2,1,0:T(8,128)(2,1)} %copy-done.2, ...), custom_call_target="tpu_custom_call" | custom-call | flops 14495514624 | bytes 12582912 | tf_op jit(solution)/shard_map/conv_dx/pallas_call | solution.py:369
  274.8 9.8 %conv_dw.5 = (bf16[16,64,1152]{2,1,0:T(8,128)(2,1)}, bf16[16,64,1152]{2,1,0:T(8,128)(2,1)}) custom-call(s32[3]{0:T(128)} %pad_add_fusion.info_ref, bf16[1024,512]{1,0:T(8,128)(2,1)} %get-tuple-element.398.dt_ref, bf16[1088,1536]{1,0:T(8,128)(2,1)} %get-tuple-element.392.a3_ref), custom_call_target="tpu_custom_call" | custom-call | flops 9663676416 | bytes 12582912 | tf_op jit(solution)/shard_map/conv_dw/pallas_call | solution.py:278
  294.6 16.0 %conv_dx.5 = (f32[1024,512]{1,0:T(8,128)}, f32[2,512]{1,0:T(2,128)}) custom-call(s32[3]{0:T(128)} %pad_add_fusion.info_ref, bf16[1024,512]{1,0:T(8,128)(2,1)} %get-tuple-element.398.dt_ref, f32[1024,512]{1,0:T(8,128)} %get-tuple-element.399.x_ref.rest_8_, f32[2,512]{1,0:T(2,128)} %pad_maximum_fusion.6.gain_ref, bf16[4,64,1152]{2,1,0:T(8,128)(2,1)} %slice.314.rest_0_, ...), custom_call_target="tpu_custom_call" | custom-call | flops 14495514624 | bytes 12582912 | tf_op jit(solution)/shard_map/conv_dx/pallas_call | solution.py:369
  314.7 11.4 %mid_bwd.1 = (bf16[16,64,1152]{2,1,0:T(8,128)(2,1)}, bf16[16,64,1152]{2,1,0:T(8,128)(2,1)}, f32[1024,512]{1,0:T(8,128)}) custom-call(s32[3]{0:T(128)} %pad_add_fusion.info_ref, f32[1024,512]{1,0:T(8,128)} %get-tuple-element.411.dg_ref, bf16[256,2048]{1,0:T(8,128)(2,1)} %get-tuple-element.412.e_ref, f32[256,512]{1,0:T(8,128)} %get-tuple-element.413.d_ref, ...), custom_call_target="tpu_custom_call" | custom-call | flops 4294967296 | bytes 12582912 | tf_op jit(solution)/shard_map/mid_bwd/pallas_call | solution.py:530
  335.3 10.3 %conv_dw.6 = (bf16[16,64,1152]{2,1,0:T(8,128)(2,1)}, bf16[16,64,1152]{2,1,0:T(8,128)(2,1)}) custom-call(s32[3]{0:T(128)} %pad_add_fusion.info_ref, f32[1024,512]{1,0:T(8,128)} %get-tuple-element.444.dt_ref.rest_8_, bf16[1088,1536]{1,0:T(8,128)(2,1)} %get-tuple-element.429.a3_ref), custom_call_target="tpu_custom_call" | custom-call | flops 9663676416 | bytes 12582912 | tf_op jit(solution)/shard_map/conv_dw/pallas_call | solution.py:278
  345.7 8.8 %reduce-scatter.6.cloned.1.call-done = bf16[1,64,1152]{2,1,0:T(8,128)(2,1)} async-done(((bf16[4,64,1152]{2,1,0:T(8,128)(2,1)}), bf16[1,64,1152]{2,1,0:T(8,128)(2,1)}) %reduce-scatter.6.cloned.1.call-update) | async-done | bytes 147472 | tf_op jit(solution)/shard_map/reduce_scatter | solution.py:713
  365.3 14.9 %conv_dx.6 = (bf16[1024,512]{1,0:T(8,128)(2,1)}, f32[2,512]{1,0:T(2,128)}) custom-call(s32[3]{0:T(128)} %pad_add_fusion.info_ref, f32[1024,512]{1,0:T(8,128)} %get-tuple-element.444.dt_ref.rest_8_, f32[1024,512]{1,0:T(8,128)} %get-tuple-element.445.x_ref, f32[2,512]{1,0:T(2,128)} %pad_maximum_fusion.5.gain_ref, ...), custom_call_target="tpu_custom_call" | custom-call | flops 14495514624 | bytes 12582912 | tf_op jit(solution)/shard_map/conv_dx/pallas_call | solution.py:369
  380.2 6.0 %collective-permute-done.44 = bf16[8,64,1152]{2,1,0:T(8,128)(2,1)} collective-permute-done((bf16[8,64,1152]{2,1,0:T(8,128)(2,1)}, bf16[8,64,1152]{2,1,0:T(8,128)(2,1)}, u32[]{:S(2)}, u32[]{:S(2)}) %collective-permute-start.44) | collective-permute-done | bytes 1179680 | tf_op jit(solution)/shard_map/ppermute | solution.py:590
  393.0 9.8 %conv_dw.7 = (bf16[16,64,1152]{2,1,0:T(8,128)(2,1)}, bf16[16,64,1152]{2,1,0:T(8,128)(2,1)}) custom-call(s32[3]{0:T(128)} %pad_add_fusion.info_ref, bf16[1024,512]{1,0:T(8,128)(2,1)} %get-tuple-element.473.dt_ref, bf16[1088,1536]{1,0:T(8,128)(2,1)} %get-tuple-element.457.a3_ref), custom_call_target="tpu_custom_call" | custom-call | flops 9663676416 | bytes 12582912 | tf_op jit(solution)/shard_map/conv_dw/pallas_call | solution.py:278
  416.8 15.4 %conv_dx.7 = (bf16[1024,512]{1,0:T(8,128)(2,1)}, f32[2,512]{1,0:T(2,128)}) custom-call(s32[3]{0:T(128)} %pad_add_fusion.info_ref, bf16[1024,512]{1,0:T(8,128)(2,1)} %get-tuple-element.473.dt_ref, f32[1024,512]{1,0:T(8,128)} %convolution_bitcast_fusion.x_ref.rest_8_, f32[2,512]{1,0:T(2,128)} %pad_maximum_fusion.4.gain_ref, ...), custom_call_target="tpu_custom_call" | custom-call | flops 14495514624 | bytes 12582912 | tf_op jit(solution)/shard_map/conv_dx/pallas_call | solution.py:369
  453.7 10.7 %all-to-all-done.6 = bf16[8,4,64,192]{3,2,1,0:T(8,128)(2,1)S(1)} async-done(((bf16[8,4,64,192]{3,2,1,0:T(8,128)(2,1)}), bf16[8,4,64,192]{3,2,1,0:T(8,128)(2,1)S(1)}, u32[]{:S(2)}, u32[]{:S(2)}) %all-to-all-start.6) | async-done | bytes 786464 | tf_op jit(solution)/shard_map/all_to_all | solution.py:608
  (356 shorter events, 215.4 us)
Async XLA Ops:
  7.2 49.8 %all-gather.5.cloned.1.call-start = ((), (), s32[]{:S(2)}) async-start(), calls=%async_computation.18 | async-start | bytes 1474560 | tf_op jit(solution)/shard_map/all_gather | solution.py:643
  12.3 41.3 %all-to-all-start = ((bf16[4,64,1408]{2,1,0:T(8,128)(2,1)}), bf16[4,64,1408]{2,1,0:T(8,128)(2,1)}, u32[]{:S(2)}, u32[]{:S(2)}) async-start(bf16[4,64,1408]{2,1,0:T(8,128)(2,1)} %broadcast_in_dim.10), calls=%async_computation | async-start | bytes 1441792 | tf_op jit(solution)/shard_map/all_to_all | solution.py:608
  18.8 72.8 %all-gather.7.cloned.1.call-start = ((), (), s32[]{:S(2)}) async-start(), calls=%async_computation.19 | async-start | bytes 1638400 | tf_op jit(solution)/shard_map/all_gather | solution.py:643
  68.3 23.3 %collective-permute-start.2 = (bf16[4,64,1408]{2,1,0:T(8,128)(2,1)S(1)}, bf16[4,64,1408]{2,1,0:T(8,128)(2,1)}, u32[]{:S(2)}, u32[]{:S(2)}) collective-permute-start(bf16[4,64,1408]{2,1,0:T(8,128)(2,1)S(1)} %collective-permute-done.1.rest_1_), channel_id=1, source_target_pairs={{0,1},{1,0},{2,3},{3,2},{4,6},{5,7},{6,4},{7,5},{8,9},{9,8},{10,11... | collective-permute-start | bytes 2162696 | tf_op jit(solution)/shard_map/ppermute | solution.py:590
  93.8 33.2 %collective-permute-start.16 = (bf16[4,64,1152]{2,1,0:T(8,128)(2,1)}, bf16[4,64,1152]{2,1,0:T(8,128)(2,1)}, u32[]{:S(2)}, u32[]{:S(2)}) collective-permute-start(bf16[4,64,1152]{2,1,0:T(8,128)(2,1)} %get-tuple-element.535.rest_0_), channel_id=1, source_target_pairs={{0,4},{4,0},{1,5},{5,1},{2,6},{6,2},{3,7},{7,3},{8,12},{12,8},{9,1... | collective-permute-start | bytes 1769480 | tf_op jit(solution)/shard_map/ppermute | solution.py:594
  99.2 24.4 %collective-permute-start.6 = (bf16[4,64,1152]{2,1,0:T(8,128)(2,1)S(1)}, bf16[4,64,1152]{2,1,0:T(8,128)(2,1)}, u32[]{:S(2)}, u32[]{:S(2)}) collective-permute-start(bf16[4,64,1152]{2,1,0:T(8,128)(2,1)S(1)} %get-tuple-element.278.rest_0_), channel_id=1, source_target_pairs={{0,1},{1,0},{2,3},{3,2},{4,6},{5,7},{6,4},{7,5},{8,9},{9,8},{10,11... | collective-permute-start | bytes 1769480 | tf_op jit(solution)/shard_map/ppermute | solution.py:590
  102.7 26.1 %collective-permute-start.17 = (bf16[4,64,1152]{2,1,0:T(8,128)(2,1)}, bf16[4,64,1152]{2,1,0:T(8,128)(2,1)}, u32[]{:S(2)}, u32[]{:S(2)}) collective-permute-start(bf16[4,64,1152]{2,1,0:T(8,128)(2,1)} %collective-permute-done.4.rest_1_), channel_id=1, source_target_pairs={{0,4},{4,0},{1,5},{5,1},{2,6},{6,2},{3,7},{7,3},{8,12},{12,8},{9,1... | collective-permute-start | bytes 1769480 | tf_op jit(solution)/shard_map/ppermute | solution.py:594
  123.7 46.4 %all-to-all-start.2 = ((bf16[32,64,256]{2,1,0:T(8,128)(2,1)}), bf16[32,64,256]{2,1,0:T(8,128)(2,1)S(1)}, u32[]{:S(2)}, u32[]{:S(2)}) async-start(bf16[32,64,256]{2,1,0:T(8,128)(2,1)} %bitcast.27), calls=%async_computation.2 | async-start | bytes 2097152 | tf_op jit(solution)/shard_map/all_to_all | solution.py:608
  126.9 33.8 %collective-permute-start.23 = (bf16[4,64,1152]{2,1,0:T(8,128)(2,1)S(1)}, bf16[4,64,1152]{2,1,0:T(8,128)(2,1)}, u32[]{:S(2)}, u32[]{:S(2)}) collective-permute-start(bf16[4,64,1152]{2,1,0:T(8,128)(2,1)S(1)} %get-tuple-element.278.rest_0_), channel_id=1, source_target_pairs={{0,4},{4,0},{1,5},{5,1},{2,6},{6,2},{3,7},{7,3},{8,12},{12,8},{9,1... | collective-permute-start | bytes 1769480 | tf_op jit(solution)/shard_map/ppermute | solution.py:594
  127.1 32.4 %collective-permute-start.14 = (bf16[4,64,1152]{2,1,0:T(8,128)(2,1)S(1)}, bf16[4,64,1152]{2,1,0:T(8,128)(2,1)}, u32[]{:S(2)}, u32[]{:S(2)}) collective-permute-start(bf16[4,64,1152]{2,1,0:T(8,128)(2,1)S(1)} %copy-done.20), channel_id=1, source_target_pairs={{0,1},{1,0},{2,3},{3,2},{4,6},{5,7},{6,4},{7,5},{8,9},{9,8},{10,11... | collective-permute-start | bytes 1769480 | tf_op jit(solution)/shard_map/ppermute | solution.py:590
  128.7 30.8 %collective-permute-start.15 = (bf16[4,64,1152]{2,1,0:T(8,128)(2,1)S(1)}, bf16[4,64,1152]{2,1,0:T(8,128)(2,1)}, u32[]{:S(2)}, u32[]{:S(2)}) collective-permute-start(bf16[4,64,1152]{2,1,0:T(8,128)(2,1)S(1)} %copy-done.20), channel_id=1, source_target_pairs={{0,2},{1,3},{2,0},{3,1},{4,5},{5,4},{6,7},{7,6},{8,10},{9,11},{10,... | collective-permute-start | bytes 1769480 | tf_op jit(solution)/shard_map/ppermute | solution.py:590
  130.2 29.1 %collective-permute-start.13 = (bf16[4,64,1152]{2,1,0:T(8,128)(2,1)}, bf16[4,64,1152]{2,1,0:T(8,128)(2,1)}, u32[]{:S(2)}, u32[]{:S(2)}) collective-permute-start(bf16[4,64,1152]{2,1,0:T(8,128)(2,1)} %collective-permute-done.7.rest_1_), channel_id=1, source_target_pairs={{0,1},{1,0},{2,3},{3,2},{4,6},{5,7},{6,4},{7,5},{8,9},{9,8},{10,11... | collective-permute-start | bytes 1769480 | tf_op jit(solution)/shard_map/ppermute | solution.py:590
  130.8 31.1 %collective-permute-start.24 = (bf16[4,64,1152]{2,1,0:T(8,128)(2,1)}, bf16[4,64,1152]{2,1,0:T(8,128)(2,1)}, u32[]{:S(2)}, u32[]{:S(2)}) collective-permute-start(bf16[4,64,1152]{2,1,0:T(8,128)(2,1)} %collective-permute-done.7.rest_1_), channel_id=1, source_target_pairs={{0,4},{4,0},{1,5},{5,1},{2,6},{6,2},{3,7},{7,3},{8,12},{12,8},{9,1... | collective-permute-start | bytes 1769480 | tf_op jit(solution)/shard_map/ppermute | solution.py:594
  161.9 24.5 %collective-permute-start.30 = (bf16[4,64,1152]{2,1,0:T(8,128)(2,1)}, bf16[4,64,1152]{2,1,0:T(8,128)(2,1)}, u32[]{:S(2)}, u32[]{:S(2)}) collective-permute-start(bf16[4,64,1152]{2,1,0:T(8,128)(2,1)} %slice.314.rest_0_), channel_id=1, source_target_pairs={{0,4},{4,0},{1,5},{5,1},{2,6},{6,2},{3,7},{7,3},{8,12},{12,8},{9,1... | collective-permute-start | bytes 1769480 | tf_op jit(solution)/shard_map/ppermute | solution.py:594
  161.9 23.4 %collective-permute-start.20 = (bf16[4,64,1152]{2,1,0:T(8,128)(2,1)}, bf16[4,64,1152]{2,1,0:T(8,128)(2,1)}, u32[]{:S(2)}, u32[]{:S(2)}) collective-permute-start(bf16[4,64,1152]{2,1,0:T(8,128)(2,1)} %collective-permute-done.15.rest_1_), channel_id=1, source_target_pairs={{0,1},{1,0},{2,3},{3,2},{4,6},{5,7},{6,4},{7,5},{8,9},{9,8},{10,11... | collective-permute-start | bytes 1769480 | tf_op jit(solution)/shard_map/ppermute | solution.py:590
  202.6 34.1 %all-to-all-start.3 = ((bf16[32,64,256]{2,1,0:T(8,128)(2,1)}), bf16[32,64,256]{2,1,0:T(8,128)(2,1)}, u32[]{:S(2)}, u32[]{:S(2)}) async-start(bf16[32,64,256]{2,1,0:T(8,128)(2,1)} %bitcast.32), calls=%async_computation.3 | async-start | bytes 2097152 | tf_op jit(solution)/shard_map/all_to_all | solution.py:608
  246.9 23.6 %collective-permute-start.35 = (bf16[16,64,1152]{2,1,0:T(8,128)(2,1)}, bf16[16,64,1152]{2,1,0:T(8,128)(2,1)}, u32[]{:S(2)}, u32[]{:S(2)}) collective-permute-start(bf16[16,64,1152]{2,1,0:T(8,128)(2,1)} %get-tuple-element.390), channel_id=1, source_target_pairs={{0,4},{4,0},{1,5},{5,1},{2,6},{6,2},{3,7},{7,3},{8,12},{12,8},{9,1... | collective-permute-start | bytes 7077896 | tf_op jit(solution)/shard_map/ppermute | solution.py:594
  249.6 35.1 %all-to-all-start.4 = ((bf16[32,64,192]{2,1,0:T(8,128)(2,1)}), bf16[32,64,192]{2,1,0:T(8,128)(2,1)S(1)}, u32[]{:S(2)}, u32[]{:S(2)}) async-start(bf16[32,64,192]{2,1,0:T(8,128)(2,1)} %bitcast.34), calls=%async_computation.4 | async-start | bytes 2097152 | tf_op jit(solution)/shard_map/all_to_all | solution.py:608
  255.3 99.2 %reduce-scatter.6.cloned.1.call-start = ((), (), s32[]{:S(2)}) async-start(), calls=%async_computation.13 | async-start | bytes 737280 | tf_op jit(solution)/shard_map/reduce_scatter | solution.py:713
  329.7 24.8 %collective-permute-start.41 = (bf16[16,64,1152]{2,1,0:T(8,128)(2,1)}, bf16[16,64,1152]{2,1,0:T(8,128)(2,1)}, u32[]{:S(2)}, u32[]{:S(2)}) collective-permute-start(bf16[16,64,1152]{2,1,0:T(8,128)(2,1)} %get-tuple-element.440), channel_id=1, source_target_pairs={{0,4},{4,0},{1,5},{5,1},{2,6},{6,2},{3,7},{7,3},{8,12},{12,8},{9,1... | collective-permute-start | bytes 7077896 | tf_op jit(solution)/shard_map/ppermute | solution.py:594
  332.5 70.3 %reduce-scatter.8.cloned.1.call-start = ((), (), s32[]{:S(2)}) async-start(), calls=%async_computation.14 | async-start | bytes 737280 | tf_op jit(solution)/shard_map/reduce_scatter | solution.py:713
  361.2 75.0 %reduce-scatter.14.cloned.1.call-start = ((), (), s32[]{:S(2)}) async-start(), calls=%async_computation.17 | async-start | bytes 737280 | tf_op jit(solution)/shard_map/reduce_scatter | solution.py:713
  407.7 69.0 %reduce-scatter.12.cloned.1.call-start = ((), (), s32[]{:S(2)}) async-start(), calls=%async_computation.16 | async-start | bytes 737280 | tf_op jit(solution)/shard_map/reduce_scatter | solution.py:713
  449.6 27.1 %reduce-scatter.10.cloned.1.call-start = ((), (), s32[]{:S(2)}) async-start(), calls=%async_computation.15 | async-start | bytes 737280 | tf_op jit(solution)/shard_map/reduce_scatter | solution.py:713
  (98 other events, 1328.7 us)
Sparse Core Ops, SparseCore 0:
  11.5 45.1 all-gather.4
  58.9 32.6 all-gather.6
  332.6 21.8 reduce-scatter.5
  361.3 19.4 reduce-scatter.7
  407.8 20.4 reduce-scatter.13
  431.0 20.2 reduce-scatter.11
  454.2 21.1 reduce-scatter.9
